TPU v7x, 32 devices: a whole 2x2x4 slice. The times are simulated.
32 devices in a mesh: wide: 8 (over z, y), narrow: 4 (over x, core).
Axes of the slice: x: 2, y: 2, z: 4, core: 2. Of those that a mesh axis runs over, the one named last changes fastest.
Arguments:
- latents: bfloat16 [8192, 128], P(('wide', 'narrow')), may hold values from -40 to 40
- targets: int32 [8192], P(('wide', 'narrow')), may hold values from 0 to 8191, as said below
- embed_weight: bfloat16 [128, 3072], replicated, may hold values from -4 to 4
- mod_shift: float32 [3072], replicated, may hold values from -3 to 3
- mod_scale: float32 [3072], replicated, may hold values from -0.5 to 0.5
- qkv_weight: bfloat16 [3, 3072, 2048], P(None, 'wide', 'narrow'), may hold values from -0.109375 to 0.109375
- out_weight: bfloat16 [3072, 2048], P('wide', 'narrow'), may hold values from -0.75 to 0.75
- mod_gate: float32 [3072], replicated, may hold values from 2 to 6
- block_list: int32 [64, 8], P('wide'), may hold values from 0 to 15, as said below
- block_count: int32 [64], P('wide'), may hold values from 1 to 8, as said below
Outputs:
- mixed: bfloat16 [8192, 3072], P(('wide', 'narrow'))
Inputs may be any that keep to these rules, and one draw needn't show every extreme that they name: `targets`: A permutation of the positions. Raster row r goes to position p with p // 256 and r // 256 equal modulo 1024 // 256; of every aligned block of 256 raster rows exactly 32 go to each tile p // 1024. `block_list`: key block b holds tile positions b * 512 to b * 512 + 511. Slot 0 holds the block containing the query block; the slots below block_count hold distinct blocks whose tile b * 512 // 1024 is within two of the query block's tile; the later slots repeat slot 0. `block_count`: some row of every draw uses all 8 slots.
All inputs are finite; a program needn't handle non-finite values.
Results may differ from a plain program's by a relative error of at most 0.015.
Values may be sent and summed in bfloat16 or wider, within the bound.
No kernel may reach another device: no remote copies, remote signals or barrier semaphores. Data moves between devices by JAX's collectives and lax.ppermute only.
A program may use at most 192 MiB of HBM per device.

v0:
```python
import jax
import jax.numpy as jnp
from jax import lax
from jax.sharding import PartitionSpec as P

HEAD = 64
NB = 8
KB = 512
QB = 128


EPSILON = 1e-06


def shifted(block, axis, distance):
    devices = range(lax.axis_size(axis))
    route = [(i - distance, i) for i in devices if i - distance in devices]
    return lax.ppermute(block, axis, route)


def layer_norm(inputs):
    row_mean = jnp.mean(inputs, axis=-1, keepdims=True)
    centred = inputs - row_mean
    variance = jnp.mean(centred * centred, axis=-1, keepdims=True)
    return centred * lax.rsqrt(variance + EPSILON)


def head_norm(inputs):
    shaped = inputs.reshape(inputs.shape[0], -1, HEAD)
    return layer_norm(shaped).reshape(inputs.shape)


def per_device(
    latents,
    targets,
    embed_weight,
    mod_shift,
    mod_scale,
    qkv_weight,
    out_weight,
    mod_gate,
    block_list,
    block_count,
):
    row_total = latents.shape[0]
    wide_count = lax.axis_size("wide")
    narrow_count = lax.axis_size("narrow")
    tile_size = row_total * narrow_count
    wide_index = lax.axis_index("wide")
    ordering = jnp.argsort(targets)
    outgoing = latents[ordering].reshape(wide_count, row_total // wide_count, latents.shape[1])
    outgoing_pos = targets[ordering].reshape(wide_count, row_total // wide_count)
    incoming, incoming_pos = (
        lax.all_to_all(outgoing, "wide", split_axis=0, concat_axis=0, tiled=True),
        lax.all_to_all(outgoing_pos, "wide", split_axis=0, concat_axis=0, tiled=True),
    )
    incoming = incoming.reshape(row_total, latents.shape[1])
    local_pos = incoming_pos.reshape(row_total) % row_total
    placed = incoming[jnp.argsort(local_pos)]
    tile_patches = lax.all_gather(placed, "narrow", axis=0, tiled=True)
    heads_width = qkv_weight.shape[2]
    local_heads = heads_width // HEAD
    near_patches = {}
    for offset in (2, 1, -1, -2):
        near_patches[offset] = shifted(tile_patches, "wide", offset)
    stacked = jnp.concatenate(
        [near_patches[2], near_patches[1], tile_patches, near_patches[-1], near_patches[-2]], axis=0
    )
    embedded_all = jnp.dot(stacked, embed_weight, preferred_element_type=jnp.float32)
    normed_all = (layer_norm(embedded_all) * (1.0 + mod_scale) + mod_shift).astype(jnp.bfloat16)
    weight_piece = lax.all_gather(qkv_weight, "wide", axis=1, tiled=True)
    own_columns = lax.dynamic_slice_in_dim(normed_all, 2 * tile_size, tile_size, 0)
    query_run = jnp.dot(own_columns, weight_piece[0], preferred_element_type=jnp.float32)
    pair_run = jnp.einsum(
        "tr,crh->cth", normed_all, weight_piece[1:], preferred_element_type=jnp.float32
    )
    queries = head_norm(query_run).astype(jnp.bfloat16)
    extended = jnp.stack(
        [head_norm(pair_run[0]).astype(jnp.bfloat16), pair_run[1].astype(jnp.bfloat16)]
    )
    base_row = (wide_index - 2) * tile_size

    def attend(inputs):
        block_index, blocks, live_count = inputs
        query_rows = lax.dynamic_slice_in_dim(queries, block_index * QB, QB, 0).reshape(
            QB, local_heads, HEAD
        )
        starts = blocks * KB - base_row
        selected = jax.vmap(lambda start_row: lax.dynamic_slice_in_dim(extended, start_row, KB, 1))(
            starts
        )
        key_rows = selected[:, 0].reshape(NB * KB, local_heads, HEAD)
        value_rows = selected[:, 1].reshape(NB * KB, local_heads, HEAD)
        scores = (
            jnp.einsum("qhd,khd->hqk", query_rows, key_rows, preferred_element_type=jnp.float32)
            * 0.125
        )
        live_mask = (jnp.arange(NB * KB) // KB < live_count).astype(jnp.float32)
        weighted = jnp.exp(scores) * live_mask
        probs = (weighted / jnp.sum(weighted, axis=-1, keepdims=True)).astype(jnp.bfloat16)
        attended = jnp.einsum("hqk,khd->qhd", probs, value_rows, preferred_element_type=jnp.float32)
        return attended.astype(jnp.bfloat16).reshape(QB, heads_width)

    block_ids = jnp.arange(tile_size // QB, dtype=jnp.int32)
    attended_all = lax.map(attend, (block_ids, block_list, block_count)).reshape(
        tile_size, heads_width
    )
    out_columns = lax.all_gather(out_weight, "wide", axis=0, tiled=True)
    summed = lax.psum_scatter(
        lax.dot_general(
            attended_all, out_columns, (((1,), (1,)), ((), ())), preferred_element_type=jnp.float32
        ).astype(jnp.bfloat16),
        "narrow",
        scatter_dimension=0,
        tiled=True,
    ).astype(jnp.float32)
    return (mod_gate * summed).astype(jnp.bfloat16)


def solution(mesh):
    in_specs = (
        P(("wide", "narrow"), None),
        P(("wide", "narrow")),
        P(),
        P(),
        P(),
        P(None, "wide", "narrow"),
        P("wide", "narrow"),
        P(),
        P("wide", None),
        P("wide"),
    )
    out_specs = P(("wide", "narrow"), None)
    return jax.shard_map(
        per_device, mesh=mesh, in_specs=in_specs, out_specs=out_specs, check_vma=False
    )
```

profile of v0, /device:TPU:16, one launch (start us, length us, event | category | flops | bytes accessed | tf_op | source)
XLA Modules:
  0.0 1068.0 jit_solution(12998917395195378932)
XLA Ops:
  76.3 23.6 %fusion.21 = (f32[5120]{0:T(1024)S(1)}, f32[5120,3072]{0,1:T(8,128)}) fusion(bf16[5120,128]{1,0:T(8,128)(2,1)S(1)} %constant_dynamic-update-slice_fusion.1, bf16[128,3072]{1,0:T(8,128)(2,1)S(1)} %copy-done), kind=kOutput, calls=%fused_computation.66 | convolution fusion | flops 4042255360 | bytes 65032192 | tf_op jit(solution)/shard_map/dot_general | solution.py:69
  99.9 20.0 %multiply_reduce_fusion = f32[5120]{0:T(1024)S(1)} fusion(f32[5120,3072]{0,1:T(8,128)} %get-tuple-element.165, f32[5120]{0:T(1024)S(1)} %broadcast_multiply_fusion.2), kind=kLoop, calls=%fused_computation.28 | loop fusion | flops 47180800 | bytes 62955520 | tf_op jit(solution)/shard_map/reduce_sum | solution.py:24
  120.0 31.4 %add_convert_fusion = bf16[5120,3072]{0,1:T(8,128)(2,1)} fusion(f32[5120,3072]{0,1:T(8,128)} %get-tuple-element.165, f32[3072]{0:T(1024)S(1)} %copy-done.2, f32[3072]{0:T(1024)S(1)} %broadcast_add_fusion, f32[5120]{0:T(1024)S(1)} %add_rsqrt_fusion.2, f32[5120]{0:T(1024)S(1)} %broadcast_multiply_fusion.2), kind=kLoop, calls=%fused_computation.27 | loop fusion | flops 78643200 | bytes 94437376 | tf_op jit(solution)/shard_map/convert_element_type | solution.py:70
  158.0 40.0 %fusion.13 = f32[2,5120,512]{1,2,0:T(8,128)} fusion(bf16[5120,3072]{0,1:T(8,128)(2,1)} %add_convert_fusion, bf16[3,3072,512]{1,2,0:T(8,128)(2,1)} %all-gather.4.cloned.1.call-done), kind=kOutput, calls=%fused_computation.31 | convolution fusion | flops 32212254720 | bytes 58720256 | tf_op jit(solution)/shard_map/tr,crh->cth/dot_general | solution.py:74
  198.0 9.2 slice.51
  231.3 7.8 fusion.16
  239.1 9.0 pad_maximum_fusion
  248.1 13.8 %copy.22 = bf16[2,5120,512]{2,1,0:T(8,128)(2,1)} copy(bf16[2,5120,512]{1,2,0:T(8,128)(2,1)} %pad_maximum_fusion) | data formatting | bytes 20971520 | tf_op jit(solution)/shard_map/while | solution.py:105
  261.9 731.1 %while.15 = (s32[]{:T(128)}, bf16[8,128,512]{2,1,0:T(8,128)(2,1)S(1)}, s32[8,8]{1,0:T(8,128)}, s32[]{:T(128)}, bf16[2,5120,512]{2,1,0:T(8,128)(2,1)}, /*index=5*...) while((s32[]{:T(128)}, ...), condition=%wide.region_10.11_spmd, body=%wide.region_8.10_spmd.sunk | while | flops 1103207424 | bytes 95479392 | solution.py:105
  264.2 29.0 %while.16 = (s32[]{:T(128)}, bf16[2,5120,512]{2,1,0:T(8,128)(2,1)}, s32[8,3]{0,1:T(4,128)S(1)}, bf16[8,2,512,512]{3,2,1,0:T(8,128)(2,1)}, s32[]{:T(128)}) while((s32[]{:T(128)}, bf16[2,5120,512]{2,1,0:T(8,128)(2,1)}, s32[8,3]{0,1:T(4,128)S(1)}, bf16[8,2,512,512]{3,2,1,0:T(8,128)(2,1)}, s32[]{:T(128)}) %tuple.51), condition=%wide.while_cond, body=%wide.while_body.sunk | while | flops 2 | bytes 2098273 | solution.py:89
  299.1 8.0 copy.34
  307.1 7.4 squeeze.33
  315.7 11.5 %fusion.43 = (f32[8,128]{1,0:T(8,128)S(1)}, f32[8,128,4096]{2,1,0:T(8,128)}) fusion(f32[4096]{0:T(1024)S(1)} %fusion.42, bf16[128,8,64]{0,2,1:T(8,128)(2,1)S(1)} %bitcast.79, bf16[4096,8,64]{0,2,1:T(8,128)(2,1)} %squeeze.33), kind=kOutput, calls=%fused_computation.7.clone.1 | convolution fusion | flops 549452800 | bytes 21123072 | tf_op jit(solution)/shard_map/while/body/eval_jaxpr/qhd,khd->hqk/dot_general | solution.py:95
  327.3 8.1 copy.33
  335.3 7.4 squeeze.32
  342.7 10.6 fusion.44
  355.6 29.0 %while.16 = (s32[]{:T(128)}, bf16[2,5120,512]{2,1,0:T(8,128)(2,1)}, s32[8,3]{0,1:T(4,128)S(1)}, bf16[8,2,512,512]{3,2,1,0:T(8,128)(2,1)}, s32[]{:T(128)}) while((s32[]{:T(128)}, bf16[2,5120,512]{2,1,0:T(8,128)(2,1)}, s32[8,3]{0,1:T(4,128)S(1)}, bf16[8,2,512,512]{3,2,1,0:T(8,128)(2,1)}, s32[]{:T(128)}) %tuple.51), condition=%wide.while_cond, body=%wide.while_body.sunk | while | flops 2 | bytes 2098273 | solution.py:89
  390.5 8.0 copy.34
  398.5 7.4 squeeze.33
  407.1 11.5 %fusion.43 = (f32[8,128]{1,0:T(8,128)S(1)}, f32[8,128,4096]{2,1,0:T(8,128)}) fusion(f32[4096]{0:T(1024)S(1)} %fusion.42, bf16[128,8,64]{0,2,1:T(8,128)(2,1)S(1)} %bitcast.79, bf16[4096,8,64]{0,2,1:T(8,128)(2,1)} %squeeze.33), kind=kOutput, calls=%fused_computation.7.clone.1 | convolution fusion | flops 549452800 | bytes 21123072 | tf_op jit(solution)/shard_map/while/body/eval_jaxpr/qhd,khd->hqk/dot_general | solution.py:95
  418.6 8.1 copy.33
  426.7 7.4 squeeze.32
  434.1 10.6 fusion.44
  446.9 29.0 %while.16 = (s32[]{:T(128)}, bf16[2,5120,512]{2,1,0:T(8,128)(2,1)}, s32[8,3]{0,1:T(4,128)S(1)}, bf16[8,2,512,512]{3,2,1,0:T(8,128)(2,1)}, s32[]{:T(128)}) while((s32[]{:T(128)}, bf16[2,5120,512]{2,1,0:T(8,128)(2,1)}, s32[8,3]{0,1:T(4,128)S(1)}, bf16[8,2,512,512]{3,2,1,0:T(8,128)(2,1)}, s32[]{:T(128)}) %tuple.51), condition=%wide.while_cond, body=%wide.while_body.sunk | while | flops 2 | bytes 2098273 | solution.py:89
  481.8 8.0 copy.34
  489.8 7.4 squeeze.33
  498.4 11.5 %fusion.43 = (f32[8,128]{1,0:T(8,128)S(1)}, f32[8,128,4096]{2,1,0:T(8,128)}) fusion(f32[4096]{0:T(1024)S(1)} %fusion.42, bf16[128,8,64]{0,2,1:T(8,128)(2,1)S(1)} %bitcast.79, bf16[4096,8,64]{0,2,1:T(8,128)(2,1)} %squeeze.33), kind=kOutput, calls=%fused_computation.7.clone.1 | convolution fusion | flops 549452800 | bytes 21123072 | tf_op jit(solution)/shard_map/while/body/eval_jaxpr/qhd,khd->hqk/dot_general | solution.py:95
  510.0 8.1 copy.33
  518.0 7.4 squeeze.32
  525.4 10.6 fusion.44
  538.3 29.0 %while.16 = (s32[]{:T(128)}, bf16[2,5120,512]{2,1,0:T(8,128)(2,1)}, s32[8,3]{0,1:T(4,128)S(1)}, bf16[8,2,512,512]{3,2,1,0:T(8,128)(2,1)}, s32[]{:T(128)}) while((s32[]{:T(128)}, bf16[2,5120,512]{2,1,0:T(8,128)(2,1)}, s32[8,3]{0,1:T(4,128)S(1)}, bf16[8,2,512,512]{3,2,1,0:T(8,128)(2,1)}, s32[]{:T(128)}) %tuple.51), condition=%wide.while_cond, body=%wide.while_body.sunk | while | flops 2 | bytes 2098273 | solution.py:89
  573.2 8.0 copy.34
  581.2 7.4 squeeze.33
  589.8 11.5 %fusion.43 = (f32[8,128]{1,0:T(8,128)S(1)}, f32[8,128,4096]{2,1,0:T(8,128)}) fusion(f32[4096]{0:T(1024)S(1)} %fusion.42, bf16[128,8,64]{0,2,1:T(8,128)(2,1)S(1)} %bitcast.79, bf16[4096,8,64]{0,2,1:T(8,128)(2,1)} %squeeze.33), kind=kOutput, calls=%fused_computation.7.clone.1 | convolution fusion | flops 549452800 | bytes 21123072 | tf_op jit(solution)/shard_map/while/body/eval_jaxpr/qhd,khd->hqk/dot_general | solution.py:95
  601.3 8.1 copy.33
  609.4 7.4 squeeze.32
  616.8 10.6 fusion.44
  629.6 29.0 %while.16 = (s32[]{:T(128)}, bf16[2,5120,512]{2,1,0:T(8,128)(2,1)}, s32[8,3]{0,1:T(4,128)S(1)}, bf16[8,2,512,512]{3,2,1,0:T(8,128)(2,1)}, s32[]{:T(128)}) while((s32[]{:T(128)}, bf16[2,5120,512]{2,1,0:T(8,128)(2,1)}, s32[8,3]{0,1:T(4,128)S(1)}, bf16[8,2,512,512]{3,2,1,0:T(8,128)(2,1)}, s32[]{:T(128)}) %tuple.51), condition=%wide.while_cond, body=%wide.while_body.sunk | while | flops 2 | bytes 2098273 | solution.py:89
  664.5 8.0 copy.34
  672.5 7.4 squeeze.33
  681.1 11.5 %fusion.43 = (f32[8,128]{1,0:T(8,128)S(1)}, f32[8,128,4096]{2,1,0:T(8,128)}) fusion(f32[4096]{0:T(1024)S(1)} %fusion.42, bf16[128,8,64]{0,2,1:T(8,128)(2,1)S(1)} %bitcast.79, bf16[4096,8,64]{0,2,1:T(8,128)(2,1)} %squeeze.33), kind=kOutput, calls=%fused_computation.7.clone.1 | convolution fusion | flops 549452800 | bytes 21123072 | tf_op jit(solution)/shard_map/while/body/eval_jaxpr/qhd,khd->hqk/dot_general | solution.py:95
  692.7 8.1 copy.33
  700.7 7.4 squeeze.32
  708.1 10.6 fusion.44
  721.0 29.0 %while.16 = (s32[]{:T(128)}, bf16[2,5120,512]{2,1,0:T(8,128)(2,1)}, s32[8,3]{0,1:T(4,128)S(1)}, bf16[8,2,512,512]{3,2,1,0:T(8,128)(2,1)}, s32[]{:T(128)}) while((s32[]{:T(128)}, bf16[2,5120,512]{2,1,0:T(8,128)(2,1)}, s32[8,3]{0,1:T(4,128)S(1)}, bf16[8,2,512,512]{3,2,1,0:T(8,128)(2,1)}, s32[]{:T(128)}) %tuple.51), condition=%wide.while_cond, body=%wide.while_body.sunk | while | flops 2 | bytes 2098273 | solution.py:89
  755.8 8.0 copy.34
  763.9 7.4 squeeze.33
  772.5 11.5 %fusion.43 = (f32[8,128]{1,0:T(8,128)S(1)}, f32[8,128,4096]{2,1,0:T(8,128)}) fusion(f32[4096]{0:T(1024)S(1)} %fusion.42, bf16[128,8,64]{0,2,1:T(8,128)(2,1)S(1)} %bitcast.79, bf16[4096,8,64]{0,2,1:T(8,128)(2,1)} %squeeze.33), kind=kOutput, calls=%fused_computation.7.clone.1 | convolution fusion | flops 549452800 | bytes 21123072 | tf_op jit(solution)/shard_map/while/body/eval_jaxpr/qhd,khd->hqk/dot_general | solution.py:95
  784.0 8.1 copy.33
  792.1 7.4 squeeze.32
  799.5 10.6 fusion.44
  812.3 29.0 %while.16 = (s32[]{:T(128)}, bf16[2,5120,512]{2,1,0:T(8,128)(2,1)}, s32[8,3]{0,1:T(4,128)S(1)}, bf16[8,2,512,512]{3,2,1,0:T(8,128)(2,1)}, s32[]{:T(128)}) while((s32[]{:T(128)}, bf16[2,5120,512]{2,1,0:T(8,128)(2,1)}, s32[8,3]{0,1:T(4,128)S(1)}, bf16[8,2,512,512]{3,2,1,0:T(8,128)(2,1)}, s32[]{:T(128)}) %tuple.51), condition=%wide.while_cond, body=%wide.while_body.sunk | while | flops 2 | bytes 2098273 | solution.py:89
  847.2 8.0 copy.34
  863.8 11.5 %fusion.43 = (f32[8,128]{1,0:T(8,128)S(1)}, f32[8,128,4096]{2,1,0:T(8,128)}) fusion(f32[4096]{0:T(1024)S(1)} %fusion.42, bf16[128,8,64]{0,2,1:T(8,128)(2,1)S(1)} %bitcast.79, bf16[4096,8,64]{0,2,1:T(8,128)(2,1)} %squeeze.33), kind=kOutput, calls=%fused_computation.7.clone.1 | convolution fusion | flops 549452800 | bytes 21123072 | tf_op jit(solution)/shard_map/while/body/eval_jaxpr/qhd,khd->hqk/dot_general | solution.py:95
  875.4 8.1 copy.33
  883.4 7.4 squeeze.32
  890.8 10.6 fusion.44
  903.6 29.0 %while.16 = (s32[]{:T(128)}, bf16[2,5120,512]{2,1,0:T(8,128)(2,1)}, s32[8,3]{0,1:T(4,128)S(1)}, bf16[8,2,512,512]{3,2,1,0:T(8,128)(2,1)}, s32[]{:T(128)}) while((s32[]{:T(128)}, bf16[2,5120,512]{2,1,0:T(8,128)(2,1)}, s32[8,3]{0,1:T(4,128)S(1)}, bf16[8,2,512,512]{3,2,1,0:T(8,128)(2,1)}, s32[]{:T(128)}) %tuple.51), condition=%wide.while_cond, body=%wide.while_body.sunk | while | flops 2 | bytes 2098273 | solution.py:89
  938.5 8.0 copy.34
  955.2 11.5 %fusion.43 = (f32[8,128]{1,0:T(8,128)S(1)}, f32[8,128,4096]{2,1,0:T(8,128)}) fusion(f32[4096]{0:T(1024)S(1)} %fusion.42, bf16[128,8,64]{0,2,1:T(8,128)(2,1)S(1)} %bitcast.79, bf16[4096,8,64]{0,2,1:T(8,128)(2,1)} %squeeze.33), kind=kOutput, calls=%fused_computation.7.clone.1 | convolution fusion | flops 549452800 | bytes 21123072 | tf_op jit(solution)/shard_map/while/body/eval_jaxpr/qhd,khd->hqk/dot_general | solution.py:95
  966.7 8.1 copy.33
  974.8 7.4 squeeze.32
  982.2 10.6 fusion.44
  1000.4 58.1 %reduce-scatter.2.cloned.1.call-done = bf16[256,3072]{1,0:T(8,128)(2,1)} async-done(((bf16[1024,3072]{1,0:T(8,128)(2,1)}), bf16[256,3072]{1,0:T(8,128)(2,1)}) %reduce-scatter.2.cloned.1.call-update) | async-done | bytes 1572880 | tf_op jit(solution)/shard_map/reduce_scatter | solution.py:109
  (356 shorter events, 426.1 us)
Async XLA Ops:
  6.5 69.8 %copy-start = (bf16[128,3072]{1,0:T(8,128)(2,1)S(1)}, bf16[128,3072]{1,0:T(8,128)(2,1)}, u32[]{:S(2)}) copy-start(bf16[128,3072]{1,0:T(8,128)(2,1)} %param.14) | copy-start | bytes 2359300
  6.5 151.5 %all-gather.4.cloned.1.call-start = ((), (), s32[]{:S(2)}) async-start(), calls=%async_computation.3 | async-start | bytes 10616832 | tf_op jit(solution)/shard_map/all_gather | solution.py:71
  15.6 12.9 %all-to-all-start.1 = ((s32[8,1,32]{2,1,0:T(1,128)}), s32[8,1,32]{2,1,0:T(1,128)S(1)}, u32[]{:S(2)}, u32[]{:S(2)}) async-start(s32[8,1,32]{2,1,0:T(1,128)} %all_to_all.10), calls=%async_computation.1 | async-start | bytes 8192 | tf_op jit(solution)/shard_map/all_to_all | solution.py:55
  28.4 15.5 %all-to-all-start = ((bf16[8,32,128]{2,1,0:T(8,128)(2,1)}), bf16[8,32,128]{2,1,0:T(8,128)(2,1)S(1)}, u32[]{:S(2)}, u32[]{:S(2)}) async-start(bf16[8,32,128]{2,1,0:T(8,128)(2,1)} %bitcast.6), calls=%async_computation | async-start | bytes 131072 | tf_op jit(solution)/shard_map/all_to_all | solution.py:54
  35.0 958.0 %all-gather.6.cloned.1.call-start = ((), (), s32[]{:S(2)}) async-start(), calls=%async_computation.4 | async-start | bytes 3538944 | tf_op jit(solution)/shard_map/all_gather | solution.py:108
  50.6 16.9 %collective-permute-start = (bf16[1024,128]{1,0:T(8,128)(2,1)S(1)}, bf16[1024,128]{1,0:T(8,128)(2,1)S(1)}, u32[]{:S(2)}, u32[]{:S(2)}) collective-permute-start(bf16[1024,128]{1,0:T(8,128)(2,1)S(1)} %all-gather), channel_id=1, source_target_pairs={{0,8},{4,12},{8,16},{12,20},{16,24},{20,28},{1,9},{5,13},{9,17},{1... | collective-permute-start | bytes 786440 | tf_op jit(solution)/shard_map/ppermute | solution.py:18
  54.4 1004.2 %reduce-scatter.2.cloned.1.call-start = ((), (), s32[]{:S(2)}) async-start(), calls=%async_computation.5 | async-start | bytes 7864320 | tf_op jit(solution)/shard_map/reduce_scatter | solution.py:109
  54.4 19.4 %collective-permute-start.1 = (bf16[1024,128]{1,0:T(8,128)(2,1)S(1)}, bf16[1024,128]{1,0:T(8,128)(2,1)S(1)}, u32[]{:S(2)}, u32[]{:S(2)}) collective-permute-start(bf16[1024,128]{1,0:T(8,128)(2,1)S(1)} %all-gather), channel_id=1, source_target_pairs={{0,4},{4,8},{8,12},{12,16},{16,20},{20,24},{24,28},{1,5},{5,9},{9,... | collective-permute-start | bytes 786440 | tf_op jit(solution)/shard_map/ppermute | solution.py:18
  58.2 15.6 %collective-permute-start.2 = (bf16[1024,128]{1,0:T(8,128)(2,1)S(1)}, bf16[1024,128]{1,0:T(8,128)(2,1)S(1)}, u32[]{:S(2)}, u32[]{:S(2)}) collective-permute-start(bf16[1024,128]{1,0:T(8,128)(2,1)S(1)} %all-gather), channel_id=1, source_target_pairs={{4,0},{8,4},{12,8},{16,12},{20,16},{24,20},{28,24},{5,1},{9,5},{13... | collective-permute-start | bytes 786440 | tf_op jit(solution)/shard_map/ppermute | solution.py:18
  61.9 14.4 %collective-permute-start.3 = (bf16[1024,128]{1,0:T(8,128)(2,1)S(1)}, bf16[1024,128]{1,0:T(8,128)(2,1)S(1)}, u32[]{:S(2)}, u32[]{:S(2)}) collective-permute-start(bf16[1024,128]{1,0:T(8,128)(2,1)S(1)} %all-gather), channel_id=1, source_target_pairs={{8,0},{12,4},{16,8},{20,12},{24,16},{28,20},{9,1},{13,5},{17,9},{2... | collective-permute-start | bytes 786440 | tf_op jit(solution)/shard_map/ppermute | solution.py:18
  99.9 20.0 %copy-start.2 = (f32[3072]{0:T(1024)S(1)}, f32[3072]{0:T(1024)}, u32[]{:S(2)}) copy-start(f32[3072]{0:T(1024)} %param.15) | copy-start | bytes 36868
  207.2 7.3 slice-start
  248.1 13.8 %copy-start.4 = (bf16[8,128,512]{2,1,0:T(8,128)(2,1)S(1)}, bf16[8,128,512]{2,1,0:T(8,128)(2,1)}, u32[]{:S(2)}) copy-start(bf16[8,128,512]{2,1,0:T(8,128)(2,1)} %custom-call.8) | copy-start | bytes 3145732
  248.1 13.8 %copy-start.5 = (s32[8]{0:T(128)S(1)}, s32[8]{0:T(128)}, u32[]{:S(2)}) copy-start(s32[8]{0:T(128)} %param.21) | copy-start | bytes 100
  993.0 65.5 %copy-start.3 = (f32[3072]{0:T(1024)S(1)}, f32[3072]{0:T(1024)}, u32[]{:S(2)}) copy-start(f32[3072]{0:T(1024)} %param.19) | copy-start | bytes 36868
  993.0 68.4 %copy-start.1 = (bf16[128,3072]{1,0:T(8,128)(2,1)S(1)}, bf16[128,3072]{1,0:T(8,128)(2,1)}, u32[]{:S(2)}) copy-start(bf16[128,3072]{1,0:T(8,128)(2,1)} %param.14) | copy-start | bytes 2359300
Sparse Core Ops, SparseCore 0:
  9.4 148.6 all-gather.3
  160.2 58.6 all-gather.5
  1000.5 57.9 reduce-scatter.1
where the time goes:
time: 1080 us; the launch traced here: 1070 us
  local copies, waits for them, and re-layouts  576 us (53%)
  matrix products  254 us (24%)
  other arithmetic  102 us (9%)
  waiting for transfers between devices  85.7 us (8%)
  starting transfers between devices  25.7 us (2%)
  between operations  13.3 us (1%)
    gather x192, local copies, waits for them, and re-layouts  232 us
    slice x16, local copies, waits for them, and re-layouts, attend(): key_rows = selected[:, 0].reshape(NB * KB, local_heads, HEAD)  111 us
    dot_general x8, matrix products, attend(): jnp.einsum('qhd,khd->hqk', query_rows, key_rows, preferred_element_type=j...  92.3 us
    dot_general x8, matrix products, attend(): jnp.einsum('hqk,khd->qhd', probs, value_rows, preferred_element_type=jnp....  85.1 us
    slice x8, local copies, waits for them, and re-layouts, attend(): value_rows = selected[:, 1].reshape(NB * KB, local_heads, HEAD)  64.5 us
    squeeze x8, local copies, waits for them, and re-layouts, attend(): value_rows = selected[:, 1].reshape(NB * KB, local_heads, HEAD)  59.2 us
    squeeze x8, local copies, waits for them, and re-layouts, attend(): key_rows = selected[:, 0].reshape(NB * KB, local_heads, HEAD)  58.9 us
    reduce_scatter x1, waiting for transfers between devices, per_device(): lax.psum_scatter(lax.dot_general(attended_all, out_columns, (((1,), (1,))...  58.1 us
  transfers between devices with their start and end apart: 9, of which 7 were waited for; matrix products, arithmetic and copies ran while one was open for 86% of the time, Pallas kernels for 0%

commit v1 on v0

v1 whole, which is shorter than its diff:
```python
import functools

import jax
import jax.numpy as jnp
from jax import lax
from jax.experimental import pallas as pl
from jax.experimental.pallas import tpu as pltpu
from jax.sharding import PartitionSpec as P

HEAD = 64
NB = 8
KB = 512
QB = 128
REACH = 2
SPAN = 2 * REACH + 1
EPSILON = 1e-06

f32 = jnp.float32
bf16 = jnp.bfloat16
NT = (((1,), (1,)), ((), ()))
TN = (((0,), (0,)), ((), ()))


def ntdot(a, b):
    return lax.dot_general(a, b, NT, preferred_element_type=f32)


def whole_spec():
    return pl.BlockSpec(memory_space=pltpu.VMEM)


def split3(value):
    high = value.astype(bf16)
    rest = value - high.astype(f32)
    mid = rest.astype(bf16)
    low = (rest - mid.astype(f32)).astype(bf16)
    return high, mid, low


def gram_kernel(embed_ref, gram_ref):
    embed = embed_ref[...].astype(f32)
    width = embed.shape[1]
    centred = embed - jnp.mean(embed, axis=1, keepdims=True)
    gram = lax.dot_general(
        centred, centred, NT, preferred_element_type=f32, precision=lax.Precision.HIGHEST
    ) * (1.0 / width)
    for index, term in enumerate(split3(gram)):
        gram_ref[index] = term


def prep_kernel(
    wide_count,
    embed_ref,
    slice_ref,
    scale_ref,
    shift_ref,
    qkv_ref,
    latents_ref,
    row_ref,
    column_ref,
    weight_ref,
    bias_ref,
    rows_ref,
    place_ref,
):
    row_mean = jnp.mean(embed_ref[...].astype(f32), axis=1, keepdims=True)
    factor = (slice_ref[...].astype(f32) - row_mean) * (1.0 + scale_ref[...])
    high, mid, _ = split3(factor)
    shift_terms = split3(jnp.broadcast_to(shift_ref[...], (16, shift_ref.shape[1])))
    heads_width = qkv_ref.shape[2]
    for part in range(3):
        piece = qkv_ref[part]
        product = jnp.dot(high, piece, preferred_element_type=f32) + jnp.dot(
            mid, piece, preferred_element_type=f32
        )
        turned = product.T
        if part < 2:
            grouped = turned.reshape(heads_width // HEAD, HEAD, turned.shape[1])
            grouped = grouped - jnp.mean(grouped, axis=1, keepdims=True)
            turned = grouped.reshape(turned.shape)
        weight_ref[part * heads_width : (part + 1) * heads_width, :] = turned.astype(bf16)
        bias = (
            jnp.dot(shift_terms[0], piece, preferred_element_type=f32)
            + jnp.dot(shift_terms[1], piece, preferred_element_type=f32)
            + jnp.dot(shift_terms[2], piece, preferred_element_type=f32)
        )
        bias_ref[part : part + 1, :] = bias[0:1, :].astype(bf16)
    row_total = latents_ref.shape[0]
    share = row_total // wide_count
    across = row_ref[...]
    down = column_ref[...]
    slot_across = jnp.sum((down < across).astype(f32), axis=0, keepdims=True)
    slot_down = jnp.sum((across < down).astype(f32), axis=1, keepdims=True)
    local = (down % row_total).astype(f32)
    count = rows_ref.shape[1]
    latents = latents_ref[...]
    for receiver in range(wide_count):
        first = (receiver - REACH) * share
        wanted = lax.broadcasted_iota(jnp.int32, (count, row_total), 0)
        chosen = (slot_across == (wanted + first).astype(f32)) & (wanted < SPAN * share)
        rows_ref[receiver] = jnp.dot(
            chosen.astype(bf16), latents, preferred_element_type=f32
        ).astype(bf16)
        lane = lax.broadcasted_iota(jnp.int32, (row_total, 128), 1)
        mine = (slot_down == (lane + receiver * share).astype(f32)) & (lane < share)
        spots = jnp.sum(jnp.where(mine, local, 0.0), axis=0, keepdims=True)
        place_ref[receiver] = jnp.broadcast_to(spots, (16, 128)).astype(bf16)


def attend_kernel(
    row_total,
    tile_size,
    order_ref,
    starts_ref,
    counts_ref,
    patches_ref,
    spots_ref,
    weight_ref,
    bias_ref,
    value_bias_ref,
    gram_ref,
    out_ref,
    keys_ref,
    values_ref,
    queries_ref,
    twin_ref,
    total_ref,
):
    heads_width = out_ref.shape[1]
    local_heads = heads_width // HEAD
    pairs = heads_width // 128
    narrow_count = tile_size // row_total

    def doubled(part):
        weight = weight_ref[part * heads_width : (part + 1) * heads_width, :]
        return jnp.concatenate([weight, weight], axis=1)

    def centred_bias(part):
        bias = bias_ref[part * heads_width : (part + 1) * heads_width, :]
        grouped = bias.reshape(local_heads, HEAD, 1)
        grouped = grouped - jnp.mean(grouped, axis=1, keepdims=True)
        return grouped.reshape(heads_width, 1)

    def unit_heads(turned, bias):
        grouped = (turned + bias).reshape(local_heads, HEAD, turned.shape[1])
        square = jnp.mean(grouped * grouped, axis=1, keepdims=True)
        return (grouped * lax.rsqrt(square + EPSILON)).reshape(turned.shape)

    gram_top = jnp.concatenate([gram_ref[0], gram_ref[1]], axis=0)
    key_bias = centred_bias(1)

    def project(step, carry):
        tile = step // narrow_count
        block = step % narrow_count
        place = order_ref[block] * row_total
        rows = patches_ref[block, pl.ds(pl.multiple_of(tile * row_total, row_total), row_total), :]
        wide_rows = rows.astype(f32)
        image = jnp.dot(
            jnp.concatenate([rows, rows], axis=1), gram_top, preferred_element_type=f32
        ) + jnp.dot(rows, gram_ref[2], preferred_element_type=f32)
        variance = jnp.sum(image * wide_rows, axis=1, keepdims=True)
        scaled = wide_rows * lax.rsqrt(variance + EPSILON)
        high = scaled.astype(bf16)
        low = (scaled - high.astype(f32)).astype(bf16)
        both = jnp.concatenate([high, low], axis=1)
        at = pl.multiple_of(tile * tile_size + place, row_total)
        keys_ref[:, pl.ds(at, row_total)] = unit_heads(ntdot(doubled(1), both), key_bias).astype(bf16)
        values_ref[pl.ds(at, row_total), :] = (
            ntdot(both, doubled(2)) + value_bias_ref[...]
        ).astype(bf16)

        @pl.when(tile == REACH)
        def _():
            wanted = lax.broadcasted_iota(jnp.int32, (row_total, row_total), 0).astype(f32)
            chosen = (spots_ref[block].astype(f32) == wanted).astype(bf16)
            placed = jnp.dot(chosen, both, preferred_element_type=f32).astype(bf16)
            turned = unit_heads(ntdot(doubled(0), placed), centred_bias(0)).astype(bf16) * 0.125
            queries_ref[pl.ds(pl.multiple_of(place, row_total), row_total), :] = (
                turned.astype(f32).T.astype(bf16)
            )

        return carry

    lax.fori_loop(0, SPAN * narrow_count, project, 0)

    left = lax.broadcasted_iota(jnp.int32, (QB, 128), 1) < HEAD
    ones = jnp.ones((KB, 128), bf16)

    def attend(block, carry):
        at = pl.multiple_of(block * QB, QB)
        for pair in range(pairs):
            rows = queries_ref[pl.ds(at, QB), pair * 128 : (pair + 1) * 128]
            twin_ref[pair, 0:QB, :] = jnp.where(left, rows, jnp.zeros_like(rows))
            twin_ref[pair, QB : 2 * QB, :] = jnp.where(left, jnp.zeros_like(rows), rows)
            total_ref[pair] = jnp.zeros_like(total_ref[pair])

        def visit(slot, inner):
            start = pl.multiple_of(starts_ref[block * NB + slot], KB)
            for pair in range(pairs):
                columns = slice(pair * 128, (pair + 1) * 128)
                scores = jnp.dot(
                    twin_ref[pair],
                    keys_ref[columns, pl.ds(start, KB)],
                    preferred_element_type=f32,
                )
                weights = jnp.exp(scores).astype(bf16)
                side = jnp.concatenate([values_ref[pl.ds(start, KB), columns], ones], axis=1)
                total_ref[pair] += jnp.dot(weights, side, preferred_element_type=f32)
            return inner

        lax.fori_loop(0, counts_ref[block], visit, 0)
        for pair in range(pairs):
            both = total_ref[pair, :, 0:128] / total_ref[pair, :, 128:256]
            out_ref[pl.ds(at, QB), pair * 128 : (pair + 1) * 128] = jnp.where(
                left, both[0:QB], both[QB : 2 * QB]
            ).astype(bf16)
        return carry

    lax.fori_loop(0, tile_size // QB, attend, 0)


def output_kernel(narrow_count, attended_ref, weight_ref, gate_ref, out_ref):
    rows = weight_ref.shape[0] // narrow_count
    width = weight_ref.shape[1]
    total = None
    for index in range(narrow_count):
        term = ntdot(
            attended_ref[:, index * width : (index + 1) * width],
            weight_ref[index * rows : (index + 1) * rows, :],
        )
        total = term if total is None else total + term
    out_ref[...] = (total * gate_ref[...]).astype(bf16)


def flip(block, axis, bit):
    devices = range(lax.axis_size(axis))
    return lax.ppermute(block, axis, [(i, i ^ bit) for i in devices])


def per_device(
    latents,
    targets,
    embed_weight,
    mod_shift,
    mod_scale,
    qkv_weight,
    out_weight,
    mod_gate,
    block_list,
    block_count,
):
    row_total, patch = latents.shape
    width = embed_weight.shape[1]
    wide_count = lax.axis_size("wide")
    narrow_count = lax.axis_size("narrow")
    wide_index = lax.axis_index("wide")
    narrow_index = lax.axis_index("narrow")
    tile_size = row_total * narrow_count
    depth, heads_width = qkv_weight.shape[1:]
    share = row_total // wide_count
    count = -(-SPAN * share // 16) * 16
    piece = 3 * heads_width // wide_count

    out_all = lax.all_gather(out_weight, ("wide", "narrow"), axis=0, tiled=True)

    first = wide_index * depth
    weight_part, bias_part, rows, spots = pl.pallas_call(
        functools.partial(prep_kernel, wide_count),
        out_shape=(
            jax.ShapeDtypeStruct((3 * heads_width, patch), bf16),
            jax.ShapeDtypeStruct((3, heads_width), bf16),
            jax.ShapeDtypeStruct((wide_count, count, patch), bf16),
            jax.ShapeDtypeStruct((wide_count, 16, 128), bf16),
        ),
        in_specs=[whole_spec()] * 8,
        out_specs=(whole_spec(),) * 4,
        name="prep",
    )(
        embed_weight,
        lax.dynamic_slice_in_dim(embed_weight, first, depth, 1),
        lax.dynamic_slice_in_dim(mod_scale, first, depth, 0).reshape(1, depth),
        lax.dynamic_slice_in_dim(mod_shift, first, depth, 0).reshape(1, depth),
        qkv_weight,
        latents,
        targets.reshape(1, row_total),
        targets.reshape(row_total, 1),
    )
    gram = pl.pallas_call(
        gram_kernel,
        out_shape=jax.ShapeDtypeStruct((3, patch, patch), bf16),
        in_specs=[whole_spec()],
        out_specs=whole_spec(),
        name="gram",
    )(embed_weight)

    bias_rows = -(-piece // 128)
    bias_block = jnp.pad(bias_part.reshape(wide_count, piece), ((0, 0), (0, 16 * 128 - piece)))
    payload = jnp.concatenate(
        [weight_part.reshape(wide_count, piece, patch), bias_block.reshape(wide_count, 16, 128), rows, spots],
        axis=1,
    )
    arrived = lax.all_to_all(payload, "wide", split_axis=0, concat_axis=0, tiled=True)

    summed = jnp.sum(arrived[:, : piece + 16].astype(f32), axis=0).astype(bf16)
    spread = jnp.broadcast_to(summed[None], (wide_count,) + summed.shape)
    near = arrived[:, piece + 16 : piece + 16 + SPAN * share]
    near = near.reshape(wide_count, SPAN, share, patch).transpose(1, 0, 2, 3)
    near = near.reshape(SPAN * row_total, patch)
    mine = arrived[:, piece + 16 + count, :share].reshape(-1)
    mine = jnp.pad(mine, (0, 16 * 128 - row_total)).reshape(16, 128)
    group = jnp.concatenate([near, mine], axis=0)[None]
    order = [0]
    bits = [1 << k for k in range(1, narrow_count.bit_length() - 1)] + [1]
    for bit in bits:
        group = jnp.concatenate([group, flip(group, "narrow", bit)], axis=0)
        order = order + [index ^ bit for index in order]
    everything = lax.all_to_all(spread, "wide", split_axis=0, concat_axis=0, tiled=True)
    weight_all = everything[:, :piece].reshape(3 * heads_width, patch)
    bias_all = everything[:, piece:].reshape(wide_count, 16 * 128)[:, :piece].reshape(-1).astype(f32)

    order_ids = jnp.bitwise_xor(jnp.array(order, jnp.int32), narrow_index)
    starts = (block_list * KB - (wide_index - REACH) * tile_size).reshape(-1)
    spots_all = group[:, SPAN * row_total :].reshape(narrow_count, 1, 16 * 128)[:, :, :row_total]
    smem = pl.BlockSpec(memory_space=pltpu.SMEM)
    attended = pl.pallas_call(
        functools.partial(attend_kernel, row_total, tile_size),
        out_shape=jax.ShapeDtypeStruct((tile_size, heads_width), bf16),
        in_specs=[smem] * 3 + [whole_spec()] * 6,
        out_specs=whole_spec(),
        scratch_shapes=[
            pltpu.VMEM((heads_width, SPAN * tile_size), bf16),
            pltpu.VMEM((SPAN * tile_size, heads_width), bf16),
            pltpu.VMEM((tile_size, heads_width), bf16),
            pltpu.VMEM((heads_width // 128, 2 * QB, 128), bf16),
            pltpu.VMEM((heads_width // 128, 2 * QB, 256), f32),
        ],
        name="attend",
    )(
        order_ids,
        starts,
        block_count,
        group,
        spots_all,
        weight_all,
        bias_all.reshape(-1, 1),
        bias_all[2 * heads_width :].reshape(1, heads_width),
        gram,
    )

    merged = lax.all_to_all(attended, "narrow", split_axis=0, concat_axis=1, tiled=True)
    out_rows = out_weight.shape[0]
    gate = mod_gate.reshape(1, width)
    if out_rows % 128 == 0:
        return pl.pallas_call(
            functools.partial(output_kernel, narrow_count),
            grid=(wide_count,),
            out_shape=jax.ShapeDtypeStruct((row_total, width), bf16),
            in_specs=[
                pl.BlockSpec((row_total, narrow_count * heads_width), lambda i: (0, 0)),
                pl.BlockSpec((narrow_count * out_rows, heads_width), lambda i: (i, 0)),
                pl.BlockSpec((1, out_rows), lambda i: (0, i)),
            ],
            out_specs=pl.BlockSpec((row_total, out_rows), lambda i: (0, i)),
            name="output",
        )(merged, out_all, gate)
    weights = out_all.reshape(wide_count, narrow_count, out_rows, heads_width)
    product = jnp.einsum(
        "tnk,wnfk->twf",
        merged.reshape(row_total, narrow_count, heads_width),
        weights,
        preferred_element_type=f32,
    )
    return (gate * product.reshape(row_total, width)).astype(bf16)


def solution(mesh):
    in_specs = (
        P(("wide", "narrow"), None),
        P(("wide", "narrow")),
        P(),
        P(),
        P(),
        P(None, "wide", "narrow"),
        P("wide", "narrow"),
        P(),
        P("wide", None),
        P("wide"),
    )
    out_specs = P(("wide", "narrow"), None)
    return jax.shard_map(
        per_device, mesh=mesh, in_specs=in_specs, out_specs=out_specs, check_vma=False
    )
```

time: 1080 us -> 176 us (0.16)
  local copies, waits for them, and re-layouts: 576 us -> 12.6 us
  matrix products: 254 us -> 0 us
  other arithmetic: 102 us -> 3.5 us
  Pallas kernels: 0 us -> 78.6 us
  waiting for transfers between devices: 85.7 us -> 33.5 us
  blocking collectives: 5.77 us -> 17.9 us
    dot_general x20 -> x0, matrix products: 254 us -> none  [the longest x8 92.3 us: attend(): jnp.einsum('qhd,khd->hqk', query_rows, key_rows, preferred_element_type=j...]
    gather x195 -> x0, local copies, waits for them, and re-layouts: 237 us -> none
    slice x28 -> x5, local copies, waits for them, and re-layouts: 192 us -> 1.5 us  [the longest x1 0.77 us: per_device(): weight_all = everything[:, :piece].reshape(3 * heads_width, patch)]
    squeeze x16 -> x0, local copies, waits for them, and re-layouts: 118 us -> none  [the longest x8 59.2 us: attend(): value_rows = selected[:, 1].reshape(NB * KB, local_heads, HEAD)]
    pallas_call x0 -> x4, Pallas kernels: none -> 78.6 us  [the longest x1 60.5 us: per_device(): pl.pallas_call(functools.partial(attend_kernel, row_total, tile_size), ou...]
    reduce_scatter x1 -> x0, waiting for transfers between devices: 58.1 us -> none  [per_device(): lax.psum_scatter(lax.dot_general(attended_all, out_columns, (((1,), (1,))...]
    convert_element_type x12 -> x0, other arithmetic: 47.6 us -> none  [the longest x1 31.4 us: per_device(): (layer_norm(embedded_all) * (1.0 + mod_scale) + mod_shift).astype(jnp.bfl...]
    reduce_sum x4 -> x1, other arithmetic: 30.8 us -> 0.06 us  [per_device(): summed = jnp.sum(arrived[:, :piece + 16].astype(f32), axis=0).astype(bf16)]
  transfers between devices with their start and end apart: 9 -> 5, of which waited for: 7 -> 3; matrix products, arithmetic and copies ran while one was open for 86% -> 9% of each run, Pallas kernels for 0% -> 39%
where the time goes in v1:
time: 176 us; the launch traced here: 175 us
  Pallas kernels  78.6 us (45%)
  waiting for transfers between devices  33.5 us (19%)
  blocking collectives  17.9 us (10%)
  starting transfers between devices  15 us (9%)
  between operations  13.5 us (8%)
  local copies, waits for them, and re-layouts  12.6 us (7%)
  other arithmetic  3.5 us (2%)
    pallas_call x1, Pallas kernels, per_device(): pl.pallas_call(functools.partial(attend_kernel, row_total, tile_size), ou...  60.5 us
    all_to_all x1, waiting for transfers between devices, per_device(): lax.all_to_all(payload, 'wide', split_axis=0, concat_axis=0, tiled=True)  21.7 us
    all_to_all x1, blocking collectives, per_device(): lax.all_to_all(attended, 'narrow', split_axis=0, concat_axis=1, tiled=True)  17.9 us
    pallas_call x1, Pallas kernels, per_device(): pl.pallas_call(functools.partial(output_kernel, narrow_count), grid=(wide...  10.9 us
    all_to_all x1, starting transfers between devices, per_device(): lax.all_to_all(spread, 'wide', split_axis=0, concat_axis=0, tiled=True)  7.23 us
    all_to_all x1, starting transfers between devices, per_device(): lax.all_to_all(payload, 'wide', split_axis=0, concat_axis=0, tiled=True)  6.15 us
    all_to_all x1, waiting for transfers between devices, per_device(): lax.all_to_all(spread, 'wide', split_axis=0, concat_axis=0, tiled=True)  5.67 us
    ppermute x2, waiting for transfers between devices, flip(): return lax.ppermute(block, axis, [(i, i ^ bit) for i in devices])  5.34 us
  transfers between devices with their start and end apart: 5, of which 3 were waited for; matrix products, arithmetic and copies ran while one was open for 9% of the time, Pallas kernels for 39%

profile of v1, /device:TPU:16, one launch (start us, length us, event | category | flops | bytes accessed | tf_op | source)
XLA Modules:
  0.0 174.6 jit_solution(10109627085087749980)
XLA Ops:
  6.5 0.0 all-gather.2.cloned.1.call-start
  6.5 0.7 all-gather.2.cloned.1.call-update
  7.3 0.8 dynamic_slice.10
  8.0 0.6 reshape.71.scale_ref
  8.6 0.8 dynamic_slice.11
  9.4 0.5 reshape.72.shift_ref
  9.9 1.5 copy.19.column_ref
  11.4 1.5 constant_dynamic-slice_fusion.slice_ref
  12.9 3.8 %prep.1 = (bf16[1536,128]{1,0:T(8,128)(2,1)}, bf16[3,512]{1,0:T(4,128)(2,1)}, bf16[8,160,128]{2,1,0:T(8,128)(2,1)}, bf16[8,16,128]{2,1,0:T(8,128)(2,1)}) custom-call(bf16[128,3072]{1,0:T(8,128)(2,1)} %embed_ref.3, bf16[128,384]{1,0:T(8,128)(2,1)} %constant_dynamic-slice_fusion.slice_ref, f32[1,384]{1,0:T(1,128)} %reshape.71.scale_ref, ...), custom_call_target="tpu_custom_call" | custom-call | tf_op jit(solution)/shard_map/prep/pallas_call | solution.py:267
  16.7 0.8 reshape.76
  17.5 2.1 %pad_maximum_fusion.1 = bf16[8,384,128]{2,1,0:T(8,128)(2,1)} fusion(bf16[8,16,128]{2,1,0:T(8,128)(2,1)} %get-tuple-element.12, bf16[8,160,128]{2,1,0:T(8,128)(2,1)} %get-tuple-element.11, bf16[8,16,128]{2,1,0:T(8,128)(2,1)S(1)} %bitcast.35, bf16[8,192,128]{2,1,0:T(8,128)(2,1)} %bitcast.34), kind=kLoop, calls=%fused_computation.1 | loop fusion | flops 3145728 | bytes 1572864 | tf_op jit(solution)/shard_map/concatenate | solution.py:298
  19.6 6.1 %all-to-all-start = ((bf16[8,384,128]{2,1,0:T(8,128)(2,1)}), bf16[8,384,128]{2,1,0:T(8,128)(2,1)S(1)}, u32[]{:S(2)}, u32[]{:S(2)}) async-start(bf16[8,384,128]{2,1,0:T(8,128)(2,1)} %pad_maximum_fusion.1), calls=%async_computation | async-start | bytes 1572864 | tf_op jit(solution)/shard_map/all_to_all | solution.py:302
  25.7 21.7 %all-to-all-done = bf16[8,384,128]{2,1,0:T(8,128)(2,1)S(1)} async-done(((bf16[8,384,128]{2,1,0:T(8,128)(2,1)}), bf16[8,384,128]{2,1,0:T(8,128)(2,1)S(1)}, u32[]{:S(2)}, u32[]{:S(2)}) %all-to-all-start) | async-done | bytes 786464 | tf_op jit(solution)/shard_map/all_to_all | solution.py:302
  47.5 0.0 copy-start.1
  47.5 0.1 reshape_squeeze.3
  47.6 0.0 copy-start.2
  47.6 0.1 slice_reduce_fusion
  47.7 0.8 broadcast_in_dim.10
  48.5 7.2 %all-to-all-start.1 = ((bf16[8,208,128]{2,1,0:T(8,128)(2,1)}), bf16[8,208,128]{2,1,0:T(8,128)(2,1)S(1)}, u32[]{:S(2)}, u32[]{:S(2)}) async-start(bf16[8,208,128]{2,1,0:T(8,128)(2,1)} %broadcast_in_dim.10), calls=%async_computation.1 | async-start | bytes 851968 | tf_op jit(solution)/shard_map/all_to_all | solution.py:317
  55.8 1.5 collective-permute-start
  57.3 0.0 copy-done.1
  57.3 3.5 %gram.1.gram_ref = bf16[3,128,128]{2,1,0:T(8,128)(2,1)} custom-call(bf16[128,3072]{1,0:T(8,128)(2,1)} %embed_ref.3), custom_call_target="tpu_custom_call" | custom-call | tf_op jit(solution)/shard_map/gram/pallas_call | solution.py:288
  60.8 0.6 reshape.70.starts_ref
  61.4 0.0 copy-done.2
  61.4 0.6 broadcast_xor_fusion.order_ref
  61.9 5.3 %collective-permute-done = bf16[1,1296,128]{2,1,0:T(8,128)(2,1)S(1)} collective-permute-done((bf16[1,1296,128]{2,1,0:T(8,128)(2,1)S(1)}, bf16[1,1296,128]{2,1,0:T(8,128)(2,1)S(1)}, u32[]{:S(2)}, u32[]{:S(2)}) %collective-permute-start) | collective-permute-done | bytes 331808 | tf_op jit(solution)/shard_map/ppermute | solution.py:237
  67.3 0.1 pad_maximum_fusion.2
  67.3 0.1 collective-permute-start.1
  67.4 5.7 %all-to-all-done.1 = bf16[8,208,128]{2,1,0:T(8,128)(2,1)S(1)} async-done(((bf16[8,208,128]{2,1,0:T(8,128)(2,1)}), bf16[8,208,128]{2,1,0:T(8,128)(2,1)S(1)}, u32[]{:S(2)}, u32[]{:S(2)}) %all-to-all-start.1) | async-done | bytes 426016 | tf_op jit(solution)/shard_map/all_to_all | solution.py:317
  73.1 1.5 reshape.91.bias_ref
  74.6 0.1 convert_element_type.24
  74.7 0.8 slice.42
  75.5 0.6 slice_convert_fusion
  76.1 0.0 collective-permute-done.1
  76.1 0.1 pad_maximum_fusion.patches_ref
  76.2 0.0 copy-start
  76.2 0.7 slice.40.spots_ref
  76.9 0.3 copy-done
  77.3 60.5 %attend.1 = bf16[1024,512]{1,0:T(8,128)(2,1)} custom-call(s32[4]{0:T(128)} %broadcast_xor_fusion.order_ref, s32[64]{0:T(128)} %reshape.70.starts_ref, s32[8]{0:T(128)} %counts_ref.1, bf16[4,1296,128]{2,1,0:T(8,128)(2,1)} %copy-done, bf16[4,1,256]{2,1,0:T(2,128)(2,1)} %slice.40.spots_ref, bf16[1536,128]{1,0:T(8,128)(2,1)} %bitcast.31, ...), custom_call_target="tpu_custom_call" | custom-call | tf_op jit(solution)/shard_map/attend/pallas_call | solution.py:325
  137.8 17.9 %all_to_all.29 = bf16[4,256,512]{2,1,0:T(8,128)(2,1)S(1)} all-to-all(bf16[4,256,512]{2,1,0:T(8,128)(2,1)} %bitcast.28), channel_id=1, replica_groups=mesh['wide'=8,'narrow'=4] {'narrow'}, dimensions={0} | all-to-all | bytes 2097152 | tf_op jit(solution)/shard_map/all_to_all | solution.py:350
  155.7 1.2 copy.24
  156.9 0.0 all-gather.2.cloned.1.call-done.weight_ref
  156.9 10.9 %output.1 = bf16[256,3072]{1,0:T(8,128)(2,1)} custom-call(bf16[256,2048]{1,0:T(8,128)(2,1)} %bitcast.30, bf16[12288,512]{1,0:T(8,128)(2,1)} %all-gather.2.cloned.1.call-done.weight_ref, f32[1,3072]{1,0:T(1,128)} %bitcast.37), custom_call_target="tpu_custom_call" | custom-call | tf_op jit(solution)/shard_map/output/pallas_call | solution.py:354
  (13 shorter events, 0.2 us)
Async XLA Ops:
  6.5 150.4 %all-gather.2.cloned.1.call-start = ((), (), s32[]{:S(2)}) async-start(), calls=%async_computation.3 | async-start | bytes 12976128 | tf_op jit(solution)/shard_map/all_gather | solution.py:264
  19.6 27.9 %all-to-all-start = ((bf16[8,384,128]{2,1,0:T(8,128)(2,1)}), bf16[8,384,128]{2,1,0:T(8,128)(2,1)S(1)}, u32[]{:S(2)}, u32[]{:S(2)}) async-start(bf16[8,384,128]{2,1,0:T(8,128)(2,1)} %pad_maximum_fusion.1), calls=%async_computation | async-start | bytes 1572864 | tf_op jit(solution)/shard_map/all_to_all | solution.py:302
  47.5 9.8 %copy-start.1 = (s32[8,8]{1,0:T(8,128)S(1)}, s32[8,8]{1,0:T(8,128)}, u32[]{:S(2)}) copy-start(s32[8,8]{1,0:T(8,128)} %param.19) | copy-start | bytes 772
  47.6 13.7 %copy-start.2 = (s32[4]{0:T(128)S(1)}, s32[4]{0:T(128)}, u32[]{:S(2)}) copy-start(s32[4]{0:T(128)} %constant.28.clone) | copy-start | bytes 52
  48.5 24.6 %all-to-all-start.1 = ((bf16[8,208,128]{2,1,0:T(8,128)(2,1)}), bf16[8,208,128]{2,1,0:T(8,128)(2,1)S(1)}, u32[]{:S(2)}, u32[]{:S(2)}) async-start(bf16[8,208,128]{2,1,0:T(8,128)(2,1)} %broadcast_in_dim.10), calls=%async_computation.1 | async-start | bytes 851968 | tf_op jit(solution)/shard_map/all_to_all | solution.py:317
  55.8 11.5 %collective-permute-start = (bf16[1,1296,128]{2,1,0:T(8,128)(2,1)S(1)}, bf16[1,1296,128]{2,1,0:T(8,128)(2,1)S(1)}, u32[]{:S(2)}, u32[]{:S(2)}) collective-permute-start(bf16[1,1296,128]{2,1,0:T(8,128)(2,1)S(1)} %maximum_bitcast_fusion), channel_id=1, source_target_pairs={{0,2},{1,3},{2,0},{3,1},{4,6},{5,7},{6,4},{7,5},{8,10},{9,11},{10,... | collective-permute-start | bytes 995336 | tf_op jit(solution)/shard_map/ppermute | solution.py:237
  67.3 8.7 %collective-permute-start.1 = (bf16[2,1296,128]{2,1,0:T(8,128)(2,1)S(1)}, bf16[2,1296,128]{2,1,0:T(8,128)(2,1)S(1)}, u32[]{:S(2)}, u32[]{:S(2)}) collective-permute-start(bf16[2,1296,128]{2,1,0:T(8,128)(2,1)S(1)} %pad_maximum_fusion.2), channel_id=1, source_target_pairs={{0,1},{1,0},{2,3},{3,2},{4,5},{5,4},{6,7},{7,6},{8,9},{9,8},{10,11... | collective-permute-start | bytes 1990664 | tf_op jit(solution)/shard_map/ppermute | solution.py:237
  76.2 1.1 copy-start
Sparse Core Ops, SparseCore 0:
  10.2 110.8 all-gather.1

commit v2 on v1

v2 whole, which is shorter than its diff:
```python
import functools

import jax
import jax.numpy as jnp
from jax import lax
from jax.experimental import pallas as pl
from jax.experimental.pallas import tpu as pltpu
from jax.sharding import PartitionSpec as P

HEAD = 64
NB = 8
KB = 512
QB = 128
REACH = 2
SPAN = 2 * REACH + 1
EPSILON = 1e-06

f32 = jnp.float32
bf16 = jnp.bfloat16
NT = (((1,), (1,)), ((), ()))


def ntdot(a, b):
    return lax.dot_general(a, b, NT, preferred_element_type=f32)


def whole_spec():
    return pl.BlockSpec(memory_space=pltpu.VMEM)


def split3(value):
    high = value.astype(bf16)
    rest = value - high.astype(f32)
    mid = rest.astype(bf16)
    low = (rest - mid.astype(f32)).astype(bf16)
    return high, mid, low


def gram_kernel(embed_ref, gram_ref):
    embed = embed_ref[...].astype(f32)
    width = embed.shape[1]
    centred = embed - jnp.mean(embed, axis=1, keepdims=True)
    gram = lax.dot_general(
        centred, centred, NT, preferred_element_type=f32, precision=lax.Precision.HIGHEST
    ) * (1.0 / width)
    for index, term in enumerate(split3(gram)):
        gram_ref[index] = term


def prep_kernel(
    wide_count,
    sliced,
    at_ref,
    embed_ref,
    slice_ref,
    scale_ref,
    shift_ref,
    qkv_ref,
    latents_ref,
    targets_ref,
    *out_refs,
):
    depth, heads_width = qkv_ref.shape[1:]
    patch = embed_ref.shape[0]
    if sliced:
        own, scale, shift = slice_ref[...], scale_ref[...], shift_ref[...]
    else:
        columns = pl.ds(pl.multiple_of(at_ref[0], 128), depth)
        own, scale, shift = embed_ref[:, columns], scale_ref[:, columns], shift_ref[:, columns]
    piece = 3 * heads_width // wide_count
    row_mean = jnp.mean(embed_ref[...].astype(f32), axis=1, keepdims=True)
    factor = (own.astype(f32) - row_mean) * (1.0 + scale)
    stacked = jnp.concatenate([factor, jnp.broadcast_to(shift, (16, depth))], axis=0)
    high, mid, _ = split3(stacked)
    bias_rows = []
    for part in range(3):
        weights = qkv_ref[part]
        product = jnp.dot(high, weights, preferred_element_type=f32) + jnp.dot(
            mid, weights, preferred_element_type=f32
        )
        for chunk in range(heads_width // 128):
            bias_rows.append(product[patch : patch + 1, chunk * 128 : (chunk + 1) * 128])
        turned = product[0:patch].T
        if part < 2:
            grouped = turned.reshape(heads_width // HEAD, HEAD, patch)
            grouped = grouped - jnp.mean(grouped, axis=1, keepdims=True)
            turned = grouped.reshape(turned.shape)
        turned = turned.astype(bf16)
        top = part * heads_width
        if sliced:
            out_refs[0][top : top + heads_width, :] = turned
            continue
        for receiver in range(wide_count):
            low = max(receiver * piece, top)
            end = min((receiver + 1) * piece, top + heads_width)
            if low < end:
                base = receiver * piece
                out_refs[0][receiver, low - base : end - base, :] = turned[low - top : end - top]
    bias_rows.append(jnp.zeros((16 - len(bias_rows), 128), f32))
    bias = jnp.concatenate(bias_rows, axis=0).astype(bf16)
    row_total = latents_ref.shape[0]
    share = row_total // wide_count
    across = targets_ref[...]
    same = lax.broadcasted_iota(jnp.int32, (row_total, row_total), 0) == lax.broadcasted_iota(
        jnp.int32, (row_total, row_total), 1
    )
    down = jnp.sum(jnp.where(same, across.astype(f32), 0.0), axis=1, keepdims=True)
    across = across.astype(f32)
    slot_across = jnp.sum((down < across).astype(f32), axis=0, keepdims=True)
    slot_down = jnp.sum((across < down).astype(f32), axis=1, keepdims=True)
    local = (down.astype(jnp.int32) % row_total).astype(f32)
    count = -(-SPAN * share // 16) * 16
    latents = latents_ref[...]
    wanted = lax.broadcasted_iota(jnp.int32, (count, row_total), 0)
    lane = lax.broadcasted_iota(jnp.int32, (row_total, 128), 1)
    for receiver in range(wide_count):
        first = (receiver - REACH) * share
        chosen = (slot_across == (wanted + first).astype(f32)) & (wanted < SPAN * share)
        rows = jnp.dot(chosen.astype(bf16), latents, preferred_element_type=f32).astype(bf16)
        mine = (slot_down == (lane + receiver * share).astype(f32)) & (lane < share)
        spots = jnp.sum(jnp.where(mine, local, 0.0), axis=0, keepdims=True)
        spots = jnp.broadcast_to(spots, (16, 128)).astype(bf16)
        if sliced:
            out_refs[1][receiver, 0:16, :] = bias
            out_refs[1][receiver, 16 : 16 + count, :] = rows
            out_refs[1][receiver, 16 + count :, :] = spots
        else:
            out_refs[0][receiver, piece : piece + 16, :] = bias
            out_refs[0][receiver, piece + 16 : piece + 16 + count, :] = rows
            out_refs[0][receiver, piece + 16 + count :, :] = spots


def attend_kernel(
    row_total,
    tile_size,
    order_ref,
    starts_ref,
    counts_ref,
    patches_ref,
    weight_ref,
    bias_ref,
    gram_ref,
    out_ref,
    both_ref,
    keys_ref,
    values_ref,
    twin_ref,
    total_ref,
    even_ref,
    odd_ref,
    block_ref,
    first_ref,
):
    heads_width = out_ref.shape[1]
    local_heads = heads_width // HEAD
    pairs = heads_width // 128
    narrow_count = tile_size // row_total
    block_total = tile_size // QB
    chunks = heads_width // 128

    def doubled(part):
        weight = weight_ref[part * heads_width : (part + 1) * heads_width, :]
        return jnp.concatenate([weight, weight], axis=1)

    def centred_bias(part):
        same = lax.broadcasted_iota(jnp.int32, (128, 128), 0) == lax.broadcasted_iota(
            jnp.int32, (128, 128), 1
        )
        pieces = []
        for chunk in range(chunks):
            row = bias_ref[part * chunks + chunk : part * chunks + chunk + 1, :]
            pieces.append(jnp.sum(jnp.where(same, row, 0.0), axis=1, keepdims=True))
        grouped = jnp.concatenate(pieces, axis=0).reshape(local_heads, HEAD, 1)
        grouped = grouped - jnp.mean(grouped, axis=1, keepdims=True)
        return grouped.reshape(heads_width, 1)

    def unit_heads(turned, bias):
        grouped = (turned + bias).reshape(local_heads, HEAD, turned.shape[1])
        square = jnp.mean(grouped * grouped, axis=1, keepdims=True)
        return (grouped * lax.rsqrt(square + EPSILON)).reshape(turned.shape)

    gram_top = jnp.concatenate([gram_ref[0], gram_ref[1]], axis=0)
    gram_low = gram_ref[2]

    def scale(step, carry):
        block = step // SPAN
        tile = step % SPAN
        rows = patches_ref[block, pl.ds(pl.multiple_of(tile * row_total, row_total), row_total), :]
        wide_rows = rows.astype(f32)
        image = jnp.dot(
            jnp.concatenate([rows, rows], axis=1), gram_top, preferred_element_type=f32
        ) + jnp.dot(rows, gram_low, preferred_element_type=f32)
        variance = jnp.sum(image * wide_rows, axis=1, keepdims=True)
        scaled = wide_rows * lax.rsqrt(jnp.maximum(variance, 0.0) + EPSILON)
        high = scaled.astype(bf16)
        at = pl.multiple_of(tile * tile_size + order_ref[block] * row_total, row_total)
        both_ref[pl.ds(at, row_total), 0:128] = high
        both_ref[pl.ds(at, row_total), 128:256] = (scaled - high.astype(f32)).astype(bf16)
        return carry

    lax.fori_loop(0, SPAN * narrow_count, scale, 0, unroll=SPAN)

    key_bias = centred_bias(1)
    key_weight = doubled(1)
    value_weight = doubled(2).astype(f32).T.astype(bf16)
    value_bias = jnp.concatenate(
        [bias_ref[2 * chunks + chunk : 2 * chunks + chunk + 1, :] for chunk in range(chunks)], axis=1
    )

    def project(step, carry):
        at = pl.multiple_of(step * 256, 256)
        both = both_ref[pl.ds(at, 256), :]
        keys_ref[:, pl.ds(at, 256)] = unit_heads(ntdot(key_weight, both), key_bias).astype(bf16)
        values_ref[pl.ds(at, 256), :] = (
            jnp.dot(both, value_weight, preferred_element_type=f32) + value_bias
        ).astype(bf16)
        return carry

    lax.fori_loop(0, SPAN * tile_size // 256, project, 0, unroll=2)

    query_bias = centred_bias(0)
    query_weight = doubled(0)
    left = lax.broadcasted_iota(jnp.int32, (QB, 128), 1) < HEAD
    spot_rows = row_total // 128

    def ask(block, carry):
        place = order_ref[block] * row_total
        spots = jnp.concatenate(
            [
                patches_ref[block, SPAN * row_total + row : SPAN * row_total + row + 1, :]
                for row in range(spot_rows)
            ],
            axis=1,
        )
        wanted = lax.broadcasted_iota(jnp.int32, (row_total, row_total), 0).astype(f32)
        chosen = (spots.astype(f32) == wanted).astype(bf16)
        both = both_ref[pl.ds(pl.multiple_of(REACH * tile_size + place, row_total), row_total), :]
        placed = jnp.dot(chosen, both, preferred_element_type=f32).astype(bf16)
        turned = unit_heads(ntdot(query_weight, placed), query_bias).astype(bf16).astype(f32) * 0.125
        rows = turned.T.astype(bf16)
        for part in range(row_total // QB):
            query = order_ref[block] * (row_total // QB) + part
            for pair in range(pairs):
                piece = rows[part * QB : (part + 1) * QB, pair * 128 : (pair + 1) * 128]
                twin_ref[query, pair, 0:QB, :] = jnp.where(left, piece, jnp.zeros_like(piece))
                twin_ref[query, pair, QB : 2 * QB, :] = jnp.where(left, jnp.zeros_like(piece), piece)
        return carry

    lax.fori_loop(0, narrow_count, ask, 0)

    def listed(block, count):
        total_ref[block] = jnp.zeros_like(total_ref[block])

        def note(slot, inner):
            block_ref[count + slot] = block
            first_ref[count + slot] = starts_ref[block * NB + slot]
            return inner

        lax.fori_loop(0, counts_ref[block], note, 0)
        return count + counts_ref[block]

    steps = lax.fori_loop(0, block_total, listed, 0)
    for extra in range(2):
        block_ref[steps + extra] = block_total
        first_ref[steps + extra] = first_ref[0]

    ones = jnp.ones((KB, 128), bf16)

    def weigh(step, weights_ref):
        start = pl.multiple_of(first_ref[step], KB)
        query = jnp.minimum(block_ref[step], block_total - 1)
        for pair in range(pairs):
            scores = jnp.dot(
                twin_ref[query, pair],
                keys_ref[pair * 128 : (pair + 1) * 128, pl.ds(start, KB)],
                preferred_element_type=f32,
            )
            weights_ref[pair] = jnp.exp(scores).astype(bf16)

    def gather(step, weights_ref):
        start = pl.multiple_of(first_ref[step], KB)
        block = block_ref[step]
        for pair in range(pairs):
            side = jnp.concatenate(
                [values_ref[pl.ds(start, KB), pair * 128 : (pair + 1) * 128], ones], axis=1
            )
            total_ref[block, pair] += jnp.dot(weights_ref[pair], side, preferred_element_type=f32)

    weigh(0, even_ref)

    def visit(twice, carry):
        step = twice * 2
        weigh(step + 1, odd_ref)
        gather(step, even_ref)
        weigh(step + 2, even_ref)
        gather(step + 1, odd_ref)
        return carry

    lax.fori_loop(0, (steps + 1) // 2, visit, 0)

    def finish(block, carry):
        for pair in range(pairs):
            both = total_ref[block, pair, :, 0:128] / total_ref[block, pair, :, 128:256]
            out_ref[pl.ds(pl.multiple_of(block * QB, QB), QB), pair * 128 : (pair + 1) * 128] = (
                jnp.where(left, both[0:QB], both[QB : 2 * QB]).astype(bf16)
            )
        return carry

    lax.fori_loop(0, block_total, finish, 0)


def attend_scratch(row_total, tile_size, heads_width):
    pairs = heads_width // 128
    blocks = tile_size // QB
    return [
        pltpu.VMEM((SPAN * tile_size, 256), bf16),
        pltpu.VMEM((heads_width, SPAN * tile_size), bf16),
        pltpu.VMEM((SPAN * tile_size, heads_width), bf16),
        pltpu.VMEM((blocks, pairs, 2 * QB, 128), bf16),
        pltpu.VMEM((blocks + 1, pairs, 2 * QB, 256), f32),
        pltpu.VMEM((pairs, 2 * QB, KB), bf16),
        pltpu.VMEM((pairs, 2 * QB, KB), bf16),
        pltpu.SMEM((blocks * NB + 2,), jnp.int32),
        pltpu.SMEM((blocks * NB + 2,), jnp.int32),
    ]


def output_kernel(narrow_count, attended_ref, weight_ref, gate_ref, out_ref):
    rows = weight_ref.shape[0] // narrow_count
    width = weight_ref.shape[1]
    total = None
    for index in range(narrow_count):
        term = ntdot(
            attended_ref[:, index * width : (index + 1) * width],
            weight_ref[index * rows : (index + 1) * rows, :],
        )
        total = term if total is None else total + term
    out_ref[...] = (total * gate_ref[...]).astype(bf16)


def flip(block, axis, bit):
    devices = range(lax.axis_size(axis))
    return lax.ppermute(block, axis, [(i, i ^ bit) for i in devices])


def per_device(
    latents,
    targets,
    embed_weight,
    mod_shift,
    mod_scale,
    qkv_weight,
    out_weight,
    mod_gate,
    block_list,
    block_count,
):
    row_total, patch = latents.shape
    width = embed_weight.shape[1]
    wide_count = lax.axis_size("wide")
    narrow_count = lax.axis_size("narrow")
    wide_index = lax.axis_index("wide")
    narrow_index = lax.axis_index("narrow")
    tile_size = row_total * narrow_count
    depth, heads_width = qkv_weight.shape[1:]
    share = row_total // wide_count
    count = -(-SPAN * share // 16) * 16
    piece = 3 * heads_width // wide_count

    out_all = lax.all_gather(out_weight, ("wide", "narrow"), axis=0, tiled=True)

    first = wide_index * depth
    extra = 16 + count + 16
    sliced = depth % 128 != 0 or piece % 16 != 0
    scale = mod_scale.reshape(1, width)
    shift = mod_shift.reshape(1, width)
    own = embed_weight
    if sliced:
        own, scale, shift = (
            lax.dynamic_slice_in_dim(array, first, depth, 1) for array in (own, scale, shift)
        )
        prep_shapes = (
            jax.ShapeDtypeStruct((3 * heads_width, patch), bf16),
            jax.ShapeDtypeStruct((wide_count, extra, patch), bf16),
        )
    else:
        prep_shapes = (jax.ShapeDtypeStruct((wide_count, piece + extra, patch), bf16),)
    smem = pl.BlockSpec(memory_space=pltpu.SMEM)
    prepared = pl.pallas_call(
        functools.partial(prep_kernel, wide_count, sliced),
        out_shape=prep_shapes,
        in_specs=[smem] + [whole_spec()] * 7,
        out_specs=tuple(whole_spec() for _ in prep_shapes),
        name="prep",
    )(
        first.astype(jnp.int32).reshape(1),
        embed_weight,
        own,
        scale,
        shift,
        qkv_weight,
        latents,
        targets.reshape(1, row_total),
    )
    payload = prepared[0]
    if sliced:
        payload = jnp.concatenate(
            [payload.reshape(wide_count, piece, patch), prepared[1]], axis=1
        )
    gram = pl.pallas_call(
        gram_kernel,
        out_shape=jax.ShapeDtypeStruct((3, patch, patch), bf16),
        in_specs=[whole_spec()],
        out_specs=whole_spec(),
        name="gram",
    )(embed_weight)
    arrived = lax.all_to_all(payload, "wide", split_axis=0, concat_axis=0, tiled=True)

    summed = jnp.sum(arrived[:, :piece].astype(f32), axis=0).astype(bf16)
    bias = jnp.sum(arrived[:, piece : piece + 16].astype(f32), axis=0)
    spread = jnp.broadcast_to(summed[None], (wide_count,) + summed.shape)
    near = arrived[:, piece + 16 : piece + 16 + SPAN * share]
    near = near.reshape(wide_count, SPAN, share, patch).transpose(1, 0, 2, 3)
    near = near.reshape(SPAN * row_total, patch)
    mine = arrived[:, piece + 16 + count, :share].reshape(-1)
    mine = jnp.pad(mine, (0, 16 * 128 - row_total)).reshape(16, 128)
    group = jnp.concatenate([near, mine], axis=0)[None]
    order = [0]
    bits = [1 << k for k in range(1, narrow_count.bit_length() - 1)] + [1]
    for bit in bits:
        group = jnp.concatenate([group, flip(group, "narrow", bit)], axis=0)
        order = order + [index ^ bit for index in order]
    everything = lax.all_to_all(spread, "wide", split_axis=0, concat_axis=0, tiled=True)
    weight_all = everything.reshape(3 * heads_width, patch)

    order_ids = jnp.bitwise_xor(jnp.array(order, jnp.int32), narrow_index)
    starts = (block_list * KB - (wide_index - REACH) * tile_size).reshape(-1)
    attended = pl.pallas_call(
        functools.partial(attend_kernel, row_total, tile_size),
        out_shape=jax.ShapeDtypeStruct((tile_size, heads_width), bf16),
        in_specs=[smem] * 3 + [whole_spec()] * 4,
        out_specs=whole_spec(),
        scratch_shapes=attend_scratch(row_total, tile_size, heads_width),
        name="attend",
    )(order_ids, starts, block_count, group, weight_all, bias, gram)

    merged = lax.all_to_all(attended, "narrow", split_axis=0, concat_axis=1, tiled=True)
    out_rows = out_weight.shape[0]
    gate = mod_gate.reshape(1, width)
    if out_rows % 128 == 0:
        return pl.pallas_call(
            functools.partial(output_kernel, narrow_count),
            grid=(wide_count,),
            out_shape=jax.ShapeDtypeStruct((row_total, width), bf16),
            in_specs=[
                pl.BlockSpec((row_total, narrow_count * heads_width), lambda i: (0, 0)),
                pl.BlockSpec((narrow_count * out_rows, heads_width), lambda i: (i, 0)),
                pl.BlockSpec((1, out_rows), lambda i: (0, i)),
            ],
            out_specs=pl.BlockSpec((row_total, out_rows), lambda i: (0, i)),
            name="output",
        )(merged, out_all, gate)
    weights = out_all.reshape(wide_count, narrow_count, out_rows, heads_width)
    product = jnp.einsum(
        "tnk,wnfk->twf",
        merged.reshape(row_total, narrow_count, heads_width),
        weights,
        preferred_element_type=f32,
    )
    return (gate * product.reshape(row_total, width)).astype(bf16)


def solution(mesh):
    in_specs = (
        P(("wide", "narrow"), None),
        P(("wide", "narrow")),
        P(),
        P(),
        P(),
        P(None, "wide", "narrow"),
        P("wide", "narrow"),
        P(),
        P("wide", None),
        P("wide"),
    )
    out_specs = P(("wide", "narrow"), None)
    return jax.shard_map(
        per_device, mesh=mesh, in_specs=in_specs, out_specs=out_specs, check_vma=False
    )
```

time: 176 us -> 162 us (0.920)
  the two profiles are of different devices: /device:TPU:16 before, /device:TPU:4 now
where the time goes in v2:
time: 162 us; the launch traced here: 160 us
  Pallas kernels  59.9 us (37%)
  blocking collectives  52.2 us (32%)
  waiting for transfers between devices  23.4 us (14%)
  between operations  13.5 us (8%)
  starting transfers between devices  5.47 us (3%)
  local copies, waits for them, and re-layouts  3.49 us (2%)
  other arithmetic  2.51 us (2%)
    pallas_call x1, Pallas kernels, per_device(): pl.pallas_call(functools.partial(attend_kernel, row_total, tile_size), ou...  41.8 us
    all_to_all x1, blocking collectives, per_device(): lax.all_to_all(payload, 'wide', split_axis=0, concat_axis=0, tiled=True)  34.3 us
    all_to_all x1, blocking collectives, per_device(): lax.all_to_all(attended, 'narrow', split_axis=0, concat_axis=1, tiled=True)  17.9 us
    ppermute x2, waiting for transfers between devices, flip(): return lax.ppermute(block, axis, [(i, i ^ bit) for i in devices])  14 us
    pallas_call x1, Pallas kernels, per_device(): pl.pallas_call(functools.partial(output_kernel, narrow_count), grid=(wide...  10.9 us
    all_to_all x1, waiting for transfers between devices, per_device(): lax.all_to_all(spread, 'wide', split_axis=0, concat_axis=0, tiled=True)  8.6 us
    all_to_all x1, starting transfers between devices, per_device(): lax.all_to_all(spread, 'wide', split_axis=0, concat_axis=0, tiled=True)  3.85 us
    pallas_call x1, Pallas kernels, per_device(): pl.pallas_call(functools.partial(prep_kernel, wide_count, sliced), out_sh...  3.64 us
  transfers between devices with their start and end apart: 4, of which 2 were waited for; matrix products, arithmetic and copies ran while one was open for 3% of the time, Pallas kernels for 31%

profile of v2, /device:TPU:4, one launch (start us, length us, event | category | flops | bytes accessed | tf_op | source)
XLA Modules:
  0.0 160.4 jit_solution(11461327253176422590)
XLA Ops:
  6.5 0.0 all-gather.2.cloned.1.call-start
  6.5 0.7 all-gather.2.cloned.1.call-update
  7.3 3.6 %prep.1 = bf16[8,384,128]{2,1,0:T(8,128)(2,1)} custom-call(s32[1]{0:T(128)} %bitcast.at_ref, bf16[128,3072]{1,0:T(8,128)(2,1)} %embed_ref.3, bf16[128,3072]{1,0:T(8,128)(2,1)} %embed_ref.3, f32[1,3072]{1,0:T(1,128)} %bitcast.25, f32[1,3072]{1,0:T(1,128)} %bitcast.26, bf16[3,384,512]{2,1,0:T(8,128)(2,1)} %qkv_ref.1, bf16[256,128]{1,0:T(8,128)(2,1)} %latents_ref.1, ...), custom_call_target="tpu_custom_call" | custom-call | tf_op jit(solution)/shard_map/prep/pallas_call | solution.py:389
  10.9 34.3 %all_to_all.29 = bf16[8,384,128]{2,1,0:T(8,128)(2,1)S(1)} all-to-all(bf16[8,384,128]{2,1,0:T(8,128)(2,1)} %prep.1), channel_id=1, replica_groups=mesh['wide'=8,'narrow'=4] {'wide'}, dimensions={0} | all-to-all | bytes 1572864 | tf_op jit(solution)/shard_map/all_to_all | solution.py:417
  45.3 0.1 reshape_squeeze.3
  45.4 1.5 collective-permute-start
  47.0 0.0 copy-start.1
  47.0 14.0 %collective-permute-done = bf16[1,1296,128]{2,1,0:T(8,128)(2,1)S(1)} collective-permute-done((bf16[1,1296,128]{2,1,0:T(8,128)(2,1)S(1)}, bf16[1,1296,128]{2,1,0:T(8,128)(2,1)S(1)}, u32[]{:S(2)}, u32[]{:S(2)}) %collective-permute-start) | collective-permute-done | bytes 331808 | tf_op jit(solution)/shard_map/ppermute | solution.py:343
  61.0 0.1 pad_maximum_fusion.1
  61.1 0.0 copy-start.2
  61.1 0.1 collective-permute-start.1
  61.2 0.1 slice_reduce_fusion
  61.2 0.8 broadcast_in_dim.10
  62.0 3.9 %all-to-all-start.1 = ((bf16[8,192,128]{2,1,0:T(8,128)(2,1)}), bf16[8,192,128]{2,1,0:T(8,128)(2,1)S(1)}, u32[]{:S(2)}, u32[]{:S(2)}) async-start(bf16[8,192,128]{2,1,0:T(8,128)(2,1)} %broadcast_in_dim.10), calls=%async_computation.1 | async-start | bytes 786432 | tf_op jit(solution)/shard_map/all_to_all | solution.py:433
  65.9 0.0 copy-done.1
  65.9 3.5 %gram.1.gram_ref = bf16[3,128,128]{2,1,0:T(8,128)(2,1)} custom-call(bf16[128,3072]{1,0:T(8,128)(2,1)} %embed_ref.3), custom_call_target="tpu_custom_call" | custom-call | tf_op jit(solution)/shard_map/gram/pallas_call | solution.py:410
  69.4 0.6 reshape.34.starts_ref
  70.0 0.0 copy-done.2
  70.0 0.6 broadcast_xor_fusion.order_ref
  70.6 0.6 convert_reduce_fusion.bias_ref
  71.2 0.0 collective-permute-done.1
  71.2 1.2 pad_maximum_fusion.patches_ref
  72.4 8.6 %all-to-all-done.1 = bf16[8,192,128]{2,1,0:T(8,128)(2,1)S(1)} async-done(((bf16[8,192,128]{2,1,0:T(8,128)(2,1)}), bf16[8,192,128]{2,1,0:T(8,128)(2,1)S(1)}, u32[]{:S(2)}, u32[]{:S(2)}) %all-to-all-start.1) | async-done | bytes 393248 | tf_op jit(solution)/shard_map/all_to_all | solution.py:433
  81.0 0.0 copy-start
  81.0 0.7 copy-done
  81.7 41.8 %attend.1 = bf16[1024,512]{1,0:T(8,128)(2,1)} custom-call(s32[4]{0:T(128)} %broadcast_xor_fusion.order_ref, s32[64]{0:T(128)} %reshape.34.starts_ref, s32[8]{0:T(128)} %counts_ref.1, bf16[4,1296,128]{2,1,0:T(8,128)(2,1)} %pad_maximum_fusion.patches_ref, bf16[1536,128]{1,0:T(8,128)(2,1)} %bitcast.21, f32[16,128]{1,0:T(8,128)} %convert_reduce_fusion.bias_ref, ...), custom_call_target="tpu_custom_call" | custom-call | tf_op jit(solution)/shard_map/attend/pallas_call | solution.py:438
  123.6 17.9 %all_to_all.30 = bf16[4,256,512]{2,1,0:T(8,128)(2,1)S(1)} all-to-all(bf16[4,256,512]{2,1,0:T(8,128)(2,1)} %bitcast.18), channel_id=1, replica_groups=mesh['wide'=8,'narrow'=4] {'narrow'}, dimensions={0} | all-to-all | bytes 2097152 | tf_op jit(solution)/shard_map/all_to_all | solution.py:447
  141.5 1.2 copy.18
  142.6 0.0 all-gather.2.cloned.1.call-done.weight_ref
  142.6 10.9 %output.1 = bf16[256,3072]{1,0:T(8,128)(2,1)} custom-call(bf16[256,2048]{1,0:T(8,128)(2,1)} %bitcast.20, bf16[12288,512]{1,0:T(8,128)(2,1)} %all-gather.2.cloned.1.call-done.weight_ref, f32[1,3072]{1,0:T(1,128)} %bitcast.24), custom_call_target="tpu_custom_call" | custom-call | tf_op jit(solution)/shard_map/output/pallas_call | solution.py:451
  (6 shorter events, 0.1 us)
Async XLA Ops:
  6.5 136.1 %all-gather.2.cloned.1.call-start = ((), (), s32[]{:S(2)}) async-start(), calls=%async_computation.3 | async-start | bytes 12976128 | tf_op jit(solution)/shard_map/all_gather | solution.py:370
  45.4 15.6 %collective-permute-start = (bf16[1,1296,128]{2,1,0:T(8,128)(2,1)S(1)}, bf16[1,1296,128]{2,1,0:T(8,128)(2,1)S(1)}, u32[]{:S(2)}, u32[]{:S(2)}) collective-permute-start(bf16[1,1296,128]{2,1,0:T(8,128)(2,1)S(1)} %maximum_bitcast_fusion), channel_id=1, source_target_pairs={{0,2},{1,3},{2,0},{3,1},{4,6},{5,7},{6,4},{7,5},{8,10},{9,11},{10,... | collective-permute-start | bytes 995336 | tf_op jit(solution)/shard_map/ppermute | solution.py:343
  47.0 18.9 %copy-start.1 = (s32[8,8]{1,0:T(8,128)S(1)}, s32[8,8]{1,0:T(8,128)}, u32[]{:S(2)}) copy-start(s32[8,8]{1,0:T(8,128)} %param.19) | copy-start | bytes 772
  61.1 8.9 %copy-start.2 = (s32[4]{0:T(128)S(1)}, s32[4]{0:T(128)}, u32[]{:S(2)}) copy-start(s32[4]{0:T(128)} %constant.26.clone) | copy-start | bytes 52
  61.1 10.1 %collective-permute-start.1 = (bf16[2,1296,128]{2,1,0:T(8,128)(2,1)S(1)}, bf16[2,1296,128]{2,1,0:T(8,128)(2,1)S(1)}, u32[]{:S(2)}, u32[]{:S(2)}) collective-permute-start(bf16[2,1296,128]{2,1,0:T(8,128)(2,1)S(1)} %pad_maximum_fusion.1), channel_id=1, source_target_pairs={{0,1},{1,0},{2,3},{3,2},{4,5},{5,4},{6,7},{7,6},{8,9},{9,8},{10,11... | collective-permute-start | bytes 1990664 | tf_op jit(solution)/shard_map/ppermute | solution.py:343
  62.0 18.9 %all-to-all-start.1 = ((bf16[8,192,128]{2,1,0:T(8,128)(2,1)}), bf16[8,192,128]{2,1,0:T(8,128)(2,1)S(1)}, u32[]{:S(2)}, u32[]{:S(2)}) async-start(bf16[8,192,128]{2,1,0:T(8,128)(2,1)} %broadcast_in_dim.10), calls=%async_computation.1 | async-start | bytes 786432 | tf_op jit(solution)/shard_map/all_to_all | solution.py:433
  81.0 0.7 copy-start
Sparse Core Ops, SparseCore 0:
  10.2 113.4 all-gather.1

commit v3 on v2

--- a/solution.py
+++ b/solution.py
@@ -14,6 +14,9 @@
 REACH = 2
 SPAN = 2 * REACH + 1
 EPSILON = 1e-06
+PROJECT_VMEM = 32 << 20
+ATTEND_VMEM = 32 << 20
+OUTPUT_VMEM = 53 << 20
 
 f32 = jnp.float32
 bf16 = jnp.bfloat16
@@ -130,32 +133,23 @@
             out_refs[0][receiver, piece + 16 + count :, :] = spots
 
 
-def attend_kernel(
+def project_kernel(
     row_total,
     tile_size,
     order_ref,
-    starts_ref,
-    counts_ref,
     patches_ref,
     weight_ref,
     bias_ref,
     gram_ref,
-    out_ref,
-    both_ref,
     keys_ref,
     values_ref,
     twin_ref,
-    total_ref,
-    even_ref,
-    odd_ref,
-    block_ref,
-    first_ref,
+    both_ref,
 ):
-    heads_width = out_ref.shape[1]
+    heads_width = keys_ref.shape[0]
     local_heads = heads_width // HEAD
     pairs = heads_width // 128
     narrow_count = tile_size // row_total
-    block_total = tile_size // QB
     chunks = heads_width // 128
 
     def doubled(part):
@@ -248,27 +242,38 @@
 
     lax.fori_loop(0, narrow_count, ask, 0)
 
-    def listed(block, count):
-        total_ref[block] = jnp.zeros_like(total_ref[block])
+
+def attend_kernel(
+    parts, chunk, order_ref, starts_ref, counts_ref, keys_ref, values_ref, twin_ref, *rest
+):
+    out_refs = rest[:-5]
+    total_ref, even_ref, odd_ref, block_ref, first_ref = rest[-5:]
+    receivers = len(out_refs)
+    pairs = twin_ref.shape[1]
+    left = lax.broadcasted_iota(jnp.int32, (QB, 128), 1) < HEAD
+
+    def listed(index, count):
+        total_ref[index] = jnp.zeros_like(total_ref[index])
+        block = index * parts + chunk
 
         def note(slot, inner):
-            block_ref[count + slot] = block
+            block_ref[count + slot] = index
             first_ref[count + slot] = starts_ref[block * NB + slot]
             return inner
 
         lax.fori_loop(0, counts_ref[block], note, 0)
         return count + counts_ref[block]
 
-    steps = lax.fori_loop(0, block_total, listed, 0)
+    steps = lax.fori_loop(0, receivers, listed, 0)
     for extra in range(2):
-        block_ref[steps + extra] = block_total
+        block_ref[steps + extra] = receivers
         first_ref[steps + extra] = first_ref[0]
 
     ones = jnp.ones((KB, 128), bf16)
 
     def weigh(step, weights_ref):
         start = pl.multiple_of(first_ref[step], KB)
-        query = jnp.minimum(block_ref[step], block_total - 1)
+        query = jnp.minimum(block_ref[step], receivers - 1) * parts + chunk
         for pair in range(pairs):
             scores = jnp.dot(
                 twin_ref[query, pair],
@@ -298,44 +303,42 @@
 
     lax.fori_loop(0, (steps + 1) // 2, visit, 0)
 
-    def finish(block, carry):
+    for away in range(receivers):
+        block = order_ref[0] ^ away
         for pair in range(pairs):
             both = total_ref[block, pair, :, 0:128] / total_ref[block, pair, :, 128:256]
-            out_ref[pl.ds(pl.multiple_of(block * QB, QB), QB), pair * 128 : (pair + 1) * 128] = (
-                jnp.where(left, both[0:QB], both[QB : 2 * QB]).astype(bf16)
-            )
-        return carry
-
-    lax.fori_loop(0, block_total, finish, 0)
-
-
-def attend_scratch(row_total, tile_size, heads_width):
+            out_refs[away][:, pair * 128 : (pair + 1) * 128] = jnp.where(
+                left, both[0:QB], both[QB : 2 * QB]
+            ).astype(bf16)
+
+
+def attend_scratch(receivers, heads_width):
     pairs = heads_width // 128
-    blocks = tile_size // QB
     return [
-        pltpu.VMEM((SPAN * tile_size, 256), bf16),
-        pltpu.VMEM((heads_width, SPAN * tile_size), bf16),
-        pltpu.VMEM((SPAN * tile_size, heads_width), bf16),
-        pltpu.VMEM((blocks, pairs, 2 * QB, 128), bf16),
-        pltpu.VMEM((blocks + 1, pairs, 2 * QB, 256), f32),
+        pltpu.VMEM((receivers + 1, pairs, 2 * QB, 256), f32),
         pltpu.VMEM((pairs, 2 * QB, KB), bf16),
         pltpu.VMEM((pairs, 2 * QB, KB), bf16),
-        pltpu.SMEM((blocks * NB + 2,), jnp.int32),
-        pltpu.SMEM((blocks * NB + 2,), jnp.int32),
+        pltpu.SMEM((receivers * NB + 2,), jnp.int32),
+        pltpu.SMEM((receivers * NB + 2,), jnp.int32),
     ]
 
 
-def output_kernel(narrow_count, attended_ref, weight_ref, gate_ref, out_ref):
-    rows = weight_ref.shape[0] // narrow_count
-    width = weight_ref.shape[1]
-    total = None
-    for index in range(narrow_count):
-        term = ntdot(
-            attended_ref[:, index * width : (index + 1) * width],
-            weight_ref[index * rows : (index + 1) * rows, :],
-        )
-        total = term if total is None else total + term
-    out_ref[...] = (total * gate_ref[...]).astype(bf16)
+def output_kernel(parts, narrow_count, together, order_ref, *refs):
+    attended_refs = refs[: parts * narrow_count]
+    weight_ref, gate_ref, out_ref = refs[parts * narrow_count :]
+    rows = out_ref.shape[1] // together
+    totals = [None] * together
+    for away in range(narrow_count):
+        attended = jnp.concatenate(
+            [attended_refs[chunk * narrow_count + away][...] for chunk in range(parts)], axis=0
+        )
+        for index in range(together):
+            at = pl.multiple_of((index * narrow_count + (order_ref[0] ^ away)) * rows, 16)
+            term = ntdot(attended, weight_ref[pl.ds(at, rows), :])
+            totals[index] = term if away == 0 else totals[index] + term
+    for index, total in enumerate(totals):
+        columns = slice(index * rows, (index + 1) * rows)
+        out_ref[:, columns] = (total * gate_ref[:, columns]).astype(bf16)
 
 
 def flip(block, axis, bit):
@@ -343,7 +346,11 @@
     return lax.ppermute(block, axis, [(i, i ^ bit) for i in devices])
 
 
-def per_device(
+def cost(flops, moved):
+    return pl.CostEstimate(flops=flops, bytes_accessed=moved, transcendentals=0)
+
+
+def block(
     latents,
     targets,
     embed_weight,
@@ -428,45 +435,73 @@
     order = [0]
     bits = [1 << k for k in range(1, narrow_count.bit_length() - 1)] + [1]
     for bit in bits:
-        group = jnp.concatenate([group, flip(group, "narrow", bit)], axis=0)
+        other = flip(group, "narrow", bit)
+        group = jnp.concatenate([group, other], axis=0)
         order = order + [index ^ bit for index in order]
     everything = lax.all_to_all(spread, "wide", split_axis=0, concat_axis=0, tiled=True)
     weight_all = everything.reshape(3 * heads_width, patch)
 
     order_ids = jnp.bitwise_xor(jnp.array(order, jnp.int32), narrow_index)
     starts = (block_list * KB - (wide_index - REACH) * tile_size).reshape(-1)
-    attended = pl.pallas_call(
-        functools.partial(attend_kernel, row_total, tile_size),
-        out_shape=jax.ShapeDtypeStruct((tile_size, heads_width), bf16),
-        in_specs=[smem] * 3 + [whole_spec()] * 4,
-        out_specs=whole_spec(),
-        scratch_shapes=attend_scratch(row_total, tile_size, heads_width),
-        name="attend",
-    )(order_ids, starts, block_count, group, weight_all, bias, gram)
-
-    merged = lax.all_to_all(attended, "narrow", split_axis=0, concat_axis=1, tiled=True)
+    parts = row_total // QB
+    pairs = heads_width // 128
+    keys, values, twin = pl.pallas_call(
+        functools.partial(project_kernel, row_total, tile_size),
+        out_shape=(
+            pltpu.VMEM((heads_width, SPAN * tile_size), bf16),
+            pltpu.VMEM((SPAN * tile_size, heads_width), bf16),
+            pltpu.VMEM((tile_size // QB, pairs, 2 * QB, 128), bf16),
+        ),
+        in_specs=[smem] + [whole_spec()] * 4,
+        out_specs=(whole_spec(),) * 3,
+        scratch_shapes=[pltpu.VMEM((SPAN * tile_size, 256), bf16)],
+        compiler_params=pltpu.CompilerParams(vmem_limit_bytes=PROJECT_VMEM),
+        cost_estimate=cost(10 * SPAN * tile_size * patch * heads_width, 16 << 20),
+        name="project",
+    )(order_ids, group, weight_all, bias, gram)
+
+    pieces = []
+    for chunk in range(parts):
+        mine = pl.pallas_call(
+            functools.partial(attend_kernel, parts, chunk),
+            out_shape=(jax.ShapeDtypeStruct((QB, heads_width), bf16),) * narrow_count,
+            in_specs=[smem] * 3 + [whole_spec()] * 3,
+            out_specs=(whole_spec(),) * narrow_count,
+            scratch_shapes=attend_scratch(narrow_count, heads_width),
+            compiler_params=pltpu.CompilerParams(vmem_limit_bytes=ATTEND_VMEM),
+            cost_estimate=cost(4 * tile_size // parts * NB * KB * heads_width, 16 << 20),
+        )(order_ids, starts, block_count, keys, values, twin)
+        pieces.append(mine[0])
+        for away in range(1, narrow_count):
+            pieces.append(flip(mine[away], "narrow", away))
+
     out_rows = out_weight.shape[0]
     gate = mod_gate.reshape(1, width)
     if out_rows % 128 == 0:
+        together = 2 if wide_count % 2 == 0 else 1
+        span = together * out_rows
         return pl.pallas_call(
-            functools.partial(output_kernel, narrow_count),
-            grid=(wide_count,),
+            functools.partial(output_kernel, parts, narrow_count, together),
+            grid=(wide_count // together,),
             out_shape=jax.ShapeDtypeStruct((row_total, width), bf16),
-            in_specs=[
-                pl.BlockSpec((row_total, narrow_count * heads_width), lambda i: (0, 0)),
-                pl.BlockSpec((narrow_count * out_rows, heads_width), lambda i: (i, 0)),
-                pl.BlockSpec((1, out_rows), lambda i: (0, i)),
+            in_specs=[smem]
+            + [pl.BlockSpec((QB, heads_width), lambda i: (0, 0))] * (parts * narrow_count)
+            + [
+                pl.BlockSpec((narrow_count * span, heads_width), lambda i: (i, 0)),
+                pl.BlockSpec((1, span), lambda i: (0, i)),
             ],
-            out_specs=pl.BlockSpec((row_total, out_rows), lambda i: (0, i)),
+            out_specs=pl.BlockSpec((row_total, span), lambda i: (0, i)),
+            compiler_params=pltpu.CompilerParams(vmem_limit_bytes=OUTPUT_VMEM),
             name="output",
-        )(merged, out_all, gate)
+        )(order_ids, *pieces, out_all, gate)
     weights = out_all.reshape(wide_count, narrow_count, out_rows, heads_width)
-    product = jnp.einsum(
-        "tnk,wnfk->twf",
-        merged.reshape(row_total, narrow_count, heads_width),
-        weights,
-        preferred_element_type=f32,
-    )
+    product = 0.0
+    for away in range(narrow_count):
+        attended = jnp.concatenate(pieces[away::narrow_count], axis=0)
+        weight = lax.dynamic_index_in_dim(weights, narrow_index ^ away, 1, False)
+        product = product + jnp.einsum(
+            "tk,wfk->twf", attended, weight, preferred_element_type=f32
+        )
     return (gate * product.reshape(row_total, width)).astype(bf16)
 
 
@@ -484,6 +519,4 @@
         P("wide"),
     )
     out_specs = P(("wide", "narrow"), None)
-    return jax.shard_map(
-        per_device, mesh=mesh, in_specs=in_specs, out_specs=out_specs, check_vma=False
-    )
+    return jax.shard_map(block, mesh=mesh, in_specs=in_specs, out_specs=out_specs, check_vma=False)

time: 162 us -> 152 us (0.938)
  the two profiles are of different devices: /device:TPU:4 before, /device:TPU:25 now
where the time goes in v3:
time: 152 us; the launch traced here: 151 us
  Pallas kernels  56.9 us (37%)
  blocking collectives  31.5 us (21%)
  waiting for transfers between devices  29 us (19%)
  starting transfers between devices  17.8 us (12%)
  between operations  13.5 us (9%)
    all_to_all x1, blocking collectives, block(): lax.all_to_all(payload, 'wide', split_axis=0, concat_axis=0, tiled=True)  31.5 us
    pallas_call x2, Pallas kernels, block(): pl.pallas_call(functools.partial(attend_kernel, parts, chunk), out_shape=...  30.6 us
    ppermute x8, waiting for transfers between devices, flip(): return lax.ppermute(block, axis, [(i, i ^ bit) for i in devices])  18.8 us
    ppermute x8, starting transfers between devices, flip(): return lax.ppermute(block, axis, [(i, i ^ bit) for i in devices])  10.7 us
    pallas_call x1, Pallas kernels, block(): pl.pallas_call(functools.partial(project_kernel, row_total, tile_size), o...  10.5 us
    all_to_all x1, waiting for transfers between devices, block(): lax.all_to_all(spread, 'wide', split_axis=0, concat_axis=0, tiled=True)  9.44 us
    pallas_call x1, Pallas kernels, block(): pl.pallas_call(functools.partial(output_kernel, parts, narrow_count, toge...  8.71 us
    all_to_all x1, starting transfers between devices, block(): lax.all_to_all(spread, 'wide', split_axis=0, concat_axis=0, tiled=True)  7.14 us
  transfers between devices with their start and end apart: 10, of which 6 were waited for; matrix products, arithmetic and copies ran while one was open for 2% of the time, Pallas kernels for 32%

profile of v3, /device:TPU:25, one launch (start us, length us, event | category | flops | bytes accessed | tf_op | source)
XLA Modules:
  0.0 151.2 jit_solution(10021799235795124834)
XLA Ops:
  6.5 0.0 all-gather.2.cloned.1.call-start
  6.5 0.7 all-gather.2.cloned.1.call-update
  7.3 3.6 %prep.1 = bf16[8,384,128]{2,1,0:T(8,128)(2,1)} custom-call(s32[1]{0:T(128)} %bitcast.at_ref, bf16[128,3072]{1,0:T(8,128)(2,1)} %embed_ref.3, bf16[128,3072]{1,0:T(8,128)(2,1)} %embed_ref.3, f32[1,3072]{1,0:T(1,128)} %bitcast.18, f32[1,3072]{1,0:T(1,128)} %bitcast.19, bf16[3,384,512]{2,1,0:T(8,128)(2,1)} %qkv_ref.1, bf16[256,128]{1,0:T(8,128)(2,1)} %latents_ref.1, ...), custom_call_target="tpu_custom_call" | custom-call | tf_op jit(solution)/shard_map/prep/pallas_call | solution.py:396
  10.9 31.5 %all_to_all.10 = bf16[8,384,128]{2,1,0:T(8,128)(2,1)S(1)} all-to-all(bf16[8,384,128]{2,1,0:T(8,128)(2,1)} %prep.1), channel_id=1, replica_groups=mesh['wide'=8,'narrow'=4] {'wide'}, dimensions={0} | all-to-all | bytes 1572864 | tf_op jit(solution)/shard_map/all_to_all | solution.py:424
  42.5 0.1 reshape_squeeze.3
  42.6 1.3 collective-permute-start
  43.9 0.0 copy-start.4
  43.9 9.0 %collective-permute-done = bf16[1,1296,128]{2,1,0:T(8,128)(2,1)S(1)} collective-permute-done((bf16[1,1296,128]{2,1,0:T(8,128)(2,1)S(1)}, bf16[1,1296,128]{2,1,0:T(8,128)(2,1)S(1)}, u32[]{:S(2)}, u32[]{:S(2)}) %collective-permute-start) | collective-permute-done | bytes 331808 | tf_op jit(solution)/shard_map/ppermute | solution.py:346
  52.9 0.1 pad_maximum_fusion.1
  53.0 0.0 copy-start.5
  53.0 5.0 %collective-permute-start.1 = (bf16[2,1296,128]{2,1,0:T(8,128)(2,1)S(1)}, bf16[2,1296,128]{2,1,0:T(8,128)(2,1)}, u32[]{:S(2)}, u32[]{:S(2)}) collective-permute-start(bf16[2,1296,128]{2,1,0:T(8,128)(2,1)S(1)} %pad_maximum_fusion.1), channel_id=1, source_target_pairs={{0,1},{1,0},{2,3},{3,2},{4,5},{5,4},{6,7},{7,6},{8,9},{9,8},{10,11... | collective-permute-start | bytes 1990664 | tf_op jit(solution)/shard_map/ppermute | solution.py:346
  58.0 0.1 slice_reduce_fusion
  58.1 0.8 broadcast_in_dim.10
  58.9 7.1 %all-to-all-start.1 = ((bf16[8,192,128]{2,1,0:T(8,128)(2,1)}), bf16[8,192,128]{2,1,0:T(8,128)(2,1)S(1)}, u32[]{:S(2)}, u32[]{:S(2)}) async-start(bf16[8,192,128]{2,1,0:T(8,128)(2,1)} %broadcast_in_dim.10), calls=%async_computation.1 | async-start | bytes 786432 | tf_op jit(solution)/shard_map/all_to_all | solution.py:441
  66.0 0.0 copy-done.4
  66.0 3.5 %gram.1.gram_ref = bf16[3,128,128]{2,1,0:T(8,128)(2,1)} custom-call(bf16[128,3072]{1,0:T(8,128)(2,1)} %embed_ref.3), custom_call_target="tpu_custom_call" | custom-call | tf_op jit(solution)/shard_map/gram/pallas_call | solution.py:417
  69.5 0.1 reshape.31.starts_ref
  69.5 0.0 copy-done.5
  69.6 0.0 copy-start
  69.6 0.0 collective-permute-done.1
  69.6 1.3 pad_maximum_fusion.patches_ref
  70.9 9.4 %all-to-all-done.1 = bf16[8,192,128]{2,1,0:T(8,128)(2,1)S(1)} async-done(((bf16[8,192,128]{2,1,0:T(8,128)(2,1)}), bf16[8,192,128]{2,1,0:T(8,128)(2,1)S(1)}, u32[]{:S(2)}, u32[]{:S(2)}) %all-to-all-start.1) | async-done | bytes 393248 | tf_op jit(solution)/shard_map/all_to_all | solution.py:441
  80.3 0.0 copy-done
  80.3 0.0 copy-start.2
  80.3 10.5 %project.1 = (bf16[512,5120]{1,0:T(8,128)(2,1)S(1)}, bf16[5120,512]{1,0:T(8,128)(2,1)S(1)}, bf16[8,4,256,128]{3,2,1,0:T(8,128)(2,1)S(1)}) custom-call(s32[4]{0:T(128)S(1)} %broadcast_xor_fusion.order_ref, bf16[4,1296,128]{2,1,0:T(8,128)(2,1)S(1)} %pad_maximum_fusion.patches_ref, bf16[1536,128]{1,0:T(8,128)(2,1)S(1)} %bitcast.14, ...), custom_call_target="tpu_custom_call" | custom-call | flops 3355443200 | bytes 16777216 | tf_op jit(solution)/shard_map/project/pallas_call | solution.py:448
  90.8 0.0 copy-done.2
  90.8 17.8 %shard_map.110 = (bf16[128,512]{1,0:T(8,128)(2,1)S(1)}, bf16[128,512]{1,0:T(8,128)(2,1)S(1)}, bf16[128,512]{1,0:T(8,128)(2,1)S(1)}, bf16[128,512]{1,0:T(8,128)(2,1)S(1)}) custom-call(s32[4]{0:T(128)S(1)} %broadcast_xor_fusion.order_ref, s32[64]{0:T(128)S(1)} %reshape.31.starts_ref, s32[8]{0:T(128)S(1)} %copy-done.2, ...), custom_call_target="tpu_custom_call" | custom-call | flops 4294967296 | bytes 16777216 | tf_op jit(solution)/shard_map/pallas_call | solution.py:465
  108.6 0.0 copy-start.1
  108.6 0.5 collective-permute-start.5
  109.1 12.8 %shard_map.109 = (bf16[128,512]{1,0:T(8,128)(2,1)S(1)}, bf16[128,512]{1,0:T(8,128)(2,1)S(1)}, bf16[128,512]{1,0:T(8,128)(2,1)S(1)}, bf16[128,512]{1,0:T(8,128)(2,1)S(1)}) custom-call(s32[4]{0:T(128)S(1)} %broadcast_xor_fusion.order_ref, s32[64]{0:T(128)S(1)} %reshape.31.starts_ref, s32[8]{0:T(128)S(1)} %copy-done.2, ...), custom_call_target="tpu_custom_call" | custom-call | flops 4294967296 | bytes 16777216 | tf_op jit(solution)/shard_map/pallas_call | solution.py:465
  122.0 1.2 collective-permute-start.6
  123.1 0.6 collective-permute-start.7
  123.7 0.2 collective-permute-start.2
  123.9 1.1 collective-permute-start.3
  125.0 0.0 collective-permute-done.5.refs_5_
  125.0 0.8 collective-permute-start.4
  125.9 1.2 collective-permute-done.6.refs_6_
  127.0 3.6 %collective-permute-done.7.refs_7_ = bf16[128,512]{1,0:T(8,128)(2,1)S(1)} collective-permute-done((bf16[128,512]{1,0:T(8,128)(2,1)S(1)}, bf16[128,512]{1,0:T(8,128)(2,1)S(1)}, u32[]{:S(2)}, u32[]{:S(2)}) %collective-permute-start.7) | collective-permute-done | bytes 131104 | tf_op jit(solution)/shard_map/ppermute | solution.py:346
  130.6 0.0 copy-start.3
  130.6 0.0 collective-permute-done.2.refs_1_
  130.6 2.1 %collective-permute-done.3.refs_2_ = bf16[128,512]{1,0:T(8,128)(2,1)S(1)} collective-permute-done((bf16[128,512]{1,0:T(8,128)(2,1)S(1)}, bf16[128,512]{1,0:T(8,128)(2,1)S(1)}, u32[]{:S(2)}, u32[]{:S(2)}) %collective-permute-start.3) | collective-permute-done | bytes 131104 | tf_op jit(solution)/shard_map/ppermute | solution.py:346
  132.6 3.0 %collective-permute-done.4.refs_3_ = bf16[128,512]{1,0:T(8,128)(2,1)S(1)} collective-permute-done((bf16[128,512]{1,0:T(8,128)(2,1)S(1)}, bf16[128,512]{1,0:T(8,128)(2,1)S(1)}, u32[]{:S(2)}, u32[]{:S(2)}) %collective-permute-start.4) | collective-permute-done | bytes 131104 | tf_op jit(solution)/shard_map/ppermute | solution.py:346
  135.7 0.0 all-gather.2.cloned.1.call-done.refs_8_
  135.7 0.0 copy-done.3
  135.7 0.0 copy-done.1
  135.7 8.7 %output.1 = bf16[256,3072]{1,0:T(8,128)(2,1)} custom-call(s32[4]{0:T(128)S(1)} %broadcast_xor_fusion.order_ref, bf16[128,512]{1,0:T(8,128)(2,1)S(1)} %get-tuple-element.19.refs_0_, bf16[128,512]{1,0:T(8,128)(2,1)S(1)} %collective-permute-done.2.refs_1_, bf16[128,512]{1,0:T(8,128)(2,1)S(1)} %collective-permute-done.3.refs_2_, ...), custom_call_target="tpu_custom_call" | custom-call | tf_op jit(solution)/shard_map/output/pallas_call | solution.py:483
  (8 shorter events, 0.1 us)
Async XLA Ops:
  6.5 129.1 %all-gather.2.cloned.1.call-start = ((), (), s32[]{:S(2)}) async-start(), calls=%async_computation.2 | async-start | bytes 12976128 | tf_op jit(solution)/shard_map/all_gather | solution.py:377
  42.6 10.3 %collective-permute-start = (bf16[1,1296,128]{2,1,0:T(8,128)(2,1)S(1)}, bf16[1,1296,128]{2,1,0:T(8,128)(2,1)S(1)}, u32[]{:S(2)}, u32[]{:S(2)}) collective-permute-start(bf16[1,1296,128]{2,1,0:T(8,128)(2,1)S(1)} %maximum_bitcast_fusion), channel_id=1, source_target_pairs={{0,2},{1,3},{2,0},{3,1},{4,6},{5,7},{6,4},{7,5},{8,10},{9,11},{10,... | collective-permute-start | bytes 995336 | tf_op jit(solution)/shard_map/ppermute | solution.py:346
  43.9 22.1 %copy-start.4 = (s32[8,8]{1,0:T(8,128)S(1)}, s32[8,8]{1,0:T(8,128)}, u32[]{:S(2)}) copy-start(s32[8,8]{1,0:T(8,128)} %param.19) | copy-start | bytes 772
  53.0 16.6 %copy-start.5 = (s32[4]{0:T(128)S(1)}, s32[4]{0:T(128)}, u32[]{:S(2)}) copy-start(s32[4]{0:T(128)} %constant.26.clone) | copy-start | bytes 52
  53.0 16.6 %collective-permute-start.1 = (bf16[2,1296,128]{2,1,0:T(8,128)(2,1)S(1)}, bf16[2,1296,128]{2,1,0:T(8,128)(2,1)}, u32[]{:S(2)}, u32[]{:S(2)}) collective-permute-start(bf16[2,1296,128]{2,1,0:T(8,128)(2,1)S(1)} %pad_maximum_fusion.1), channel_id=1, source_target_pairs={{0,1},{1,0},{2,3},{3,2},{4,5},{5,4},{6,7},{7,6},{8,9},{9,8},{10,11... | collective-permute-start | bytes 1990664 | tf_op jit(solution)/shard_map/ppermute | solution.py:346
  58.9 21.4 %all-to-all-start.1 = ((bf16[8,192,128]{2,1,0:T(8,128)(2,1)}), bf16[8,192,128]{2,1,0:T(8,128)(2,1)S(1)}, u32[]{:S(2)}, u32[]{:S(2)}) async-start(bf16[8,192,128]{2,1,0:T(8,128)(2,1)} %broadcast_in_dim.10), calls=%async_computation.1 | async-start | bytes 786432 | tf_op jit(solution)/shard_map/all_to_all | solution.py:441
  69.6 10.7 %copy-start = (bf16[3,128,128]{2,1,0:T(8,128)(2,1)S(1)}, bf16[3,128,128]{2,1,0:T(8,128)(2,1)}, u32[]{:S(2)}) copy-start(bf16[3,128,128]{2,1,0:T(8,128)(2,1)} %gram.1.gram_ref) | copy-start | bytes 294916
  80.3 10.5 %copy-start.2 = (s32[8]{0:T(128)S(1)}, s32[8]{0:T(128)}, u32[]{:S(2)}) copy-start(s32[8]{0:T(128)} %counts_ref.3) | copy-start | bytes 100
  108.6 27.1 %copy-start.1 = (f32[3072]{0:T(1024)S(1)}, f32[3072]{0:T(1024)}, u32[]{:S(2)}) copy-start(f32[3072]{0:T(1024)} %param.18) | copy-start | bytes 36868
  108.6 16.4 %collective-permute-start.5 = (bf16[128,512]{1,0:T(8,128)(2,1)S(1)}, bf16[128,512]{1,0:T(8,128)(2,1)S(1)}, u32[]{:S(2)}, u32[]{:S(2)}) collective-permute-start(bf16[128,512]{1,0:T(8,128)(2,1)S(1)} %get-tuple-element.24), channel_id=1, source_target_pairs={{0,1},{1,0},{2,3},{3,2},{4,5},{5,4},{6,7},{7,6},{8,9},{9,8},{10,11... | collective-permute-start | bytes 393224 | tf_op jit(solution)/shard_map/ppermute | solution.py:346
  122.0 5.1 %collective-permute-start.6 = (bf16[128,512]{1,0:T(8,128)(2,1)S(1)}, bf16[128,512]{1,0:T(8,128)(2,1)S(1)}, u32[]{:S(2)}, u32[]{:S(2)}) collective-permute-start(bf16[128,512]{1,0:T(8,128)(2,1)S(1)} %get-tuple-element.25), channel_id=1, source_target_pairs={{0,2},{1,3},{2,0},{3,1},{4,6},{5,7},{6,4},{7,5},{8,10},{9,11},{10,... | collective-permute-start | bytes 393224 | tf_op jit(solution)/shard_map/ppermute | solution.py:346
  123.1 7.4 %collective-permute-start.7 = (bf16[128,512]{1,0:T(8,128)(2,1)S(1)}, bf16[128,512]{1,0:T(8,128)(2,1)S(1)}, u32[]{:S(2)}, u32[]{:S(2)}) collective-permute-start(bf16[128,512]{1,0:T(8,128)(2,1)S(1)} %get-tuple-element.26), channel_id=1, source_target_pairs={{0,3},{1,2},{2,1},{3,0},{4,7},{5,6},{6,5},{7,4},{8,11},{9,10},{10,... | collective-permute-start | bytes 393224 | tf_op jit(solution)/shard_map/ppermute | solution.py:346
  123.7 6.9 %collective-permute-start.2 = (bf16[128,512]{1,0:T(8,128)(2,1)S(1)}, bf16[128,512]{1,0:T(8,128)(2,1)S(1)}, u32[]{:S(2)}, u32[]{:S(2)}) collective-permute-start(bf16[128,512]{1,0:T(8,128)(2,1)S(1)} %get-tuple-element.20), channel_id=1, source_target_pairs={{0,1},{1,0},{2,3},{3,2},{4,5},{5,4},{6,7},{7,6},{8,9},{9,8},{10,11... | collective-permute-start | bytes 393224 | tf_op jit(solution)/shard_map/ppermute | solution.py:346
  123.9 8.8 %collective-permute-start.3 = (bf16[128,512]{1,0:T(8,128)(2,1)S(1)}, bf16[128,512]{1,0:T(8,128)(2,1)S(1)}, u32[]{:S(2)}, u32[]{:S(2)}) collective-permute-start(bf16[128,512]{1,0:T(8,128)(2,1)S(1)} %get-tuple-element.21), channel_id=1, source_target_pairs={{0,2},{1,3},{2,0},{3,1},{4,6},{5,7},{6,4},{7,5},{8,10},{9,11},{10,... | collective-permute-start | bytes 393224 | tf_op jit(solution)/shard_map/ppermute | solution.py:346
  125.0 10.7 %collective-permute-start.4 = (bf16[128,512]{1,0:T(8,128)(2,1)S(1)}, bf16[128,512]{1,0:T(8,128)(2,1)S(1)}, u32[]{:S(2)}, u32[]{:S(2)}) collective-permute-start(bf16[128,512]{1,0:T(8,128)(2,1)S(1)} %get-tuple-element.22), channel_id=1, source_target_pairs={{0,3},{1,2},{2,1},{3,0},{4,7},{5,6},{6,5},{7,4},{8,11},{9,10},{10,... | collective-permute-start | bytes 393224 | tf_op jit(solution)/shard_map/ppermute | solution.py:346
  130.6 5.1 %copy-start.3 = (bf16[128,512]{1,0:T(8,128)(2,1)}, bf16[128,512]{1,0:T(8,128)(2,1)S(1)}, u32[]{:S(2)}) copy-start(bf16[128,512]{1,0:T(8,128)(2,1)S(1)} %collective-permute-done.7.refs_7_) | copy-start | bytes 393220
Sparse Core Ops, SparseCore 0:
  10.2 112.2 all-gather.1

commit v4 on v3

--- a/solution.py
+++ b/solution.py
@@ -6,6 +6,7 @@
 from jax.experimental import pallas as pl
 from jax.experimental.pallas import tpu as pltpu
 from jax.sharding import PartitionSpec as P
+
 
 HEAD = 64
 NB = 8
@@ -17,6 +18,7 @@
 PROJECT_VMEM = 32 << 20
 ATTEND_VMEM = 32 << 20
 OUTPUT_VMEM = 53 << 20
+PARTIAL_VMEM = 24 << 20
 
 f32 = jnp.float32
 bf16 = jnp.bfloat16
@@ -244,36 +246,35 @@
 
 
 def attend_kernel(
-    parts, chunk, order_ref, starts_ref, counts_ref, keys_ref, values_ref, twin_ref, *rest
+    parts, entries, order_ref, starts_ref, counts_ref, keys_ref, values_ref, twin_ref, *rest
 ):
-    out_refs = rest[:-5]
-    total_ref, even_ref, odd_ref, block_ref, first_ref = rest[-5:]
-    receivers = len(out_refs)
+    out_refs = rest[:-6]
+    total_ref, even_ref, odd_ref, block_ref, query_ref, first_ref = rest[-6:]
     pairs = twin_ref.shape[1]
     left = lax.broadcasted_iota(jnp.int32, (QB, 128), 1) < HEAD
 
-    def listed(index, count):
+    steps = jnp.int32(0)
+    for index, (away, part) in enumerate(entries):
         total_ref[index] = jnp.zeros_like(total_ref[index])
-        block = index * parts + chunk
-
-        def note(slot, inner):
-            block_ref[count + slot] = index
-            first_ref[count + slot] = starts_ref[block * NB + slot]
-            return inner
-
-        lax.fori_loop(0, counts_ref[block], note, 0)
-        return count + counts_ref[block]
-
-    steps = lax.fori_loop(0, receivers, listed, 0)
+        block = (order_ref[0] ^ away) * parts + part
+
+        def note(slot, at, index=index, block=block):
+            block_ref[at] = index
+            query_ref[at] = block
+            first_ref[at] = starts_ref[block * NB + slot]
+            return at + 1
+
+        steps = lax.fori_loop(0, counts_ref[block], note, steps)
     for extra in range(2):
-        block_ref[steps + extra] = receivers
+        block_ref[steps + extra] = len(entries)
+        query_ref[steps + extra] = query_ref[0]
         first_ref[steps + extra] = first_ref[0]
 
     ones = jnp.ones((KB, 128), bf16)
 
     def weigh(step, weights_ref):
         start = pl.multiple_of(first_ref[step], KB)
-        query = jnp.minimum(block_ref[step], receivers - 1) * parts + chunk
+        query = query_ref[step]
         for pair in range(pairs):
             scores = jnp.dot(
                 twin_ref[query, pair],
@@ -303,23 +304,23 @@
 
     lax.fori_loop(0, (steps + 1) // 2, visit, 0)
 
-    for away in range(receivers):
-        block = order_ref[0] ^ away
+    for index in range(len(entries)):
         for pair in range(pairs):
-            both = total_ref[block, pair, :, 0:128] / total_ref[block, pair, :, 128:256]
-            out_refs[away][:, pair * 128 : (pair + 1) * 128] = jnp.where(
+            both = total_ref[index, pair, :, 0:128] / total_ref[index, pair, :, 128:256]
+            out_refs[index][:, pair * 128 : (pair + 1) * 128] = jnp.where(
                 left, both[0:QB], both[QB : 2 * QB]
             ).astype(bf16)
 
 
-def attend_scratch(receivers, heads_width):
+def attend_scratch(entries, heads_width):
     pairs = heads_width // 128
     return [
-        pltpu.VMEM((receivers + 1, pairs, 2 * QB, 256), f32),
+        pltpu.VMEM((entries + 1, pairs, 2 * QB, 256), f32),
         pltpu.VMEM((pairs, 2 * QB, KB), bf16),
         pltpu.VMEM((pairs, 2 * QB, KB), bf16),
-        pltpu.SMEM((receivers * NB + 2,), jnp.int32),
-        pltpu.SMEM((receivers * NB + 2,), jnp.int32),
+        pltpu.SMEM((entries * NB + 2,), jnp.int32),
+        pltpu.SMEM((entries * NB + 2,), jnp.int32),
+        pltpu.SMEM((entries * NB + 2,), jnp.int32),
     ]
 
 
@@ -341,6 +342,29 @@
         out_ref[:, columns] = (total * gate_ref[:, columns]).astype(bf16)
 
 
+def partial_kernel(kept, total, held_ref, *refs):
+    attended_refs = refs[:total]
+    weight_refs = refs[total:-2]
+    keep_ref, send_ref = refs[-2:]
+    rows = weight_refs[0].shape[0]
+    keep = kept * QB
+    for index, weight_ref in enumerate(weight_refs):
+
+        @pl.when(held_ref[index] >= 0)
+        def _():
+            attended = jnp.concatenate([ref[...] for ref in attended_refs], axis=0)
+            product = ntdot(attended, weight_ref[...])
+            columns = pl.ds(pl.multiple_of(held_ref[index] * rows, 128), rows)
+            keep_ref[:, columns] = product[0:keep]
+            send_ref[:, columns] = product[keep:].astype(bf16)
+
+
+def final_kernel(own_ref, first_ref, second_ref, third_ref, gate_ref, out_ref):
+    far = jnp.concatenate([second_ref[...], third_ref[...]], axis=0).astype(f32)
+    total = own_ref[...] + first_ref[...].astype(f32) + far
+    out_ref[...] = (total * gate_ref[...]).astype(bf16)
+
+
 def flip(block, axis, bit):
     devices = range(lax.axis_size(axis))
     return lax.ppermute(block, axis, [(i, i ^ bit) for i in devices])
@@ -348,6 +372,33 @@
 
 def cost(flops, moved):
     return pl.CostEstimate(flops=flops, bytes_accessed=moved, transcendentals=0)
+
+
+def gathered_rows(own):
+    count = lax.axis_size("wide")
+    index = lax.axis_index("wide")
+    length = count // 2
+    blocks, held = [own], [index]
+    blocks.append(lax.ppermute(own, "wide", [(i, i ^ 1) for i in range(count)]))
+    held.append(index ^ 1)
+    for sign in (1, -1):
+        current = own
+        for step in range(1, length):
+            move = 2 * sign
+            route = [
+                (i, i + move)
+                for i in range(count)
+                if 0 <= i + move < count and 0 <= i - move * (step - 1) < count
+            ]
+            current = lax.ppermute(current, "wide", route)
+            source = index - move * step
+            valid = (source >= 0) & (source < count)
+            blocks.append(current)
+            held.append(jnp.where(valid, source, -1))
+            swap = [(i, i ^ 1) for i in range(count) if 0 <= i - move * step < count]
+            blocks.append(lax.ppermute(current, "wide", swap))
+            held.append(jnp.where(valid, source ^ 1, -1))
+    return blocks, jnp.stack(held).astype(jnp.int32)
 
 
 def block(
@@ -374,7 +425,11 @@
     count = -(-SPAN * share // 16) * 16
     piece = 3 * heads_width // wide_count
 
-    out_all = lax.all_gather(out_weight, ("wide", "narrow"), axis=0, tiled=True)
+    chained = narrow_count == 4 and out_weight.shape[0] % 128 == 0 and row_total == 2 * QB
+    if chained:
+        blocks, held = gathered_rows(out_weight)
+    else:
+        out_all = lax.all_gather(out_weight, ("wide", "narrow"), axis=0, tiled=True)
 
     first = wide_index * depth
     extra = 16 + count + 16
@@ -393,13 +448,15 @@
     else:
         prep_shapes = (jax.ShapeDtypeStruct((wide_count, piece + extra, patch), bf16),)
     smem = pl.BlockSpec(memory_space=pltpu.SMEM)
-    prepared = pl.pallas_call(
+    prepare = pl.pallas_call(
         functools.partial(prep_kernel, wide_count, sliced),
         out_shape=prep_shapes,
         in_specs=[smem] + [whole_spec()] * 7,
         out_specs=tuple(whole_spec() for _ in prep_shapes),
+        cost_estimate=cost(1 << 28, 4 << 20),
         name="prep",
-    )(
+    )
+    prepared = prepare(
         first.astype(jnp.int32).reshape(1),
         embed_weight,
         own,
@@ -460,17 +517,55 @@
         name="project",
     )(order_ids, group, weight_all, bias, gram)
 
+    def attend(entries):
+        return pl.pallas_call(
+            functools.partial(attend_kernel, parts, entries),
+            out_shape=(jax.ShapeDtypeStruct((QB, heads_width), bf16),) * len(entries),
+            in_specs=[smem] * 3 + [whole_spec()] * 3,
+            out_specs=(whole_spec(),) * len(entries),
+            scratch_shapes=attend_scratch(len(entries), heads_width),
+            compiler_params=pltpu.CompilerParams(vmem_limit_bytes=ATTEND_VMEM),
+            cost_estimate=cost(4 * QB * len(entries) * NB * KB * heads_width, 16 << 20),
+        )(order_ids, starts, block_count, keys, values, twin)
+
+    if chained:
+        gate = mod_gate.reshape(1, width)
+
+        def multiply(attended, kept):
+            rows = len(attended) * QB
+            return pl.pallas_call(
+                functools.partial(partial_kernel, kept, len(attended)),
+                out_shape=(
+                    jax.ShapeDtypeStruct((kept * QB, width), f32),
+                    jax.ShapeDtypeStruct((rows - kept * QB, width), bf16),
+                ),
+                in_specs=[smem] + [whole_spec()] * (len(attended) + len(blocks)),
+                out_specs=(whole_spec(),) * 2,
+                compiler_params=pltpu.CompilerParams(vmem_limit_bytes=PARTIAL_VMEM),
+                cost_estimate=cost(2 * rows * heads_width * width, 8 << 20),
+            )(held, *attended, *blocks)
+
+        far = []
+        for part in range(parts):
+            attended = attend(((2, part), (3, part)))
+            keep, send = multiply(attended, 1)
+            other = flip(send, "narrow", 1)
+            joined = (keep + other.astype(f32)).astype(bf16)
+            far.append(flip(joined, "narrow", 2))
+        attended = attend(((0, 0), (0, 1), (1, 0), (1, 1)))
+        own, send = multiply(attended, 2)
+        other = flip(send, "narrow", 1)
+        return pl.pallas_call(
+            final_kernel,
+            out_shape=jax.ShapeDtypeStruct((row_total, width), bf16),
+            in_specs=[whole_spec()] * 5,
+            out_specs=whole_spec(),
+            name="final",
+        )(own, other, *far, gate)
+
     pieces = []
     for chunk in range(parts):
-        mine = pl.pallas_call(
-            functools.partial(attend_kernel, parts, chunk),
-            out_shape=(jax.ShapeDtypeStruct((QB, heads_width), bf16),) * narrow_count,
-            in_specs=[smem] * 3 + [whole_spec()] * 3,
-            out_specs=(whole_spec(),) * narrow_count,
-            scratch_shapes=attend_scratch(narrow_count, heads_width),
-            compiler_params=pltpu.CompilerParams(vmem_limit_bytes=ATTEND_VMEM),
-            cost_estimate=cost(4 * tile_size // parts * NB * KB * heads_width, 16 << 20),
-        )(order_ids, starts, block_count, keys, values, twin)
+        mine = attend(tuple((away, chunk) for away in range(narrow_count)))
         pieces.append(mine[0])
         for away in range(1, narrow_count):
             pieces.append(flip(mine[away], "narrow", away))

time: 152 us -> 177 us (1.16)
  the two profiles are of different devices: /device:TPU:25 before, /device:TPU:16 now
where the time goes in v4:
time: 177 us; the launch traced here: 175 us
  Pallas kernels  65.4 us (37%)
  waiting for transfers between devices  51.9 us (29%)
  starting transfers between devices  44.8 us (25%)
  local copies, waits for them, and re-layouts  6.72 us (4%)
  other arithmetic  6.05 us (3%)
    ppermute x7, waiting for transfers between devices, flip(): return lax.ppermute(block, axis, [(i, i ^ bit) for i in devices])  34.1 us
    pallas_call x3, Pallas kernels, attend(): pl.pallas_call(functools.partial(attend_kernel, parts, entries), out_shap...  29.3 us
    ppermute x6, starting transfers between devices, gathered_rows(): current = lax.ppermute(current, 'wide', route)  14.2 us
    pallas_call x3, Pallas kernels, multiply(): pl.pallas_call(functools.partial(partial_kernel, kept, len(attended)), ou...  13.4 us
    ppermute x6, starting transfers between devices, gathered_rows(): blocks.append(lax.ppermute(current, 'wide', swap))  13.3 us
    all_to_all x1, waiting for transfers between devices, block(): lax.all_to_all(payload, 'wide', split_axis=0, concat_axis=0, tiled=True)  12.4 us
    pallas_call x1, Pallas kernels, block(): pl.pallas_call(functools.partial(project_kernel, row_total, tile_size), o...  11.1 us
    all_to_all x1, starting transfers between devices, block(): lax.all_to_all(payload, 'wide', split_axis=0, concat_axis=0, tiled=True)  6.3 us
  transfers between devices with their start and end apart: 22, of which 5 were waited for; matrix products, arithmetic and copies ran while one was open for 4% of the time, Pallas kernels for 30%

profile of v4, /device:TPU:16, one launch (start us, length us, event | category | flops | bytes accessed | tf_op | source)
XLA Modules:
  0.0 175.2 jit_solution(2969083158023639277)
XLA Ops:
  0.0 3.6 %prep.1 = bf16[8,384,128]{2,1,0:T(8,128)(2,1)} custom-call(s32[1]{0:T(128)} %bitcast.14.at_ref, bf16[128,3072]{1,0:T(8,128)(2,1)} %embed_ref.3, bf16[128,3072]{1,0:T(8,128)(2,1)} %embed_ref.3, f32[1,3072]{1,0:T(1,128)} %bitcast.31, f32[1,3072]{1,0:T(1,128)} %bitcast.32, bf16[3,384,512]{2,1,0:T(8,128)(2,1)} %qkv_ref.1, bf16[256,128]{1,0:T(8,128)(2,1)} %latents_ref.1, ...), custom_call_target="tpu_custom_call" | custom-call | flops 268435456 | bytes 4194304 | tf_op jit(solution)/shard_map/prep/pallas_call | solution.py:459
  3.7 6.3 %all-to-all-start = ((bf16[8,384,128]{2,1,0:T(8,128)(2,1)}), bf16[8,384,128]{2,1,0:T(8,128)(2,1)S(1)}, u32[]{:S(2)}, u32[]{:S(2)}) async-start(bf16[8,384,128]{2,1,0:T(8,128)(2,1)} %prep.1), calls=%async_computation | async-start | bytes 1572864 | tf_op jit(solution)/shard_map/all_to_all | solution.py:481
  10.0 2.5 %collective-permute-start.9 = (bf16[384,512]{1,0:T(8,128)(2,1)S(1)}, bf16[384,512]{1,0:T(8,128)(2,1)S(1)}, u32[]{:S(2)}, u32[]{:S(2)}) collective-permute-start(bf16[384,512]{1,0:T(8,128)(2,1)S(1)} %copy-done), channel_id=1, source_target_pairs={{8,0},{12,4},{16,8},{20,12},{24,16},{28,20},{9,1},{13,5},{17,9},{2... | collective-permute-start | bytes 1179656 | tf_op jit(solution)/shard_map/ppermute | solution.py:393
  12.4 3.4 %collective-permute-start.3 = (bf16[384,512]{1,0:T(8,128)(2,1)S(1)}, bf16[384,512]{1,0:T(8,128)(2,1)S(1)}, u32[]{:S(2)}, u32[]{:S(2)}) collective-permute-start(bf16[384,512]{1,0:T(8,128)(2,1)S(1)} %copy-done), channel_id=1, source_target_pairs={{0,8},{4,12},{8,16},{12,20},{16,24},{20,28},{1,9},{5,13},{9,17},{1... | collective-permute-start | bytes 1179656 | tf_op jit(solution)/shard_map/ppermute | solution.py:393
  15.8 12.4 %all-to-all-done = bf16[8,384,128]{2,1,0:T(8,128)(2,1)S(1)} async-done(((bf16[8,384,128]{2,1,0:T(8,128)(2,1)}), bf16[8,384,128]{2,1,0:T(8,128)(2,1)S(1)}, u32[]{:S(2)}, u32[]{:S(2)}) %all-to-all-start) | async-done | bytes 786464 | tf_op jit(solution)/shard_map/all_to_all | solution.py:481
  28.2 0.1 reshape_squeeze.3
  28.4 0.0 copy-start.12
  28.4 1.6 collective-permute-start
  30.0 1.0 collective-permute-start.2
  31.0 4.1 %collective-permute-done.9.refs_12_.refs_10_ = bf16[384,512]{1,0:T(8,128)(2,1)S(1)} collective-permute-done((bf16[384,512]{1,0:T(8,128)(2,1)S(1)}, bf16[384,512]{1,0:T(8,128)(2,1)S(1)}, u32[]{:S(2)}, u32[]{:S(2)}) %collective-permute-start.9) | collective-permute-done | bytes 393248 | tf_op jit(solution)/shard_map/ppermute | solution.py:393
  35.2 4.4 %collective-permute-start.11 = (bf16[384,512]{1,0:T(8,128)(2,1)S(1)}, bf16[384,512]{1,0:T(8,128)(2,1)S(1)}, u32[]{:S(2)}, u32[]{:S(2)}) collective-permute-start(bf16[384,512]{1,0:T(8,128)(2,1)S(1)} %collective-permute-done.9.refs_12_.refs_10_), channel_id=1, source_target_pairs={{8,0},{12,4},{16,8},{20,12},{9,1},{13,5},{17,9},{21,13},{10,2},{14... | collective-permute-start | bytes 1179656 | tf_op jit(solution)/shard_map/ppermute | solution.py:393
  39.6 1.9 %collective-permute-start.5 = (bf16[384,512]{1,0:T(8,128)(2,1)S(1)}, bf16[384,512]{1,0:T(8,128)(2,1)S(1)}, u32[]{:S(2)}, u32[]{:S(2)}) collective-permute-start(bf16[384,512]{1,0:T(8,128)(2,1)S(1)} %collective-permute-done.3.refs_6_.refs_4_), channel_id=1, source_target_pairs={{8,16},{12,20},{16,24},{20,28},{9,17},{13,21},{17,25},{21,29},{10,... | collective-permute-start | bytes 1179656 | tf_op jit(solution)/shard_map/ppermute | solution.py:393
  41.5 0.0 collective-permute-done
  41.5 1.9 %pad_maximum_fusion.1 = bf16[2,1296,128]{2,1,0:T(8,128)(2,1)} fusion(bf16[1,1296,128]{2,1,0:T(8,128)(2,1)} %collective-permute-done, bf16[1,1296,128]{2,1,0:T(8,128)(2,1)S(1)} %maximum_bitcast_fusion), kind=kLoop, calls=%fused_computation.3 | loop fusion | flops 331776 | bytes 1327104 | tf_op jit(solution)/shard_map/concatenate | solution.py:496
  43.5 0.1 slice_reduce_fusion
  43.5 0.8 broadcast_in_dim.10
  44.3 5.6 %all-to-all-start.1 = ((bf16[8,192,128]{2,1,0:T(8,128)(2,1)}), bf16[8,192,128]{2,1,0:T(8,128)(2,1)}, u32[]{:S(2)}, u32[]{:S(2)}) async-start(bf16[8,192,128]{2,1,0:T(8,128)(2,1)} %broadcast_in_dim.10), calls=%async_computation.1 | async-start | bytes 786432 | tf_op jit(solution)/shard_map/all_to_all | solution.py:498
  49.9 0.5 broadcast_xor_fusion.order_ref
  50.4 3.5 %gram.1.gram_ref = bf16[3,128,128]{2,1,0:T(8,128)(2,1)} custom-call(bf16[128,3072]{1,0:T(8,128)(2,1)} %embed_ref.3), custom_call_target="tpu_custom_call" | custom-call | tf_op jit(solution)/shard_map/gram/pallas_call | solution.py:474
  53.9 3.4 %collective-permute-start.10 = (bf16[384,512]{1,0:T(8,128)(2,1)S(1)}, bf16[384,512]{1,0:T(8,128)(2,1)S(1)}, u32[]{:S(2)}, u32[]{:S(2)}) collective-permute-start(bf16[384,512]{1,0:T(8,128)(2,1)S(1)} %collective-permute-done.9.refs_12_.refs_10_), channel_id=1, source_target_pairs={{0,4},{4,0},{8,12},{12,8},{16,20},{20,16},{1,5},{5,1},{9,13},{13,9... | collective-permute-start | bytes 1179656 | tf_op jit(solution)/shard_map/ppermute | solution.py:399
  57.3 0.0 collective-permute-done.11.refs_14_.refs_12_
  57.3 0.7 collective-permute-start.13
  58.0 1.3 collective-permute-start.7
  59.4 0.1 reshape.31.starts_ref
  59.4 0.1 stack.59.held_ref
  59.5 0.8 convert_reduce_fusion.bias_ref
  60.3 0.0 collective-permute-done.1
  60.3 2.8 %collective-permute-start.4 = (bf16[384,512]{1,0:T(8,128)(2,1)S(1)}, bf16[384,512]{1,0:T(8,128)(2,1)}, u32[]{:S(2)}, u32[]{:S(2)}) collective-permute-start(bf16[384,512]{1,0:T(8,128)(2,1)S(1)} %collective-permute-done.3.refs_6_.refs_4_), channel_id=1, source_target_pairs={{8,12},{12,8},{16,20},{20,16},{24,28},{28,24},{9,13},{13,9},{17,21... | collective-permute-start | bytes 1179656 | tf_op jit(solution)/shard_map/ppermute | solution.py:399
  63.1 2.5 %pad_maximum_fusion.patches_ref = bf16[4,1296,128]{2,1,0:T(8,128)(2,1)} fusion(bf16[2,1296,128]{2,1,0:T(8,128)(2,1)} %collective-permute-done.1, bf16[1,1296,128]{2,1,0:T(8,128)(2,1)} %collective-permute-done, bf16[1,1296,128]{2,1,0:T(8,128)(2,1)} %copy-done.7), kind=kLoop, calls=%fused_computation.2 | loop fusion | flops 1327104 | bytes 2654208 | tf_op jit(solution)/shard_map/concatenate | solution.py:496
  65.6 0.0 collective-permute-done.2.refs_5_.refs_3_
  65.6 1.4 collective-permute-start.12
  67.0 1.3 collective-permute-done.10.refs_13_.refs_11_
  68.3 2.9 %collective-permute-start.6 = (bf16[384,512]{1,0:T(8,128)(2,1)S(1)}, bf16[384,512]{1,0:T(8,128)(2,1)}, u32[]{:S(2)}, u32[]{:S(2)}) collective-permute-start(bf16[384,512]{1,0:T(8,128)(2,1)S(1)} %collective-permute-done.5.refs_8_.refs_6_), channel_id=1, source_target_pairs={{16,20},{20,16},{24,28},{28,24},{17,21},{21,17},{25,29},{29,25},{1... | collective-permute-start | bytes 1179656 | tf_op jit(solution)/shard_map/ppermute | solution.py:399
  71.1 0.0 collective-permute-done.13.refs_16_.refs_14_
  71.2 1.4 collective-permute-start.14
  72.6 0.0 collective-permute-done.7.refs_10_.refs_8_
  72.6 1.4 collective-permute-start.8
  74.0 1.3 copy-done.2
  75.3 0.9 copy-done.3
  76.2 0.6 copy-done.5
  76.8 11.1 %project.1 = (bf16[512,5120]{1,0:T(8,128)(2,1)S(1)}, bf16[5120,512]{1,0:T(8,128)(2,1)S(1)}, bf16[8,4,256,128]{3,2,1,0:T(8,128)(2,1)S(1)}) custom-call(s32[4]{0:T(128)S(1)} %copy-done.5, bf16[4,1296,128]{2,1,0:T(8,128)(2,1)S(1)} %copy-done.2, bf16[1536,128]{1,0:T(8,128)(2,1)} %bitcast.23.weight_ref, f32[16,128]{1,0:T(8,128)S(1)} %convert_reduce_fusion.bias_ref, ...), custom_call_target="tpu_custom_call" | custom-call | flops 3355443200 | bytes 16777216 | tf_op jit(solution)/shard_map/project/pallas_call | solution.py:505
  87.9 8.8 %shard_map.111 = (bf16[128,512]{1,0:T(8,128)(2,1)S(1)}, bf16[128,512]{1,0:T(8,128)(2,1)S(1)}) custom-call(s32[4]{0:T(128)S(1)} %copy-done.5, s32[64]{0:T(128)S(1)} %reshape.31.starts_ref, s32[8]{0:T(128)S(1)} %copy-done.4, bf16[512,5120]{1,0:T(8,128)(2,1)S(1)} %get-tuple-element.22.keys_ref, bf16[5120,512]{1,0:T(8,128)(2,1)S(1)} %get-tuple-element.23.values_ref, ...), custom_call_target="tpu_custom_call" | custom-call | flops 2147483648 | bytes 16777216 | tf_op jit(solution)/shard_map/pallas_call | solution.py:521
  96.7 0.0 collective-permute-done.12.refs_15_.refs_13_
  96.7 0.0 collective-permute-done.6.refs_9_.refs_7_
  96.7 4.1 %shard_map.112 = (f32[128,3072]{1,0:T(8,128)S(1)}, bf16[128,3072]{1,0:T(8,128)(2,1)S(1)}) custom-call(s32[14]{0:T(128)S(1)} %stack.59.held_ref, bf16[128,512]{1,0:T(8,128)(2,1)S(1)} %get-tuple-element.31.refs_0_, bf16[128,512]{1,0:T(8,128)(2,1)S(1)} %get-tuple-element.32.refs_1_, bf16[384,512]{1,0:T(8,128)(2,1)S(1)} %copy-done, ...), custom_call_target="tpu_custom_call" | custom-call | flops 805306368 | bytes 8388608 | tf_op jit(solution)/shard_map/pallas_call | solution.py:536
  100.8 0.1 collective-permute-start.16
  100.9 6.5 %shard_map.113 = (bf16[128,512]{1,0:T(8,128)(2,1)S(1)}, bf16[128,512]{1,0:T(8,128)(2,1)S(1)}) custom-call(s32[4]{0:T(128)S(1)} %copy-done.5, s32[64]{0:T(128)S(1)} %reshape.31.starts_ref, s32[8]{0:T(128)S(1)} %copy-done.4, bf16[512,5120]{1,0:T(8,128)(2,1)S(1)} %get-tuple-element.22.keys_ref, bf16[5120,512]{1,0:T(8,128)(2,1)S(1)} %get-tuple-element.23.values_ref, ...), custom_call_target="tpu_custom_call" | custom-call | flops 2147483648 | bytes 16777216 | tf_op jit(solution)/shard_map/pallas_call | solution.py:521
  107.4 4.1 %shard_map.114 = (f32[128,3072]{1,0:T(8,128)S(1)}, bf16[128,3072]{1,0:T(8,128)(2,1)S(1)}) custom-call(s32[14]{0:T(128)S(1)} %stack.59.held_ref, bf16[128,512]{1,0:T(8,128)(2,1)S(1)} %get-tuple-element.35.refs_0_, bf16[128,512]{1,0:T(8,128)(2,1)S(1)} %get-tuple-element.36.refs_1_, bf16[384,512]{1,0:T(8,128)(2,1)S(1)} %copy-done, ...), custom_call_target="tpu_custom_call" | custom-call | flops 805306368 | bytes 8388608 | tf_op jit(solution)/shard_map/pallas_call | solution.py:536
  111.5 0.6 collective-permute-start.18
  112.0 14.1 %shard_map.109 = (bf16[128,512]{1,0:T(8,128)(2,1)S(1)}, bf16[128,512]{1,0:T(8,128)(2,1)S(1)}, bf16[128,512]{1,0:T(8,128)(2,1)S(1)}, bf16[128,512]{1,0:T(8,128)(2,1)S(1)}) custom-call(s32[4]{0:T(128)S(1)} %copy-done.5, s32[64]{0:T(128)S(1)} %reshape.31.starts_ref, s32[8]{0:T(128)S(1)} %copy-done.4, bf16[512,5120]{1,0:T(8,128)(2,1)S(1)} %get-tuple-element.22.keys_ref, ...), custom_call_target="tpu_custom_call" | custom-call | flops 4294967296 | bytes 16777216 | tf_op jit(solution)/shard_map/pallas_call | solution.py:521
  126.1 5.2 %shard_map.110 = (f32[256,3072]{1,0:T(8,128)S(1)}, bf16[256,3072]{1,0:T(8,128)(2,1)S(1)}) custom-call(s32[14]{0:T(128)S(1)} %stack.59.held_ref, bf16[128,512]{1,0:T(8,128)(2,1)S(1)} %get-tuple-element.25.refs_0_, bf16[128,512]{1,0:T(8,128)(2,1)S(1)} %get-tuple-element.26.refs_1_, bf16[128,512]{1,0:T(8,128)(2,1)S(1)} %get-tuple-element.27.refs_2_, ...), custom_call_target="tpu_custom_call" | custom-call | flops 1610612736 | bytes 8388608 | tf_op jit(solution)/shard_map/pallas_call | solution.py:536
  131.3 0.1 collective-permute-start.15
  131.4 0.2 add_convert_fusion.1
  131.6 1.4 copy-done.1
  133.0 1.5 collective-permute-start.17
  134.4 0.0 collective-permute-done.18
  134.4 0.2 add_convert_fusion
  134.6 0.6 collective-permute-start.19
  135.2 18.2 %collective-permute-done.17.second_ref = bf16[128,3072]{1,0:T(8,128)(2,1)S(1)} collective-permute-done((bf16[128,3072]{1,0:T(8,128)(2,1)S(1)}, bf16[128,3072]{1,0:T(8,128)(2,1)S(1)}, u32[]{:S(2)}, u32[]{:S(2)}) %collective-permute-start.17) | collective-permute-done | bytes 786464 | tf_op jit(solution)/shard_map/ppermute | solution.py:370
  153.4 15.9 %collective-permute-done.19.third_ref = bf16[128,3072]{1,0:T(8,128)(2,1)S(1)} collective-permute-done((bf16[128,3072]{1,0:T(8,128)(2,1)S(1)}, bf16[128,3072]{1,0:T(8,128)(2,1)S(1)}, u32[]{:S(2)}, u32[]{:S(2)}) %collective-permute-start.19) | collective-permute-done | bytes 786464 | tf_op jit(solution)/shard_map/ppermute | solution.py:370
  169.3 0.0 collective-permute-done.15.first_ref
  169.3 0.9 copy-done.10
  170.2 0.5 copy-done.8
  170.7 4.5 %final.1 = bf16[256,3072]{1,0:T(8,128)(2,1)} custom-call(f32[256,3072]{1,0:T(8,128)} %copy-done.1, bf16[256,3072]{1,0:T(8,128)(2,1)} %copy-done.8, bf16[128,3072]{1,0:T(8,128)(2,1)} %copy-done.9, bf16[128,3072]{1,0:T(8,128)(2,1)} %copy-done.10, f32[1,3072]{1,0:T(1,128)} %bitcast.30), custom_call_target="tpu_custom_call" | custom-call | tf_op jit(solution)/shard_map/final/pallas_call | solution.py:558
  (33 shorter events, 0.2 us)
Async XLA Ops:
  3.6 6.3 %copy-start = (bf16[384,512]{1,0:T(8,128)(2,1)S(1)}, bf16[384,512]{1,0:T(8,128)(2,1)}, u32[]{:S(2)}) copy-start(bf16[384,512]{1,0:T(8,128)(2,1)} %refs_2_.3) | copy-start | bytes 1179652
  3.7 24.5 %all-to-all-start = ((bf16[8,384,128]{2,1,0:T(8,128)(2,1)}), bf16[8,384,128]{2,1,0:T(8,128)(2,1)S(1)}, u32[]{:S(2)}, u32[]{:S(2)}) async-start(bf16[8,384,128]{2,1,0:T(8,128)(2,1)} %prep.1), calls=%async_computation | async-start | bytes 1572864 | tf_op jit(solution)/shard_map/all_to_all | solution.py:481
  10.0 25.2 %collective-permute-start.9 = (bf16[384,512]{1,0:T(8,128)(2,1)S(1)}, bf16[384,512]{1,0:T(8,128)(2,1)S(1)}, u32[]{:S(2)}, u32[]{:S(2)}) collective-permute-start(bf16[384,512]{1,0:T(8,128)(2,1)S(1)} %copy-done), channel_id=1, source_target_pairs={{8,0},{12,4},{16,8},{20,12},{24,16},{28,20},{9,1},{13,5},{17,9},{2... | collective-permute-start | bytes 1179656 | tf_op jit(solution)/shard_map/ppermute | solution.py:393
  12.4 27.2 %collective-permute-start.3 = (bf16[384,512]{1,0:T(8,128)(2,1)S(1)}, bf16[384,512]{1,0:T(8,128)(2,1)S(1)}, u32[]{:S(2)}, u32[]{:S(2)}) collective-permute-start(bf16[384,512]{1,0:T(8,128)(2,1)S(1)} %copy-done), channel_id=1, source_target_pairs={{0,8},{4,12},{8,16},{12,20},{16,24},{20,28},{1,9},{5,13},{9,17},{1... | collective-permute-start | bytes 1179656 | tf_op jit(solution)/shard_map/ppermute | solution.py:393
  28.2 15.3 %copy-start.6 = (bf16[8,384,128]{2,1,0:T(8,128)(2,1)}, bf16[8,384,128]{2,1,0:T(8,128)(2,1)S(1)}, u32[]{:S(2)}) copy-start(bf16[8,384,128]{2,1,0:T(8,128)(2,1)S(1)} %all-to-all-done) | copy-start | bytes 2359300
  28.4 25.5 %copy-start.7 = (bf16[1,1296,128]{2,1,0:T(8,128)(2,1)}, bf16[1,1296,128]{2,1,0:T(8,128)(2,1)S(1)}, u32[]{:S(2)}) copy-start(bf16[1,1296,128]{2,1,0:T(8,128)(2,1)S(1)} %maximum_bitcast_fusion) | copy-start | bytes 995332
  28.4 21.5 %copy-start.12 = (s32[4]{0:T(128)S(1)}, s32[4]{0:T(128)}, u32[]{:S(2)}) copy-start(s32[4]{0:T(128)} %constant.48.clone) | copy-start | bytes 52
  28.4 13.1 %collective-permute-start = (bf16[1,1296,128]{2,1,0:T(8,128)(2,1)S(1)}, bf16[1,1296,128]{2,1,0:T(8,128)(2,1)}, u32[]{:S(2)}, u32[]{:S(2)}) collective-permute-start(bf16[1,1296,128]{2,1,0:T(8,128)(2,1)S(1)} %maximum_bitcast_fusion), channel_id=1, source_target_pairs={{0,2},{1,3},{2,0},{3,1},{4,6},{5,7},{6,4},{7,5},{8,10},{9,11},{10,... | collective-permute-start | bytes 995336 | tf_op jit(solution)/shard_map/ppermute | solution.py:370
  30.0 35.6 %collective-permute-start.2 = (bf16[384,512]{1,0:T(8,128)(2,1)S(1)}, bf16[384,512]{1,0:T(8,128)(2,1)S(1)}, u32[]{:S(2)}, u32[]{:S(2)}) collective-permute-start(bf16[384,512]{1,0:T(8,128)(2,1)S(1)} %copy-done), channel_id=1, source_target_pairs={{0,4},{4,0},{8,12},{12,8},{16,20},{20,16},{24,28},{28,24},{1,5},{5... | collective-permute-start | bytes 1179656 | tf_op jit(solution)/shard_map/ppermute | solution.py:382
  35.2 22.1 %collective-permute-start.11 = (bf16[384,512]{1,0:T(8,128)(2,1)S(1)}, bf16[384,512]{1,0:T(8,128)(2,1)S(1)}, u32[]{:S(2)}, u32[]{:S(2)}) collective-permute-start(bf16[384,512]{1,0:T(8,128)(2,1)S(1)} %collective-permute-done.9.refs_12_.refs_10_), channel_id=1, source_target_pairs={{8,0},{12,4},{16,8},{20,12},{9,1},{13,5},{17,9},{21,13},{10,2},{14... | collective-permute-start | bytes 1179656 | tf_op jit(solution)/shard_map/ppermute | solution.py:393
  39.6 18.4 %collective-permute-start.5 = (bf16[384,512]{1,0:T(8,128)(2,1)S(1)}, bf16[384,512]{1,0:T(8,128)(2,1)S(1)}, u32[]{:S(2)}, u32[]{:S(2)}) collective-permute-start(bf16[384,512]{1,0:T(8,128)(2,1)S(1)} %collective-permute-done.3.refs_6_.refs_4_), channel_id=1, source_target_pairs={{8,16},{12,20},{16,24},{20,28},{9,17},{13,21},{17,25},{21,29},{10,... | collective-permute-start | bytes 1179656 | tf_op jit(solution)/shard_map/ppermute | solution.py:393
  43.4 10.4 %copy-start.11 = (s32[8,8]{1,0:T(8,128)S(1)}, s32[8,8]{1,0:T(8,128)}, u32[]{:S(2)}) copy-start(s32[8,8]{1,0:T(8,128)} %param.19) | copy-start | bytes 772
  43.4 16.9 %collective-permute-start.1 = (bf16[2,1296,128]{2,1,0:T(8,128)(2,1)}, bf16[2,1296,128]{2,1,0:T(8,128)(2,1)}, u32[]{:S(2)}, u32[]{:S(2)}) collective-permute-start(bf16[2,1296,128]{2,1,0:T(8,128)(2,1)} %pad_maximum_fusion.1), channel_id=1, source_target_pairs={{0,1},{1,0},{2,3},{3,2},{4,5},{5,4},{6,7},{7,6},{8,9},{9,8},{10,11... | collective-permute-start | bytes 1990664 | tf_op jit(solution)/shard_map/ppermute | solution.py:370
  44.3 29.7 %all-to-all-start.1 = ((bf16[8,192,128]{2,1,0:T(8,128)(2,1)}), bf16[8,192,128]{2,1,0:T(8,128)(2,1)}, u32[]{:S(2)}, u32[]{:S(2)}) async-start(bf16[8,192,128]{2,1,0:T(8,128)(2,1)} %broadcast_in_dim.10), calls=%async_computation.1 | async-start | bytes 786432 | tf_op jit(solution)/shard_map/all_to_all | solution.py:498
  53.9 14.4 %collective-permute-start.10 = (bf16[384,512]{1,0:T(8,128)(2,1)S(1)}, bf16[384,512]{1,0:T(8,128)(2,1)S(1)}, u32[]{:S(2)}, u32[]{:S(2)}) collective-permute-start(bf16[384,512]{1,0:T(8,128)(2,1)S(1)} %collective-permute-done.9.refs_12_.refs_10_), channel_id=1, source_target_pairs={{0,4},{4,0},{8,12},{12,8},{16,20},{20,16},{1,5},{5,1},{9,13},{13,9... | collective-permute-start | bytes 1179656 | tf_op jit(solution)/shard_map/ppermute | solution.py:399
  57.3 13.9 %collective-permute-start.13 = (bf16[384,512]{1,0:T(8,128)(2,1)S(1)}, bf16[384,512]{1,0:T(8,128)(2,1)S(1)}, u32[]{:S(2)}, u32[]{:S(2)}) collective-permute-start(bf16[384,512]{1,0:T(8,128)(2,1)S(1)} %collective-permute-done.11.refs_14_.refs_12_), channel_id=1, source_target_pairs={{8,0},{12,4},{9,1},{13,5},{10,2},{14,6},{11,3},{15,7}} | collective-permute-start | bytes 1179656 | tf_op jit(solution)/shard_map/ppermute | solution.py:393
  58.0 14.6 %collective-permute-start.7 = (bf16[384,512]{1,0:T(8,128)(2,1)S(1)}, bf16[384,512]{1,0:T(8,128)(2,1)S(1)}, u32[]{:S(2)}, u32[]{:S(2)}) collective-permute-start(bf16[384,512]{1,0:T(8,128)(2,1)S(1)} %collective-permute-done.5.refs_8_.refs_6_), channel_id=1, source_target_pairs={{16,24},{20,28},{17,25},{21,29},{18,26},{22,30},{19,27},{23,31}} | collective-permute-start | bytes 1179656 | tf_op jit(solution)/shard_map/ppermute | solution.py:393
  60.3 36.4 %collective-permute-start.4 = (bf16[384,512]{1,0:T(8,128)(2,1)S(1)}, bf16[384,512]{1,0:T(8,128)(2,1)}, u32[]{:S(2)}, u32[]{:S(2)}) collective-permute-start(bf16[384,512]{1,0:T(8,128)(2,1)S(1)} %collective-permute-done.3.refs_6_.refs_4_), channel_id=1, source_target_pairs={{8,12},{12,8},{16,20},{20,16},{24,28},{28,24},{9,13},{13,9},{17,21... | collective-permute-start | bytes 1179656 | tf_op jit(solution)/shard_map/ppermute | solution.py:399
  65.6 31.1 %collective-permute-start.12 = (bf16[384,512]{1,0:T(8,128)(2,1)S(1)}, bf16[384,512]{1,0:T(8,128)(2,1)}, u32[]{:S(2)}, u32[]{:S(2)}) collective-permute-start(bf16[384,512]{1,0:T(8,128)(2,1)S(1)} %collective-permute-done.11.refs_14_.refs_12_), channel_id=1, source_target_pairs={{0,4},{4,0},{8,12},{12,8},{1,5},{5,1},{9,13},{13,9},{2,6},{6,2},{1... | collective-permute-start | bytes 1179656 | tf_op jit(solution)/shard_map/ppermute | solution.py:399
  68.3 28.5 %collective-permute-start.6 = (bf16[384,512]{1,0:T(8,128)(2,1)S(1)}, bf16[384,512]{1,0:T(8,128)(2,1)}, u32[]{:S(2)}, u32[]{:S(2)}) collective-permute-start(bf16[384,512]{1,0:T(8,128)(2,1)S(1)} %collective-permute-done.5.refs_8_.refs_6_), channel_id=1, source_target_pairs={{16,20},{20,16},{24,28},{28,24},{17,21},{21,17},{25,29},{29,25},{1... | collective-permute-start | bytes 1179656 | tf_op jit(solution)/shard_map/ppermute | solution.py:399
  71.2 25.6 %collective-permute-start.14 = (bf16[384,512]{1,0:T(8,128)(2,1)S(1)}, bf16[384,512]{1,0:T(8,128)(2,1)}, u32[]{:S(2)}, u32[]{:S(2)}) collective-permute-start(bf16[384,512]{1,0:T(8,128)(2,1)S(1)} %collective-permute-done.13.refs_16_.refs_14_), channel_id=1, source_target_pairs={{0,4},{4,0},{1,5},{5,1},{2,6},{6,2},{3,7},{7,3}} | collective-permute-start | bytes 1179656 | tf_op jit(solution)/shard_map/ppermute | solution.py:399
  72.6 24.2 %collective-permute-start.8 = (bf16[384,512]{1,0:T(8,128)(2,1)S(1)}, bf16[384,512]{1,0:T(8,128)(2,1)}, u32[]{:S(2)}, u32[]{:S(2)}) collective-permute-start(bf16[384,512]{1,0:T(8,128)(2,1)S(1)} %collective-permute-done.7.refs_10_.refs_8_), channel_id=1, source_target_pairs={{24,28},{28,24},{25,29},{29,25},{26,30},{30,26},{27,31},{31,27}} | collective-permute-start | bytes 1179656 | tf_op jit(solution)/shard_map/ppermute | solution.py:399
  74.0 1.3 copy-start.2
  75.3 0.9 copy-start.3
  76.2 0.6 copy-start.5
  76.8 11.1 %copy-start.4 = (s32[8]{0:T(128)S(1)}, s32[8]{0:T(128)}, u32[]{:S(2)}) copy-start(s32[8]{0:T(128)} %counts_ref.5) | copy-start | bytes 100
  100.8 30.6 %collective-permute-start.16 = (bf16[128,3072]{1,0:T(8,128)(2,1)S(1)}, bf16[128,3072]{1,0:T(8,128)(2,1)S(1)}, u32[]{:S(2)}, u32[]{:S(2)}) collective-permute-start(bf16[128,3072]{1,0:T(8,128)(2,1)S(1)} %get-tuple-element.34), channel_id=1, source_target_pairs={{0,1},{1,0},{2,3},{3,2},{4,5},{5,4},{6,7},{7,6},{8,9},{9,8},{10,11... | collective-permute-start | bytes 2359304 | tf_op jit(solution)/shard_map/ppermute | solution.py:370
  111.5 22.9 %collective-permute-start.18 = (bf16[128,3072]{1,0:T(8,128)(2,1)S(1)}, bf16[128,3072]{1,0:T(8,128)(2,1)S(1)}, u32[]{:S(2)}, u32[]{:S(2)}) collective-permute-start(bf16[128,3072]{1,0:T(8,128)(2,1)S(1)} %get-tuple-element.38), channel_id=1, source_target_pairs={{0,1},{1,0},{2,3},{3,2},{4,5},{5,4},{6,7},{7,6},{8,9},{9,8},{10,11... | collective-permute-start | bytes 2359304 | tf_op jit(solution)/shard_map/ppermute | solution.py:370
  131.3 1.6 copy-start.1
  131.3 38.0 %collective-permute-start.15 = (bf16[256,3072]{1,0:T(8,128)(2,1)S(1)}, bf16[256,3072]{1,0:T(8,128)(2,1)S(1)}, u32[]{:S(2)}, u32[]{:S(2)}) collective-permute-start(bf16[256,3072]{1,0:T(8,128)(2,1)S(1)} %get-tuple-element.30), channel_id=1, source_target_pairs={{0,1},{1,0},{2,3},{3,2},{4,5},{5,4},{6,7},{7,6},{8,9},{9,8},{10,11... | collective-permute-start | bytes 4718600 | tf_op jit(solution)/shard_map/ppermute | solution.py:370
  133.0 20.4 %collective-permute-start.17 = (bf16[128,3072]{1,0:T(8,128)(2,1)S(1)}, bf16[128,3072]{1,0:T(8,128)(2,1)S(1)}, u32[]{:S(2)}, u32[]{:S(2)}) collective-permute-start(bf16[128,3072]{1,0:T(8,128)(2,1)S(1)} %add_convert_fusion.1), channel_id=1, source_target_pairs={{0,2},{1,3},{2,0},{3,1},{4,6},{5,7},{6,4},{7,5},{8,10},{9,11},{10,... | collective-permute-start | bytes 2359304 | tf_op jit(solution)/shard_map/ppermute | solution.py:370
  134.6 34.7 %collective-permute-start.19 = (bf16[128,3072]{1,0:T(8,128)(2,1)S(1)}, bf16[128,3072]{1,0:T(8,128)(2,1)S(1)}, u32[]{:S(2)}, u32[]{:S(2)}) collective-permute-start(bf16[128,3072]{1,0:T(8,128)(2,1)S(1)} %add_convert_fusion), channel_id=1, source_target_pairs={{0,2},{1,3},{2,0},{3,1},{4,6},{5,7},{6,4},{7,5},{8,10},{9,11},{10,... | collective-permute-start | bytes 2359304 | tf_op jit(solution)/shard_map/ppermute | solution.py:370
  153.4 15.9 %copy-start.9 = (bf16[128,3072]{1,0:T(8,128)(2,1)}, bf16[128,3072]{1,0:T(8,128)(2,1)S(1)}, u32[]{:S(2)}) copy-start(bf16[128,3072]{1,0:T(8,128)(2,1)S(1)} %collective-permute-done.17.second_ref) | copy-start | bytes 2359300
  169.3 0.9 copy-start.10
  169.3 1.4 copy-start.8

commit v5 on v4

--- a/solution.py
+++ b/solution.py
@@ -15,10 +15,10 @@
 REACH = 2
 SPAN = 2 * REACH + 1
 EPSILON = 1e-06
-PROJECT_VMEM = 32 << 20
-ATTEND_VMEM = 32 << 20
+PROJECT_VMEM = 28 << 20
+ATTEND_VMEM = 14 << 20
 OUTPUT_VMEM = 53 << 20
-PARTIAL_VMEM = 24 << 20
+SMALL_VMEM = 14 << 20
 
 f32 = jnp.float32
 bf16 = jnp.bfloat16
@@ -342,21 +342,26 @@
         out_ref[:, columns] = (total * gate_ref[:, columns]).astype(bf16)
 
 
-def partial_kernel(kept, total, held_ref, *refs):
+def partial_kernel(kept, sent, held_ref, *refs):
+    total = kept + sent
+    outs = (kept > 0) + (sent > 0)
     attended_refs = refs[:total]
-    weight_refs = refs[total:-2]
-    keep_ref, send_ref = refs[-2:]
-    rows = weight_refs[0].shape[0]
-    keep = kept * QB
+    weight_refs = refs[total:-outs]
+    rows = weight_refs[0].shape[0] // 2
     for index, weight_ref in enumerate(weight_refs):
-
-        @pl.when(held_ref[index] >= 0)
-        def _():
+        first = held_ref[index]
+
+        @pl.when(first >= 0)
+        def _(first=first, weight_ref=weight_ref):
             attended = jnp.concatenate([ref[...] for ref in attended_refs], axis=0)
             product = ntdot(attended, weight_ref[...])
-            columns = pl.ds(pl.multiple_of(held_ref[index] * rows, 128), rows)
-            keep_ref[:, columns] = product[0:keep]
-            send_ref[:, columns] = product[keep:].astype(bf16)
+            for half in range(2):
+                columns = pl.ds(pl.multiple_of((first ^ half) * rows, 128), rows)
+                piece = product[:, half * rows : (half + 1) * rows]
+                if kept:
+                    refs[-outs][:, columns] = piece[: kept * QB]
+                if sent:
+                    refs[-1][:, columns] = piece[kept * QB :].astype(bf16)
 
 
 def final_kernel(own_ref, first_ref, second_ref, third_ref, gate_ref, out_ref):
@@ -377,13 +382,12 @@
 def gathered_rows(own):
     count = lax.axis_size("wide")
     index = lax.axis_index("wide")
-    length = count // 2
-    blocks, held = [own], [index]
-    blocks.append(lax.ppermute(own, "wide", [(i, i ^ 1) for i in range(count)]))
-    held.append(index ^ 1)
+    other = flip(own, "wide", 1)
+    pair = jnp.concatenate([own, other], axis=0)
+    blocks, held = [pair], [index]
     for sign in (1, -1):
-        current = own
-        for step in range(1, length):
+        current = pair
+        for step in range(1, count // 2):
             move = 2 * sign
             route = [
                 (i, i + move)
@@ -392,12 +396,8 @@
             ]
             current = lax.ppermute(current, "wide", route)
             source = index - move * step
-            valid = (source >= 0) & (source < count)
             blocks.append(current)
-            held.append(jnp.where(valid, source, -1))
-            swap = [(i, i ^ 1) for i in range(count) if 0 <= i - move * step < count]
-            blocks.append(lax.ppermute(current, "wide", swap))
-            held.append(jnp.where(valid, source ^ 1, -1))
+            held.append(jnp.where((source >= 0) & (source < count), source, -1))
     return blocks, jnp.stack(held).astype(jnp.int32)
 
 
@@ -425,6 +425,7 @@
     count = -(-SPAN * share // 16) * 16
     piece = 3 * heads_width // wide_count
 
+    small = pltpu.CompilerParams(vmem_limit_bytes=SMALL_VMEM)
     chained = narrow_count == 4 and out_weight.shape[0] % 128 == 0 and row_total == 2 * QB
     if chained:
         blocks, held = gathered_rows(out_weight)
@@ -453,6 +454,7 @@
         out_shape=prep_shapes,
         in_specs=[smem] + [whole_spec()] * 7,
         out_specs=tuple(whole_spec() for _ in prep_shapes),
+        compiler_params=small,
         cost_estimate=cost(1 << 28, 4 << 20),
         name="prep",
     )
@@ -476,6 +478,7 @@
         out_shape=jax.ShapeDtypeStruct((3, patch, patch), bf16),
         in_specs=[whole_spec()],
         out_specs=whole_spec(),
+        compiler_params=small,
         name="gram",
     )(embed_weight)
     arrived = lax.all_to_all(payload, "wide", split_axis=0, concat_axis=0, tiled=True)
@@ -532,17 +535,19 @@
         gate = mod_gate.reshape(1, width)
 
         def multiply(attended, kept):
-            rows = len(attended) * QB
+            sent = len(attended) - kept
+            shapes = []
+            if kept:
+                shapes.append(jax.ShapeDtypeStruct((kept * QB, width), f32))
+            if sent:
+                shapes.append(jax.ShapeDtypeStruct((sent * QB, width), bf16))
             return pl.pallas_call(
-                functools.partial(partial_kernel, kept, len(attended)),
-                out_shape=(
-                    jax.ShapeDtypeStruct((kept * QB, width), f32),
-                    jax.ShapeDtypeStruct((rows - kept * QB, width), bf16),
-                ),
+                functools.partial(partial_kernel, kept, sent),
+                out_shape=tuple(shapes),
                 in_specs=[smem] + [whole_spec()] * (len(attended) + len(blocks)),
-                out_specs=(whole_spec(),) * 2,
-                compiler_params=pltpu.CompilerParams(vmem_limit_bytes=PARTIAL_VMEM),
-                cost_estimate=cost(2 * rows * heads_width * width, 8 << 20),
+                out_specs=(whole_spec(),) * len(shapes),
+                compiler_params=small,
+                cost_estimate=cost(2 * len(attended) * QB * heads_width * width, 8 << 20),
             )(held, *attended, *blocks)
 
         far = []
@@ -552,14 +557,15 @@
             other = flip(send, "narrow", 1)
             joined = (keep + other.astype(f32)).astype(bf16)
             far.append(flip(joined, "narrow", 2))
-        attended = attend(((0, 0), (0, 1), (1, 0), (1, 1)))
-        own, send = multiply(attended, 2)
+        (send,) = multiply(attend(((1, 0), (1, 1))), 0)
         other = flip(send, "narrow", 1)
+        (own,) = multiply(attend(((0, 0), (0, 1))), parts)
         return pl.pallas_call(
             final_kernel,
             out_shape=jax.ShapeDtypeStruct((row_total, width), bf16),
             in_specs=[whole_spec()] * 5,
             out_specs=whole_spec(),
+            compiler_params=small,
             name="final",
         )(own, other, *far, gate)
 

time: 177 us -> 176 us (level)
  starting transfers between devices: 44.8 us -> 33.8 us
  waiting for transfers between devices: 51.9 us -> 62.3 us
  Pallas kernels: 65.4 us -> 60.6 us
  local copies, waits for them, and re-layouts: 6.72 us -> 11.2 us
    ppermute x6, waiting for transfers between devices: 4.15 us -> 22.6 us  [gathered_rows(): current = lax.ppermute(current, 'wide', route)]
    ppermute x7 -> x0, starting transfers between devices: 14.3 us -> none  [the longest x6 13.3 us: gathered_rows(): blocks.append(lax.ppermute(current, 'wide', swap))]
    all_to_all x1, waiting for transfers between devices: 12.4 us -> 0.01 us  [block(): lax.all_to_all(payload, 'wide', split_axis=0, concat_axis=0, tiled=True)]
    ppermute x7 -> x8, waiting for transfers between devices: 34.1 us -> 39.8 us  [flip(): return lax.ppermute(block, axis, [(i, i ^ bit) for i in devices])]
    unnamed x26 -> x39, local copies, waits for them, and re-layouts: 5.58 us -> 10.1 us
    ppermute x7 -> x8, starting transfers between devices: 4.39 us -> 7.97 us  [flip(): return lax.ppermute(block, axis, [(i, i ^ bit) for i in devices])]
    pallas_call x1, Pallas kernels: 4.52 us -> 1.8 us  [block(): pl.pallas_call(final_kernel, out_shape=jax.ShapeDtypeStruct((row_total, w...]
    pallas_call x3 -> x4, Pallas kernels: 29.3 us -> 31.5 us  [attend(): pl.pallas_call(functools.partial(attend_kernel, parts, entries), out_shap...]
  transfers between devices with their start and end apart: 22 -> 16, of which waited for: 5 -> 6; matrix products, arithmetic and copies ran while one was open for 4% -> 4% of each run, Pallas kernels for 30% -> 31%
where the time goes in v5:
time: 176 us; the launch traced here: 174 us
  waiting for transfers between devices  62.3 us (35%)
  Pallas kernels  60.6 us (34%)
  starting transfers between devices  33.8 us (19%)
  local copies, waits for them, and re-layouts  11.2 us (6%)
  other arithmetic  6.1 us (3%)
    ppermute x8, waiting for transfers between devices, flip(): return lax.ppermute(block, axis, [(i, i ^ bit) for i in devices])  39.8 us
    pallas_call x4, Pallas kernels, attend(): pl.pallas_call(functools.partial(attend_kernel, parts, entries), out_shap...  31.5 us
    ppermute x6, waiting for transfers between devices, gathered_rows(): current = lax.ppermute(current, 'wide', route)  22.6 us
    ppermute x6, starting transfers between devices, gathered_rows(): current = lax.ppermute(current, 'wide', route)  15.2 us
    pallas_call x4, Pallas kernels, multiply(): pl.pallas_call(functools.partial(partial_kernel, kept, sent), out_shape=t...  13.3 us
    pallas_call x1, Pallas kernels, block(): pl.pallas_call(functools.partial(project_kernel, row_total, tile_size), o...  10.5 us
    unnamed x39, local copies, waits for them, and re-layouts  10.1 us
    ppermute x8, starting transfers between devices, flip(): return lax.ppermute(block, axis, [(i, i ^ bit) for i in devices])  7.97 us
  transfers between devices with their start and end apart: 16, of which 6 were waited for; matrix products, arithmetic and copies ran while one was open for 4% of the time, Pallas kernels for 31%

profile of v5, /device:TPU:16, one launch (start us, length us, event | category | flops | bytes accessed | tf_op | source)
XLA Modules:
  0.0 174.4 jit_solution(3790432314664455593)
XLA Ops:
  0.0 1.1 copy-done
  1.1 1.3 copy-done.3
  2.4 0.8 copy-done.6
  3.2 0.7 copy-done.8
  4.0 0.7 copy-done.9
  4.7 0.7 copy-done.12
  5.3 1.8 %prep.1 = bf16[8,384,128]{2,1,0:T(8,128)(2,1)} custom-call(s32[1]{0:T(128)} %bitcast.7.at_ref, bf16[128,3072]{1,0:T(8,128)(2,1)S(1)} %copy-done, bf16[128,3072]{1,0:T(8,128)(2,1)S(1)} %copy-done, f32[1,3072]{1,0:T(1,128)S(1)} %bitcast.23, f32[1,3072]{1,0:T(1,128)S(1)} %bitcast.24, bf16[3,384,512]{2,1,0:T(8,128)(2,1)S(1)} %copy-done.3, ...), custom_call_target="tpu_custom_call" | custom-call | flops 268435456 | bytes 4194304 | tf_op jit(solution)/shard_map/prep/pallas_call | solution.py:461
  7.2 6.3 %all-to-all-start = ((bf16[8,384,128]{2,1,0:T(8,128)(2,1)}), bf16[8,384,128]{2,1,0:T(8,128)(2,1)S(1)}, u32[]{:S(2)}, u32[]{:S(2)}) async-start(bf16[8,384,128]{2,1,0:T(8,128)(2,1)} %prep.1), calls=%async_computation | async-start | bytes 1572864 | tf_op jit(solution)/shard_map/all_to_all | solution.py:484
  13.5 1.5 collective-permute-start.2
  15.0 17.1 %collective-permute-done.2 = bf16[384,512]{1,0:T(8,128)(2,1)S(1)} collective-permute-done((bf16[384,512]{1,0:T(8,128)(2,1)S(1)}, bf16[384,512]{1,0:T(8,128)(2,1)S(1)}, u32[]{:S(2)}, u32[]{:S(2)}) %collective-permute-start.2) | collective-permute-done | bytes 393248 | tf_op jit(solution)/shard_map/ppermute | solution.py:375
  32.1 2.5 %collective-permute-start.6 = (bf16[768,512]{1,0:T(8,128)(2,1)S(1)}, bf16[768,512]{1,0:T(8,128)(2,1)S(1)}, u32[]{:S(2)}, u32[]{:S(2)}) collective-permute-start(bf16[768,512]{1,0:T(8,128)(2,1)S(1)} %constant_dynamic-update-slice_fusion.refs_2_), channel_id=1, source_target_pairs={{8,0},{12,4},{16,8},{20,12},{24,16},{28,20},{9,1},{13,5},{17,9},{2... | collective-permute-start | bytes 2359304 | tf_op jit(solution)/shard_map/ppermute | solution.py:397
  34.6 3.4 %collective-permute-start.3 = (bf16[768,512]{1,0:T(8,128)(2,1)S(1)}, bf16[768,512]{1,0:T(8,128)(2,1)S(1)}, u32[]{:S(2)}, u32[]{:S(2)}) collective-permute-start(bf16[768,512]{1,0:T(8,128)(2,1)S(1)} %constant_dynamic-update-slice_fusion.refs_2_), channel_id=1, source_target_pairs={{0,8},{4,12},{8,16},{12,20},{16,24},{20,28},{1,9},{5,13},{9,17},{1... | collective-permute-start | bytes 2359304 | tf_op jit(solution)/shard_map/ppermute | solution.py:397
  38.1 0.0 all-to-all-done
  38.1 0.0 copy-start.13
  38.1 0.1 reshape_squeeze.3
  38.3 0.0 copy-start.17
  38.3 1.6 collective-permute-start
  39.9 13.4 %collective-permute-done.6.refs_6_ = bf16[768,512]{1,0:T(8,128)(2,1)S(1)} collective-permute-done((bf16[768,512]{1,0:T(8,128)(2,1)S(1)}, bf16[768,512]{1,0:T(8,128)(2,1)S(1)}, u32[]{:S(2)}, u32[]{:S(2)}) %collective-permute-start.6) | collective-permute-done | bytes 786464 | tf_op jit(solution)/shard_map/ppermute | solution.py:397
  53.2 2.4 %collective-permute-start.7 = (bf16[768,512]{1,0:T(8,128)(2,1)S(1)}, bf16[768,512]{1,0:T(8,128)(2,1)S(1)}, u32[]{:S(2)}, u32[]{:S(2)}) collective-permute-start(bf16[768,512]{1,0:T(8,128)(2,1)S(1)} %collective-permute-done.6.refs_6_), channel_id=1, source_target_pairs={{8,0},{12,4},{16,8},{20,12},{9,1},{13,5},{17,9},{21,13},{10,2},{14... | collective-permute-start | bytes 2359304 | tf_op jit(solution)/shard_map/ppermute | solution.py:397
  55.6 0.0 collective-permute-done.3.refs_3_
  55.6 3.2 %collective-permute-start.4 = (bf16[768,512]{1,0:T(8,128)(2,1)S(1)}, bf16[768,512]{1,0:T(8,128)(2,1)}, u32[]{:S(2)}, u32[]{:S(2)}) collective-permute-start(bf16[768,512]{1,0:T(8,128)(2,1)S(1)} %collective-permute-done.3.refs_3_), channel_id=1, source_target_pairs={{8,16},{12,20},{16,24},{20,28},{9,17},{13,21},{17,25},{21,29},{10,... | collective-permute-start | bytes 2359304 | tf_op jit(solution)/shard_map/ppermute | solution.py:397
  58.8 0.0 collective-permute-done
  58.9 1.9 %pad_maximum_fusion.1 = bf16[2,1296,128]{2,1,0:T(8,128)(2,1)} fusion(bf16[1,1296,128]{2,1,0:T(8,128)(2,1)} %collective-permute-done, bf16[1,1296,128]{2,1,0:T(8,128)(2,1)S(1)} %maximum_bitcast_fusion), kind=kLoop, calls=%fused_computation.3 | loop fusion | flops 331776 | bytes 1327104 | tf_op jit(solution)/shard_map/concatenate | solution.py:499
  60.7 0.1 slice_reduce_fusion
  60.8 0.8 broadcast_in_dim.10
  61.6 4.3 %all-to-all-start.1 = ((bf16[8,192,128]{2,1,0:T(8,128)(2,1)}), bf16[8,192,128]{2,1,0:T(8,128)(2,1)S(1)}, u32[]{:S(2)}, u32[]{:S(2)}) async-start(bf16[8,192,128]{2,1,0:T(8,128)(2,1)} %broadcast_in_dim.10), calls=%async_computation.1 | async-start | bytes 786432 | tf_op jit(solution)/shard_map/all_to_all | solution.py:501
  66.0 0.0 copy-start.1
  66.0 1.1 copy-done.1
  67.1 1.7 gram.1.gram_ref
  68.8 0.6 copy-done.4
  69.4 0.1 reshape.31.starts_ref
  69.5 0.1 stack.31.held_ref
  69.6 1.4 convert_reduce_fusion.bias_ref
  71.0 6.5 %collective-permute-done.7.refs_7_ = bf16[768,512]{1,0:T(8,128)(2,1)S(1)} collective-permute-done((bf16[768,512]{1,0:T(8,128)(2,1)S(1)}, bf16[768,512]{1,0:T(8,128)(2,1)S(1)}, u32[]{:S(2)}, u32[]{:S(2)}) %collective-permute-start.7) | collective-permute-done | bytes 786464 | tf_op jit(solution)/shard_map/ppermute | solution.py:397
  77.4 1.6 collective-permute-start.8
  79.0 2.7 %collective-permute-done.4.refs_4_ = bf16[768,512]{1,0:T(8,128)(2,1)} collective-permute-done((bf16[768,512]{1,0:T(8,128)(2,1)S(1)}, bf16[768,512]{1,0:T(8,128)(2,1)}, u32[]{:S(2)}, u32[]{:S(2)}) %collective-permute-start.4) | collective-permute-done | bytes 786464 | tf_op jit(solution)/shard_map/ppermute | solution.py:397
  81.7 2.2 %collective-permute-start.5 = (bf16[768,512]{1,0:T(8,128)(2,1)}, bf16[768,512]{1,0:T(8,128)(2,1)}, u32[]{:S(2)}, u32[]{:S(2)}) collective-permute-start(bf16[768,512]{1,0:T(8,128)(2,1)} %collective-permute-done.4.refs_4_), channel_id=1, source_target_pairs={{16,24},{20,28},{17,25},{21,29},{18,26},{22,30},{19,27},{23,31}} | collective-permute-start | bytes 2359304 | tf_op jit(solution)/shard_map/ppermute | solution.py:397
  83.9 2.5 %pad_maximum_fusion.patches_ref = bf16[4,1296,128]{2,1,0:T(8,128)(2,1)} fusion(bf16[2,1296,128]{2,1,0:T(8,128)(2,1)} %collective-permute-done.1, bf16[1,1296,128]{2,1,0:T(8,128)(2,1)} %collective-permute-done, bf16[1,1296,128]{2,1,0:T(8,128)(2,1)} %copy-done.15), kind=kLoop, calls=%fused_computation.2 | loop fusion | flops 1327104 | bytes 2654208 | tf_op jit(solution)/shard_map/concatenate | solution.py:499
  86.4 1.3 copy-done.2
  87.7 0.9 copy-done.5
  88.6 0.7 copy-done.11
  89.3 10.5 %project.1 = (bf16[512,5120]{1,0:T(8,128)(2,1)S(1)}, bf16[5120,512]{1,0:T(8,128)(2,1)S(1)}, bf16[8,4,256,128]{3,2,1,0:T(8,128)(2,1)S(1)}) custom-call(s32[4]{0:T(128)S(1)} %broadcast_xor_fusion.order_ref, bf16[4,1296,128]{2,1,0:T(8,128)(2,1)S(1)} %copy-done.2, bf16[1536,128]{1,0:T(8,128)(2,1)S(1)} %bitcast.21, f32[16,128]{1,0:T(8,128)S(1)} %copy-done.11, ...), custom_call_target="tpu_custom_call" | custom-call | flops 3355443200 | bytes 16777216 | tf_op jit(solution)/shard_map/project/pallas_call | solution.py:508
  99.8 8.8 %shard_map.113 = (bf16[128,512]{1,0:T(8,128)(2,1)S(1)}, bf16[128,512]{1,0:T(8,128)(2,1)S(1)}) custom-call(s32[4]{0:T(128)S(1)} %broadcast_xor_fusion.order_ref, s32[64]{0:T(128)S(1)} %reshape.31.starts_ref, s32[8]{0:T(128)S(1)} %copy-done.10, bf16[512,5120]{1,0:T(8,128)(2,1)S(1)} %get-tuple-element.20.keys_ref, ...), custom_call_target="tpu_custom_call" | custom-call | flops 2147483648 | bytes 16777216 | tf_op jit(solution)/shard_map/pallas_call | solution.py:524
  108.6 0.0 collective-permute-done.8.refs_8_
  108.6 0.0 collective-permute-done.5.refs_5_
  108.6 3.3 %shard_map.114 = (f32[128,3072]{1,0:T(8,128)S(1)}, bf16[128,3072]{1,0:T(8,128)(2,1)S(1)}) custom-call(s32[7]{0:T(128)S(1)} %stack.31.held_ref, bf16[128,512]{1,0:T(8,128)(2,1)S(1)} %get-tuple-element.27.refs_0_, bf16[128,512]{1,0:T(8,128)(2,1)S(1)} %get-tuple-element.28.refs_1_, bf16[768,512]{1,0:T(8,128)(2,1)S(1)} %constant_dynamic-update-slice_fusion.refs_2_, ...), custom_call_target="tpu_custom_call" | custom-call | flops 805306368 | bytes 8388608 | tf_op jit(solution)/shard_map/pallas_call | solution.py:544
  111.9 0.1 collective-permute-start.10
  112.0 6.3 %shard_map.115 = (bf16[128,512]{1,0:T(8,128)(2,1)S(1)}, bf16[128,512]{1,0:T(8,128)(2,1)S(1)}) custom-call(s32[4]{0:T(128)S(1)} %broadcast_xor_fusion.order_ref, s32[64]{0:T(128)S(1)} %reshape.31.starts_ref, s32[8]{0:T(128)S(1)} %copy-done.10, bf16[512,5120]{1,0:T(8,128)(2,1)S(1)} %get-tuple-element.20.keys_ref, ...), custom_call_target="tpu_custom_call" | custom-call | flops 2147483648 | bytes 16777216 | tf_op jit(solution)/shard_map/pallas_call | solution.py:524
  118.3 7.7 %shard_map.111 = (bf16[128,512]{1,0:T(8,128)(2,1)S(1)}, bf16[128,512]{1,0:T(8,128)(2,1)S(1)}) custom-call(s32[4]{0:T(128)S(1)} %broadcast_xor_fusion.order_ref, s32[64]{0:T(128)S(1)} %reshape.31.starts_ref, s32[8]{0:T(128)S(1)} %copy-done.10, bf16[512,5120]{1,0:T(8,128)(2,1)S(1)} %get-tuple-element.20.keys_ref, ...), custom_call_target="tpu_custom_call" | custom-call | flops 2147483648 | bytes 16777216 | tf_op jit(solution)/shard_map/pallas_call | solution.py:524
  126.0 3.3 %shard_map.116 = (f32[128,3072]{1,0:T(8,128)S(1)}, bf16[128,3072]{1,0:T(8,128)(2,1)S(1)}) custom-call(s32[7]{0:T(128)S(1)} %stack.31.held_ref, bf16[128,512]{1,0:T(8,128)(2,1)S(1)} %get-tuple-element.31.refs_0_, bf16[128,512]{1,0:T(8,128)(2,1)S(1)} %get-tuple-element.32.refs_1_, bf16[768,512]{1,0:T(8,128)(2,1)S(1)} %constant_dynamic-update-slice_fusion.refs_2_, ...), custom_call_target="tpu_custom_call" | custom-call | flops 805306368 | bytes 8388608 | tf_op jit(solution)/shard_map/pallas_call | solution.py:544
  129.3 1.8 %collective-permute-start.12 = (bf16[128,3072]{1,0:T(8,128)(2,1)S(1)}, bf16[128,3072]{1,0:T(8,128)(2,1)S(1)}, u32[]{:S(2)}, u32[]{:S(2)}) collective-permute-start(bf16[128,3072]{1,0:T(8,128)(2,1)S(1)} %get-tuple-element.34), channel_id=1, source_target_pairs={{0,1},{1,0},{2,3},{3,2},{4,5},{5,4},{6,7},{7,6},{8,9},{9,8},{10,11... | collective-permute-start | bytes 2359304 | tf_op jit(solution)/shard_map/ppermute | solution.py:375
  131.1 3.3 %shard_map.112 = bf16[256,3072]{1,0:T(8,128)(2,1)S(1)} custom-call(s32[7]{0:T(128)S(1)} %stack.31.held_ref, bf16[128,512]{1,0:T(8,128)(2,1)S(1)} %get-tuple-element.25.refs_0_, bf16[128,512]{1,0:T(8,128)(2,1)S(1)} %get-tuple-element.26.refs_1_, bf16[768,512]{1,0:T(8,128)(2,1)S(1)} %constant_dynamic-update-slice_fusion.refs_2_, ...), custom_call_target="tpu_custom_call" | custom-call | flops 805306368 | bytes 8388608 | tf_op jit(solution)/shard_map/pallas_call | solution.py:544
  134.4 0.1 collective-permute-start.9
  134.5 0.0 collective-permute-done.10
  134.5 0.2 add_convert_fusion.1
  134.7 2.9 %collective-permute-start.11 = (bf16[128,3072]{1,0:T(8,128)(2,1)S(1)}, bf16[128,3072]{1,0:T(8,128)(2,1)S(1)}, u32[]{:S(2)}, u32[]{:S(2)}) collective-permute-start(bf16[128,3072]{1,0:T(8,128)(2,1)S(1)} %add_convert_fusion.1), channel_id=1, source_target_pairs={{0,2},{1,3},{2,0},{3,1},{4,6},{5,7},{6,4},{7,5},{8,10},{9,11},{10,... | collective-permute-start | bytes 2359304 | tf_op jit(solution)/shard_map/ppermute | solution.py:375
  137.6 0.2 add_convert_fusion
  137.7 0.1 collective-permute-start.13
  137.8 8.8 %shard_map.109 = (bf16[128,512]{1,0:T(8,128)(2,1)S(1)}, bf16[128,512]{1,0:T(8,128)(2,1)S(1)}) custom-call(s32[4]{0:T(128)S(1)} %broadcast_xor_fusion.order_ref, s32[64]{0:T(128)S(1)} %reshape.31.starts_ref, s32[8]{0:T(128)S(1)} %copy-done.10, bf16[512,5120]{1,0:T(8,128)(2,1)S(1)} %get-tuple-element.20.keys_ref, ...), custom_call_target="tpu_custom_call" | custom-call | flops 2147483648 | bytes 16777216 | tf_op jit(solution)/shard_map/pallas_call | solution.py:524
  146.6 0.0 copy-start.7
  146.6 3.4 %shard_map.110.own_ref = f32[256,3072]{1,0:T(8,128)S(1)} custom-call(s32[7]{0:T(128)S(1)} %stack.31.held_ref, bf16[128,512]{1,0:T(8,128)(2,1)S(1)} %get-tuple-element.23.refs_0_, bf16[128,512]{1,0:T(8,128)(2,1)S(1)} %get-tuple-element.24.refs_1_, bf16[768,512]{1,0:T(8,128)(2,1)S(1)} %constant_dynamic-update-slice_fusion.refs_2_, ...), custom_call_target="tpu_custom_call" | custom-call | flops 805306368 | bytes 8388608 | tf_op jit(solution)/shard_map/pallas_call | solution.py:544
  150.0 6.0 %collective-permute-done.11.second_ref = bf16[128,3072]{1,0:T(8,128)(2,1)S(1)} collective-permute-done((bf16[128,3072]{1,0:T(8,128)(2,1)S(1)}, bf16[128,3072]{1,0:T(8,128)(2,1)S(1)}, u32[]{:S(2)}, u32[]{:S(2)}) %collective-permute-start.11) | collective-permute-done | bytes 786464 | tf_op jit(solution)/shard_map/ppermute | solution.py:375
  155.9 16.7 %collective-permute-done.13.third_ref = bf16[128,3072]{1,0:T(8,128)(2,1)S(1)} collective-permute-done((bf16[128,3072]{1,0:T(8,128)(2,1)S(1)}, bf16[128,3072]{1,0:T(8,128)(2,1)S(1)}, u32[]{:S(2)}, u32[]{:S(2)}) %collective-permute-start.13) | collective-permute-done | bytes 786464 | tf_op jit(solution)/shard_map/ppermute | solution.py:375
  172.6 1.8 %final.1 = bf16[256,3072]{1,0:T(8,128)(2,1)} custom-call(f32[256,3072]{1,0:T(8,128)S(1)} %shard_map.110.own_ref, bf16[256,3072]{1,0:T(8,128)(2,1)S(1)} %collective-permute-done.9.first_ref, bf16[128,3072]{1,0:T(8,128)(2,1)S(1)} %collective-permute-done.11.second_ref, bf16[128,3072]{1,0:T(8,128)(2,1)S(1)} %collective-permute-done.13.third_ref, ...), custom_call_target="tpu_custom_call" | custom-call | tf_op jit(solution)/shard_map/final/pallas_call | solution.py:563
  (37 shorter events, 0.2 us)
Async XLA Ops:
  0.0 1.1 copy-start
  1.1 1.3 copy-start.3
  2.4 0.8 copy-start.6
  3.2 0.7 copy-start.8
  4.0 0.7 copy-start.9
  4.7 0.7 copy-start.12
  7.2 6.3 %copy-start.16 = (bf16[384,512]{1,0:T(8,128)(2,1)S(1)}, bf16[384,512]{1,0:T(8,128)(2,1)}, u32[]{:S(2)}) copy-start(bf16[384,512]{1,0:T(8,128)(2,1)} %param.17) | copy-start | bytes 1179652
  7.2 30.9 %all-to-all-start = ((bf16[8,384,128]{2,1,0:T(8,128)(2,1)}), bf16[8,384,128]{2,1,0:T(8,128)(2,1)S(1)}, u32[]{:S(2)}, u32[]{:S(2)}) async-start(bf16[8,384,128]{2,1,0:T(8,128)(2,1)} %prep.1), calls=%async_computation | async-start | bytes 1572864 | tf_op jit(solution)/shard_map/all_to_all | solution.py:484
  13.5 18.6 %collective-permute-start.2 = (bf16[384,512]{1,0:T(8,128)(2,1)S(1)}, bf16[384,512]{1,0:T(8,128)(2,1)S(1)}, u32[]{:S(2)}, u32[]{:S(2)}) collective-permute-start(bf16[384,512]{1,0:T(8,128)(2,1)S(1)} %copy-done.16), channel_id=1, source_target_pairs={{0,4},{4,0},{8,12},{12,8},{16,20},{20,16},{24,28},{28,24},{1,5},{5... | collective-permute-start | bytes 1179656 | tf_op jit(solution)/shard_map/ppermute | solution.py:375
  32.1 21.1 %collective-permute-start.6 = (bf16[768,512]{1,0:T(8,128)(2,1)S(1)}, bf16[768,512]{1,0:T(8,128)(2,1)S(1)}, u32[]{:S(2)}, u32[]{:S(2)}) collective-permute-start(bf16[768,512]{1,0:T(8,128)(2,1)S(1)} %constant_dynamic-update-slice_fusion.refs_2_), channel_id=1, source_target_pairs={{8,0},{12,4},{16,8},{20,12},{24,16},{28,20},{9,1},{13,5},{17,9},{2... | collective-permute-start | bytes 2359304 | tf_op jit(solution)/shard_map/ppermute | solution.py:397
  34.6 21.0 %collective-permute-start.3 = (bf16[768,512]{1,0:T(8,128)(2,1)S(1)}, bf16[768,512]{1,0:T(8,128)(2,1)S(1)}, u32[]{:S(2)}, u32[]{:S(2)}) collective-permute-start(bf16[768,512]{1,0:T(8,128)(2,1)S(1)} %constant_dynamic-update-slice_fusion.refs_2_), channel_id=1, source_target_pairs={{0,8},{4,12},{8,16},{12,20},{16,24},{20,28},{1,9},{5,13},{9,17},{1... | collective-permute-start | bytes 2359304 | tf_op jit(solution)/shard_map/ppermute | solution.py:397
  38.1 1.8 %copy-start.13 = (bf16[8,384,128]{2,1,0:T(8,128)(2,1)}, bf16[8,384,128]{2,1,0:T(8,128)(2,1)S(1)}, u32[]{:S(2)}) copy-start(bf16[8,384,128]{2,1,0:T(8,128)(2,1)S(1)} %all-to-all-done) | copy-start | bytes 2359300
  38.3 23.3 %copy-start.15 = (bf16[1,1296,128]{2,1,0:T(8,128)(2,1)}, bf16[1,1296,128]{2,1,0:T(8,128)(2,1)S(1)}, u32[]{:S(2)}) copy-start(bf16[1,1296,128]{2,1,0:T(8,128)(2,1)S(1)} %maximum_bitcast_fusion) | copy-start | bytes 995332
  38.3 27.6 %copy-start.17 = (s32[8,8]{1,0:T(8,128)S(1)}, s32[8,8]{1,0:T(8,128)}, u32[]{:S(2)}) copy-start(s32[8,8]{1,0:T(8,128)} %param.19) | copy-start | bytes 772
  38.3 20.5 %collective-permute-start = (bf16[1,1296,128]{2,1,0:T(8,128)(2,1)S(1)}, bf16[1,1296,128]{2,1,0:T(8,128)(2,1)}, u32[]{:S(2)}, u32[]{:S(2)}) collective-permute-start(bf16[1,1296,128]{2,1,0:T(8,128)(2,1)S(1)} %maximum_bitcast_fusion), channel_id=1, source_target_pairs={{0,2},{1,3},{2,0},{3,1},{4,6},{5,7},{6,4},{7,5},{8,10},{9,11},{10,... | collective-permute-start | bytes 995336 | tf_op jit(solution)/shard_map/ppermute | solution.py:375
  53.2 7.5 %copy-start.14 = (bf16[8,384,128]{2,1,0:T(8,128)(2,1)S(1)}, bf16[8,384,128]{2,1,0:T(8,128)(2,1)}, u32[]{:S(2)}) copy-start(bf16[8,384,128]{2,1,0:T(8,128)(2,1)} %copy-done.13) | copy-start | bytes 2359300
  53.2 24.2 %collective-permute-start.7 = (bf16[768,512]{1,0:T(8,128)(2,1)S(1)}, bf16[768,512]{1,0:T(8,128)(2,1)S(1)}, u32[]{:S(2)}, u32[]{:S(2)}) collective-permute-start(bf16[768,512]{1,0:T(8,128)(2,1)S(1)} %collective-permute-done.6.refs_6_), channel_id=1, source_target_pairs={{8,0},{12,4},{16,8},{20,12},{9,1},{13,5},{17,9},{21,13},{10,2},{14... | collective-permute-start | bytes 2359304 | tf_op jit(solution)/shard_map/ppermute | solution.py:397
  55.6 26.1 %collective-permute-start.4 = (bf16[768,512]{1,0:T(8,128)(2,1)S(1)}, bf16[768,512]{1,0:T(8,128)(2,1)}, u32[]{:S(2)}, u32[]{:S(2)}) collective-permute-start(bf16[768,512]{1,0:T(8,128)(2,1)S(1)} %collective-permute-done.3.refs_3_), channel_id=1, source_target_pairs={{8,16},{12,20},{16,24},{20,28},{9,17},{13,21},{17,25},{21,29},{10,... | collective-permute-start | bytes 2359304 | tf_op jit(solution)/shard_map/ppermute | solution.py:397
  60.7 8.9 %copy-start.18 = (s32[4]{0:T(128)S(1)}, s32[4]{0:T(128)}, u32[]{:S(2)}) copy-start(s32[4]{0:T(128)} %constant.46.clone) | copy-start | bytes 52
  60.7 23.2 %collective-permute-start.1 = (bf16[2,1296,128]{2,1,0:T(8,128)(2,1)}, bf16[2,1296,128]{2,1,0:T(8,128)(2,1)}, u32[]{:S(2)}, u32[]{:S(2)}) collective-permute-start(bf16[2,1296,128]{2,1,0:T(8,128)(2,1)} %pad_maximum_fusion.1), channel_id=1, source_target_pairs={{0,1},{1,0},{2,3},{3,2},{4,5},{5,4},{6,7},{7,6},{8,9},{9,8},{10,11... | collective-permute-start | bytes 1990664 | tf_op jit(solution)/shard_map/ppermute | solution.py:375
  61.6 24.8 %all-to-all-start.1 = ((bf16[8,192,128]{2,1,0:T(8,128)(2,1)}), bf16[8,192,128]{2,1,0:T(8,128)(2,1)S(1)}, u32[]{:S(2)}, u32[]{:S(2)}) async-start(bf16[8,192,128]{2,1,0:T(8,128)(2,1)} %broadcast_in_dim.10), calls=%async_computation.1 | async-start | bytes 786432 | tf_op jit(solution)/shard_map/all_to_all | solution.py:501
  66.0 1.1 copy-start.1
  68.8 0.6 copy-start.4
  77.4 31.1 %collective-permute-start.8 = (bf16[768,512]{1,0:T(8,128)(2,1)S(1)}, bf16[768,512]{1,0:T(8,128)(2,1)}, u32[]{:S(2)}, u32[]{:S(2)}) collective-permute-start(bf16[768,512]{1,0:T(8,128)(2,1)S(1)} %collective-permute-done.7.refs_7_), channel_id=1, source_target_pairs={{8,0},{12,4},{9,1},{13,5},{10,2},{14,6},{11,3},{15,7}} | collective-permute-start | bytes 2359304 | tf_op jit(solution)/shard_map/ppermute | solution.py:397
  81.7 26.9 %collective-permute-start.5 = (bf16[768,512]{1,0:T(8,128)(2,1)}, bf16[768,512]{1,0:T(8,128)(2,1)}, u32[]{:S(2)}, u32[]{:S(2)}) collective-permute-start(bf16[768,512]{1,0:T(8,128)(2,1)} %collective-permute-done.4.refs_4_), channel_id=1, source_target_pairs={{16,24},{20,28},{17,25},{21,29},{18,26},{22,30},{19,27},{23,31}} | collective-permute-start | bytes 2359304 | tf_op jit(solution)/shard_map/ppermute | solution.py:397
  86.4 1.3 copy-start.2
  87.7 0.9 copy-start.5
  88.6 0.7 copy-start.11
  89.3 10.5 %copy-start.10 = (s32[8]{0:T(128)S(1)}, s32[8]{0:T(128)}, u32[]{:S(2)}) copy-start(s32[8]{0:T(128)} %counts_ref.7) | copy-start | bytes 100
  111.9 22.6 %collective-permute-start.10 = (bf16[128,3072]{1,0:T(8,128)(2,1)S(1)}, bf16[128,3072]{1,0:T(8,128)(2,1)S(1)}, u32[]{:S(2)}, u32[]{:S(2)}) collective-permute-start(bf16[128,3072]{1,0:T(8,128)(2,1)S(1)} %get-tuple-element.30), channel_id=1, source_target_pairs={{0,1},{1,0},{2,3},{3,2},{4,5},{5,4},{6,7},{7,6},{8,9},{9,8},{10,11... | collective-permute-start | bytes 2359304 | tf_op jit(solution)/shard_map/ppermute | solution.py:375
  129.3 8.3 %collective-permute-start.12 = (bf16[128,3072]{1,0:T(8,128)(2,1)S(1)}, bf16[128,3072]{1,0:T(8,128)(2,1)S(1)}, u32[]{:S(2)}, u32[]{:S(2)}) collective-permute-start(bf16[128,3072]{1,0:T(8,128)(2,1)S(1)} %get-tuple-element.34), channel_id=1, source_target_pairs={{0,1},{1,0},{2,3},{3,2},{4,5},{5,4},{6,7},{7,6},{8,9},{9,8},{10,11... | collective-permute-start | bytes 2359304 | tf_op jit(solution)/shard_map/ppermute | solution.py:375
  134.4 15.6 %collective-permute-start.9 = (bf16[256,3072]{1,0:T(8,128)(2,1)S(1)}, bf16[256,3072]{1,0:T(8,128)(2,1)S(1)}, u32[]{:S(2)}, u32[]{:S(2)}) collective-permute-start(bf16[256,3072]{1,0:T(8,128)(2,1)S(1)} %shard_map.112), channel_id=1, source_target_pairs={{0,1},{1,0},{2,3},{3,2},{4,5},{5,4},{6,7},{7,6},{8,9},{9,8},{10,11... | collective-permute-start | bytes 4718600 | tf_op jit(solution)/shard_map/ppermute | solution.py:375
  134.7 21.3 %collective-permute-start.11 = (bf16[128,3072]{1,0:T(8,128)(2,1)S(1)}, bf16[128,3072]{1,0:T(8,128)(2,1)S(1)}, u32[]{:S(2)}, u32[]{:S(2)}) collective-permute-start(bf16[128,3072]{1,0:T(8,128)(2,1)S(1)} %add_convert_fusion.1), channel_id=1, source_target_pairs={{0,2},{1,3},{2,0},{3,1},{4,6},{5,7},{6,4},{7,5},{8,10},{9,11},{10,... | collective-permute-start | bytes 2359304 | tf_op jit(solution)/shard_map/ppermute | solution.py:375
  137.7 34.9 %collective-permute-start.13 = (bf16[128,3072]{1,0:T(8,128)(2,1)S(1)}, bf16[128,3072]{1,0:T(8,128)(2,1)S(1)}, u32[]{:S(2)}, u32[]{:S(2)}) collective-permute-start(bf16[128,3072]{1,0:T(8,128)(2,1)S(1)} %add_convert_fusion), channel_id=1, source_target_pairs={{0,2},{1,3},{2,0},{3,1},{4,6},{5,7},{6,4},{7,5},{8,10},{9,11},{10,... | collective-permute-start | bytes 2359304 | tf_op jit(solution)/shard_map/ppermute | solution.py:375
  146.6 26.0 %copy-start.7 = (f32[3072]{0:T(1024)S(1)}, f32[3072]{0:T(1024)}, u32[]{:S(2)}) copy-start(f32[3072]{0:T(1024)} %param.18) | copy-start | bytes 36868

commit v6 on v5

--- a/solution.py
+++ b/solution.py
@@ -15,10 +15,10 @@
 REACH = 2
 SPAN = 2 * REACH + 1
 EPSILON = 1e-06
-PROJECT_VMEM = 28 << 20
-ATTEND_VMEM = 14 << 20
+PROJECT_VMEM = 19 << 20
+ATTEND_VMEM = 11 << 20
 OUTPUT_VMEM = 53 << 20
-SMALL_VMEM = 14 << 20
+SMALL_VMEM = 11 << 20
 
 f32 = jnp.float32
 bf16 = jnp.bfloat16
@@ -347,21 +347,18 @@
     outs = (kept > 0) + (sent > 0)
     attended_refs = refs[:total]
     weight_refs = refs[total:-outs]
-    rows = weight_refs[0].shape[0] // 2
+    rows = weight_refs[0].shape[0]
     for index, weight_ref in enumerate(weight_refs):
-        first = held_ref[index]
-
-        @pl.when(first >= 0)
-        def _(first=first, weight_ref=weight_ref):
+
+        @pl.when(held_ref[index] >= 0)
+        def _(index=index, weight_ref=weight_ref):
             attended = jnp.concatenate([ref[...] for ref in attended_refs], axis=0)
             product = ntdot(attended, weight_ref[...])
-            for half in range(2):
-                columns = pl.ds(pl.multiple_of((first ^ half) * rows, 128), rows)
-                piece = product[:, half * rows : (half + 1) * rows]
-                if kept:
-                    refs[-outs][:, columns] = piece[: kept * QB]
-                if sent:
-                    refs[-1][:, columns] = piece[kept * QB :].astype(bf16)
+            columns = pl.ds(pl.multiple_of(held_ref[index] * rows, 128), rows)
+            if kept:
+                refs[-outs][:, columns] = product[: kept * QB]
+            if sent:
+                refs[-1][:, columns] = product[kept * QB :].astype(bf16)
 
 
 def final_kernel(own_ref, first_ref, second_ref, third_ref, gate_ref, out_ref):
@@ -382,12 +379,13 @@
 def gathered_rows(own):
     count = lax.axis_size("wide")
     index = lax.axis_index("wide")
-    other = flip(own, "wide", 1)
-    pair = jnp.concatenate([own, other], axis=0)
-    blocks, held = [pair], [index]
+    length = count // 2
+    blocks, held = [own], [index]
+    blocks.append(lax.ppermute(own, "wide", [(i, i ^ 1) for i in range(count)]))
+    held.append(index ^ 1)
     for sign in (1, -1):
-        current = pair
-        for step in range(1, count // 2):
+        current = own
+        for step in range(1, length):
             move = 2 * sign
             route = [
                 (i, i + move)
@@ -396,8 +394,12 @@
             ]
             current = lax.ppermute(current, "wide", route)
             source = index - move * step
+            valid = (source >= 0) & (source < count)
             blocks.append(current)
-            held.append(jnp.where((source >= 0) & (source < count), source, -1))
+            held.append(jnp.where(valid, source, -1))
+            swap = [(i, i ^ 1) for i in range(count) if 0 <= i - move * step < count]
+            blocks.append(lax.ppermute(current, "wide", swap))
+            held.append(jnp.where(valid, source ^ 1, -1))
     return blocks, jnp.stack(held).astype(jnp.int32)
 
 
@@ -454,7 +456,6 @@
         out_shape=prep_shapes,
         in_specs=[smem] + [whole_spec()] * 7,
         out_specs=tuple(whole_spec() for _ in prep_shapes),
-        compiler_params=small,
         cost_estimate=cost(1 << 28, 4 << 20),
         name="prep",
     )

time: 176 us -> 167 us (0.949)
  waiting for transfers between devices: 62.3 us -> 38.7 us
  starting transfers between devices: 33.8 us -> 46 us
  Pallas kernels: 60.6 us -> 67 us
  local copies, waits for them, and re-layouts: 11.2 us -> 5.39 us
    ppermute x6, waiting for transfers between devices: 22.6 us -> 3.56 us  [gathered_rows(): current = lax.ppermute(current, 'wide', route)]
    ppermute x8 -> x7, waiting for transfers between devices: 39.8 us -> 21.2 us  [flip(): return lax.ppermute(block, axis, [(i, i ^ bit) for i in devices])]
    ppermute x0 -> x7, starting transfers between devices: none -> 13.5 us  [the longest x6 12.4 us: gathered_rows(): blocks.append(lax.ppermute(current, 'wide', swap))]
    all_to_all x1, waiting for transfers between devices: 0.01 us -> 12.4 us  [block(): lax.all_to_all(payload, 'wide', split_axis=0, concat_axis=0, tiled=True)]
    unnamed x39 -> x24, local copies, waits for them, and re-layouts: 10.1 us -> 4.25 us
    pallas_call x4, Pallas kernels: 13.3 us -> 16.4 us  [multiply(): pl.pallas_call(functools.partial(partial_kernel, kept, sent), out_shape=t...]
    pallas_call x1, Pallas kernels: 1.83 us -> 3.63 us  [block(): prepare(first.astype(jnp.int32).reshape(1), embed_weight, own, scale, shi...]
    ppermute x8 -> x7, starting transfers between devices: 7.97 us -> 6.43 us  [flip(): return lax.ppermute(block, axis, [(i, i ^ bit) for i in devices])]
  transfers between devices with their start and end apart: 16 -> 22, of which waited for: 6 -> 5; matrix products, arithmetic and copies ran while one was open for 4% -> 5% of each run, Pallas kernels for 31% -> 35%
where the time goes in v6:
time: 167 us; the launch traced here: 165 us
  Pallas kernels  67 us (40%)
  starting transfers between devices  46 us (28%)
  waiting for transfers between devices  38.7 us (23%)
  other arithmetic  7.11 us (4%)
  local copies, waits for them, and re-layouts  5.39 us (3%)
    pallas_call x4, Pallas kernels, attend(): pl.pallas_call(functools.partial(attend_kernel, parts, entries), out_shap...  32.3 us
    ppermute x7, waiting for transfers between devices, flip(): return lax.ppermute(block, axis, [(i, i ^ bit) for i in devices])  21.2 us
    pallas_call x4, Pallas kernels, multiply(): pl.pallas_call(functools.partial(partial_kernel, kept, sent), out_shape=t...  16.4 us
    ppermute x6, starting transfers between devices, gathered_rows(): current = lax.ppermute(current, 'wide', route)  14.2 us
    ppermute x6, starting transfers between devices, gathered_rows(): blocks.append(lax.ppermute(current, 'wide', swap))  12.4 us
    all_to_all x1, waiting for transfers between devices, block(): lax.all_to_all(payload, 'wide', split_axis=0, concat_axis=0, tiled=True)  12.4 us
    pallas_call x1, Pallas kernels, block(): pl.pallas_call(functools.partial(project_kernel, row_total, tile_size), o...  11.1 us
    ppermute x7, starting transfers between devices, flip(): return lax.ppermute(block, axis, [(i, i ^ bit) for i in devices])  6.43 us
  transfers between devices with their start and end apart: 22, of which 5 were waited for; matrix products, arithmetic and copies ran while one was open for 5% of the time, Pallas kernels for 35%

profile of v6, /device:TPU:16, one launch (start us, length us, event | category | flops | bytes accessed | tf_op | source)
XLA Modules:
  0.0 164.6 jit_solution(103920142984037230)
XLA Ops:
  0.0 3.6 %prep.1 = bf16[8,384,128]{2,1,0:T(8,128)(2,1)} custom-call(s32[1]{0:T(128)} %bitcast.14.at_ref, bf16[128,3072]{1,0:T(8,128)(2,1)} %embed_ref.3, bf16[128,3072]{1,0:T(8,128)(2,1)} %embed_ref.3, f32[1,3072]{1,0:T(1,128)} %bitcast.31, f32[1,3072]{1,0:T(1,128)} %bitcast.32, bf16[3,384,512]{2,1,0:T(8,128)(2,1)} %qkv_ref.1, bf16[256,128]{1,0:T(8,128)(2,1)} %latents_ref.1, ...), custom_call_target="tpu_custom_call" | custom-call | flops 268435456 | bytes 4194304 | tf_op jit(solution)/shard_map/prep/pallas_call | solution.py:462
  3.6 6.3 %all-to-all-start = ((bf16[8,384,128]{2,1,0:T(8,128)(2,1)}), bf16[8,384,128]{2,1,0:T(8,128)(2,1)S(1)}, u32[]{:S(2)}, u32[]{:S(2)}) async-start(bf16[8,384,128]{2,1,0:T(8,128)(2,1)} %prep.1), calls=%async_computation | async-start | bytes 1572864 | tf_op jit(solution)/shard_map/all_to_all | solution.py:485
  9.9 2.5 %collective-permute-start.9 = (bf16[384,512]{1,0:T(8,128)(2,1)S(1)}, bf16[384,512]{1,0:T(8,128)(2,1)S(1)}, u32[]{:S(2)}, u32[]{:S(2)}) collective-permute-start(bf16[384,512]{1,0:T(8,128)(2,1)S(1)} %copy-done.1), channel_id=1, source_target_pairs={{8,0},{12,4},{16,8},{20,12},{24,16},{28,20},{9,1},{13,5},{17,9},{2... | collective-permute-start | bytes 1179656 | tf_op jit(solution)/shard_map/ppermute | solution.py:395
  12.4 3.4 %collective-permute-start.3 = (bf16[384,512]{1,0:T(8,128)(2,1)S(1)}, bf16[384,512]{1,0:T(8,128)(2,1)S(1)}, u32[]{:S(2)}, u32[]{:S(2)}) collective-permute-start(bf16[384,512]{1,0:T(8,128)(2,1)S(1)} %copy-done.1), channel_id=1, source_target_pairs={{0,8},{4,12},{8,16},{12,20},{16,24},{20,28},{1,9},{5,13},{9,17},{1... | collective-permute-start | bytes 1179656 | tf_op jit(solution)/shard_map/ppermute | solution.py:395
  15.8 12.4 %all-to-all-done = bf16[8,384,128]{2,1,0:T(8,128)(2,1)S(1)} async-done(((bf16[8,384,128]{2,1,0:T(8,128)(2,1)}), bf16[8,384,128]{2,1,0:T(8,128)(2,1)S(1)}, u32[]{:S(2)}, u32[]{:S(2)}) %all-to-all-start) | async-done | bytes 786464 | tf_op jit(solution)/shard_map/all_to_all | solution.py:485
  28.2 0.1 reshape_squeeze.3
  28.4 0.7 copy-done.8
  29.1 1.5 collective-permute-start
  30.6 1.1 collective-permute-start.2
  31.6 3.5 %collective-permute-done.9.refs_10_ = bf16[384,512]{1,0:T(8,128)(2,1)S(1)} collective-permute-done((bf16[384,512]{1,0:T(8,128)(2,1)S(1)}, bf16[384,512]{1,0:T(8,128)(2,1)S(1)}, u32[]{:S(2)}, u32[]{:S(2)}) %collective-permute-start.9) | collective-permute-done | bytes 393248 | tf_op jit(solution)/shard_map/ppermute | solution.py:395
  35.2 4.4 %collective-permute-start.11 = (bf16[384,512]{1,0:T(8,128)(2,1)S(1)}, bf16[384,512]{1,0:T(8,128)(2,1)S(1)}, u32[]{:S(2)}, u32[]{:S(2)}) collective-permute-start(bf16[384,512]{1,0:T(8,128)(2,1)S(1)} %collective-permute-done.9.refs_10_), channel_id=1, source_target_pairs={{8,0},{12,4},{16,8},{20,12},{9,1},{13,5},{17,9},{21,13},{10,2},{14... | collective-permute-start | bytes 1179656 | tf_op jit(solution)/shard_map/ppermute | solution.py:395
  39.6 1.9 %collective-permute-start.5 = (bf16[384,512]{1,0:T(8,128)(2,1)S(1)}, bf16[384,512]{1,0:T(8,128)(2,1)S(1)}, u32[]{:S(2)}, u32[]{:S(2)}) collective-permute-start(bf16[384,512]{1,0:T(8,128)(2,1)S(1)} %collective-permute-done.3.refs_4_), channel_id=1, source_target_pairs={{8,16},{12,20},{16,24},{20,28},{9,17},{13,21},{17,25},{21,29},{10,... | collective-permute-start | bytes 1179656 | tf_op jit(solution)/shard_map/ppermute | solution.py:395
  41.5 0.0 collective-permute-done
  41.5 1.9 %pad_maximum_fusion.1 = bf16[2,1296,128]{2,1,0:T(8,128)(2,1)} fusion(bf16[1,1296,128]{2,1,0:T(8,128)(2,1)} %collective-permute-done, bf16[1,1296,128]{2,1,0:T(8,128)(2,1)S(1)} %maximum_bitcast_fusion), kind=kLoop, calls=%fused_computation.3 | loop fusion | flops 331776 | bytes 1327104 | tf_op jit(solution)/shard_map/concatenate | solution.py:500
  43.4 0.0 collective-permute-start.1
  43.4 1.1 slice_reduce_fusion
  44.5 0.8 broadcast_in_dim.10
  45.3 5.6 %all-to-all-start.1 = ((bf16[8,192,128]{2,1,0:T(8,128)(2,1)}), bf16[8,192,128]{2,1,0:T(8,128)(2,1)}, u32[]{:S(2)}, u32[]{:S(2)}) async-start(bf16[8,192,128]{2,1,0:T(8,128)(2,1)} %broadcast_in_dim.10), calls=%async_computation.1 | async-start | bytes 786432 | tf_op jit(solution)/shard_map/all_to_all | solution.py:502
  50.9 1.7 %gram.1.gram_ref = bf16[3,128,128]{2,1,0:T(8,128)(2,1)S(1)} custom-call(bf16[128,3072]{1,0:T(8,128)(2,1)S(1)} %copy-done), custom_call_target="tpu_custom_call" | custom-call | tf_op jit(solution)/shard_map/gram/pallas_call | solution.py:477
  52.6 0.6 copy-done.3
  53.3 3.4 %collective-permute-start.10 = (bf16[384,512]{1,0:T(8,128)(2,1)S(1)}, bf16[384,512]{1,0:T(8,128)(2,1)S(1)}, u32[]{:S(2)}, u32[]{:S(2)}) collective-permute-start(bf16[384,512]{1,0:T(8,128)(2,1)S(1)} %collective-permute-done.9.refs_10_), channel_id=1, source_target_pairs={{0,4},{4,0},{8,12},{12,8},{16,20},{20,16},{1,5},{5,1},{9,13},{13,9... | collective-permute-start | bytes 1179656 | tf_op jit(solution)/shard_map/ppermute | solution.py:401
  56.6 0.0 collective-permute-done.11.refs_12_
  56.6 0.7 collective-permute-start.13
  57.3 1.3 collective-permute-start.7
  58.7 0.1 reshape.31.starts_ref
  58.8 0.1 stack.59.held_ref
  58.9 1.4 convert_reduce_fusion.bias_ref
  60.3 0.0 collective-permute-done.1
  60.3 2.8 %collective-permute-start.4 = (bf16[384,512]{1,0:T(8,128)(2,1)S(1)}, bf16[384,512]{1,0:T(8,128)(2,1)}, u32[]{:S(2)}, u32[]{:S(2)}) collective-permute-start(bf16[384,512]{1,0:T(8,128)(2,1)S(1)} %collective-permute-done.3.refs_4_), channel_id=1, source_target_pairs={{8,12},{12,8},{16,20},{20,16},{24,28},{28,24},{9,13},{13,9},{17,21... | collective-permute-start | bytes 1179656 | tf_op jit(solution)/shard_map/ppermute | solution.py:401
  63.0 2.5 %pad_maximum_fusion.patches_ref = bf16[4,1296,128]{2,1,0:T(8,128)(2,1)} fusion(bf16[2,1296,128]{2,1,0:T(8,128)(2,1)} %collective-permute-done.1, bf16[1,1296,128]{2,1,0:T(8,128)(2,1)} %collective-permute-done, bf16[1,1296,128]{2,1,0:T(8,128)(2,1)} %copy-done.9), kind=kLoop, calls=%fused_computation.2 | loop fusion | flops 1327104 | bytes 2654208 | tf_op jit(solution)/shard_map/concatenate | solution.py:500
  65.5 0.0 collective-permute-done.2.refs_3_
  65.5 1.4 collective-permute-start.12
  66.9 1.5 collective-permute-done.10.refs_11_
  68.4 2.1 %collective-permute-start.6 = (bf16[384,512]{1,0:T(8,128)(2,1)S(1)}, bf16[384,512]{1,0:T(8,128)(2,1)}, u32[]{:S(2)}, u32[]{:S(2)}) collective-permute-start(bf16[384,512]{1,0:T(8,128)(2,1)S(1)} %collective-permute-done.5.refs_6_), channel_id=1, source_target_pairs={{16,20},{20,16},{24,28},{28,24},{17,21},{21,17},{25,29},{29,25},{1... | collective-permute-start | bytes 1179656 | tf_op jit(solution)/shard_map/ppermute | solution.py:401
  70.5 1.4 collective-permute-start.14
  71.9 1.4 collective-permute-start.8
  73.4 0.0 all-to-all-done.1
  73.4 1.3 copy-done.2
  74.7 0.9 copy-done.4
  75.6 0.7 copy-done.7
  76.3 11.1 %project.1 = (bf16[512,5120]{1,0:T(8,128)(2,1)S(1)}, bf16[5120,512]{1,0:T(8,128)(2,1)S(1)}, bf16[8,4,256,128]{3,2,1,0:T(8,128)(2,1)S(1)}) custom-call(s32[4]{0:T(128)S(1)} %broadcast_xor_fusion.order_ref, bf16[4,1296,128]{2,1,0:T(8,128)(2,1)S(1)} %copy-done.2, bf16[1536,128]{1,0:T(8,128)(2,1)} %bitcast.23.weight_ref, f32[16,128]{1,0:T(8,128)S(1)} %copy-done.7, ...), custom_call_target="tpu_custom_call" | custom-call | flops 3355443200 | bytes 16777216 | tf_op jit(solution)/shard_map/project/pallas_call | solution.py:509
  87.4 9.0 %shard_map.113 = (bf16[128,512]{1,0:T(8,128)(2,1)S(1)}, bf16[128,512]{1,0:T(8,128)(2,1)S(1)}) custom-call(s32[4]{0:T(128)S(1)} %broadcast_xor_fusion.order_ref, s32[64]{0:T(128)S(1)} %reshape.31.starts_ref, s32[8]{0:T(128)S(1)} %copy-done.6, bf16[512,5120]{1,0:T(8,128)(2,1)S(1)} %get-tuple-element.20.keys_ref, ...), custom_call_target="tpu_custom_call" | custom-call | flops 2147483648 | bytes 16777216 | tf_op jit(solution)/shard_map/pallas_call | solution.py:525
  96.4 0.0 collective-permute-done.4.refs_5_
  96.5 0.0 collective-permute-done.14.refs_15_
  96.5 0.0 collective-permute-done.8.refs_9_
  96.5 4.1 %shard_map.114 = (f32[128,3072]{1,0:T(8,128)S(1)}, bf16[128,3072]{1,0:T(8,128)(2,1)S(1)}) custom-call(s32[14]{0:T(128)S(1)} %stack.59.held_ref, bf16[128,512]{1,0:T(8,128)(2,1)S(1)} %get-tuple-element.27.refs_0_, bf16[128,512]{1,0:T(8,128)(2,1)S(1)} %get-tuple-element.28.refs_1_, bf16[384,512]{1,0:T(8,128)(2,1)S(1)} %copy-done.1, ...), custom_call_target="tpu_custom_call" | custom-call | flops 805306368 | bytes 8388608 | tf_op jit(solution)/shard_map/pallas_call | solution.py:545
  100.6 0.1 collective-permute-start.16
  100.7 6.6 %shard_map.115 = (bf16[128,512]{1,0:T(8,128)(2,1)S(1)}, bf16[128,512]{1,0:T(8,128)(2,1)S(1)}) custom-call(s32[4]{0:T(128)S(1)} %broadcast_xor_fusion.order_ref, s32[64]{0:T(128)S(1)} %reshape.31.starts_ref, s32[8]{0:T(128)S(1)} %copy-done.6, bf16[512,5120]{1,0:T(8,128)(2,1)S(1)} %get-tuple-element.20.keys_ref, ...), custom_call_target="tpu_custom_call" | custom-call | flops 2147483648 | bytes 16777216 | tf_op jit(solution)/shard_map/pallas_call | solution.py:525
  107.3 4.1 %shard_map.116 = (f32[128,3072]{1,0:T(8,128)S(1)}, bf16[128,3072]{1,0:T(8,128)(2,1)S(1)}) custom-call(s32[14]{0:T(128)S(1)} %stack.59.held_ref, bf16[128,512]{1,0:T(8,128)(2,1)S(1)} %get-tuple-element.31.refs_0_, bf16[128,512]{1,0:T(8,128)(2,1)S(1)} %get-tuple-element.32.refs_1_, bf16[384,512]{1,0:T(8,128)(2,1)S(1)} %copy-done.1, ...), custom_call_target="tpu_custom_call" | custom-call | flops 805306368 | bytes 8388608 | tf_op jit(solution)/shard_map/pallas_call | solution.py:545
  111.4 0.6 collective-permute-start.18
  112.0 7.7 %shard_map.111 = (bf16[128,512]{1,0:T(8,128)(2,1)S(1)}, bf16[128,512]{1,0:T(8,128)(2,1)S(1)}) custom-call(s32[4]{0:T(128)S(1)} %broadcast_xor_fusion.order_ref, s32[64]{0:T(128)S(1)} %reshape.31.starts_ref, s32[8]{0:T(128)S(1)} %copy-done.6, bf16[512,5120]{1,0:T(8,128)(2,1)S(1)} %get-tuple-element.20.keys_ref, ...), custom_call_target="tpu_custom_call" | custom-call | flops 2147483648 | bytes 16777216 | tf_op jit(solution)/shard_map/pallas_call | solution.py:525
  119.7 4.1 %shard_map.112 = bf16[256,3072]{1,0:T(8,128)(2,1)S(1)} custom-call(s32[14]{0:T(128)S(1)} %stack.59.held_ref, bf16[128,512]{1,0:T(8,128)(2,1)S(1)} %get-tuple-element.25.refs_0_, bf16[128,512]{1,0:T(8,128)(2,1)S(1)} %get-tuple-element.26.refs_1_, bf16[384,512]{1,0:T(8,128)(2,1)S(1)} %copy-done.1, bf16[384,512]{1,0:T(8,128)(2,1)S(1)} %collective-permute-done.2.refs_3_, ...), custom_call_target="tpu_custom_call" | custom-call | flops 805306368 | bytes 8388608 | tf_op jit(solution)/shard_map/pallas_call | solution.py:545
  123.8 1.4 collective-permute-start.15
  125.2 0.2 add_convert_fusion.1
  125.3 2.8 %collective-permute-start.17 = (bf16[128,3072]{1,0:T(8,128)(2,1)S(1)}, bf16[128,3072]{1,0:T(8,128)(2,1)S(1)}, u32[]{:S(2)}, u32[]{:S(2)}) collective-permute-start(bf16[128,3072]{1,0:T(8,128)(2,1)S(1)} %add_convert_fusion.1), channel_id=1, source_target_pairs={{0,2},{1,3},{2,0},{3,1},{4,6},{5,7},{6,4},{7,5},{8,10},{9,11},{10,... | collective-permute-start | bytes 2359304 | tf_op jit(solution)/shard_map/ppermute | solution.py:372
  128.2 0.0 collective-permute-done.18
  128.2 0.2 add_convert_fusion
  128.3 0.1 collective-permute-start.19
  128.4 9.0 %shard_map.109 = (bf16[128,512]{1,0:T(8,128)(2,1)S(1)}, bf16[128,512]{1,0:T(8,128)(2,1)S(1)}) custom-call(s32[4]{0:T(128)S(1)} %broadcast_xor_fusion.order_ref, s32[64]{0:T(128)S(1)} %reshape.31.starts_ref, s32[8]{0:T(128)S(1)} %copy-done.6, bf16[512,5120]{1,0:T(8,128)(2,1)S(1)} %get-tuple-element.20.keys_ref, ...), custom_call_target="tpu_custom_call" | custom-call | flops 2147483648 | bytes 16777216 | tf_op jit(solution)/shard_map/pallas_call | solution.py:525
  137.4 0.0 copy-start.5
  137.4 4.1 %shard_map.110.own_ref = f32[256,3072]{1,0:T(8,128)S(1)} custom-call(s32[14]{0:T(128)S(1)} %stack.59.held_ref, bf16[128,512]{1,0:T(8,128)(2,1)S(1)} %get-tuple-element.23.refs_0_, bf16[128,512]{1,0:T(8,128)(2,1)S(1)} %get-tuple-element.24.refs_1_, bf16[384,512]{1,0:T(8,128)(2,1)S(1)} %copy-done.1, bf16[384,512]{1,0:T(8,128)(2,1)S(1)} %collective-permute-done.2.refs_3_, ...), custom_call_target="tpu_custom_call" | custom-call | flops 805306368 | bytes 8388608 | tf_op jit(solution)/shard_map/pallas_call | solution.py:545
  141.5 5.0 %collective-permute-done.17.second_ref = bf16[128,3072]{1,0:T(8,128)(2,1)S(1)} collective-permute-done((bf16[128,3072]{1,0:T(8,128)(2,1)S(1)}, bf16[128,3072]{1,0:T(8,128)(2,1)S(1)}, u32[]{:S(2)}, u32[]{:S(2)}) %collective-permute-start.17) | collective-permute-done | bytes 786464 | tf_op jit(solution)/shard_map/ppermute | solution.py:372
  146.5 16.2 %collective-permute-done.19.third_ref = bf16[128,3072]{1,0:T(8,128)(2,1)S(1)} collective-permute-done((bf16[128,3072]{1,0:T(8,128)(2,1)S(1)}, bf16[128,3072]{1,0:T(8,128)(2,1)S(1)}, u32[]{:S(2)}, u32[]{:S(2)}) %collective-permute-start.19) | collective-permute-done | bytes 786464 | tf_op jit(solution)/shard_map/ppermute | solution.py:372
  162.7 1.8 %final.1 = bf16[256,3072]{1,0:T(8,128)(2,1)} custom-call(f32[256,3072]{1,0:T(8,128)S(1)} %shard_map.110.own_ref, bf16[256,3072]{1,0:T(8,128)(2,1)S(1)} %collective-permute-done.15.first_ref, bf16[128,3072]{1,0:T(8,128)(2,1)S(1)} %collective-permute-done.17.second_ref, bf16[128,3072]{1,0:T(8,128)(2,1)S(1)} %collective-permute-done.19.third_ref, ...), custom_call_target="tpu_custom_call" | custom-call | tf_op jit(solution)/shard_map/final/pallas_call | solution.py:564
  (33 shorter events, 0.2 us)
Async XLA Ops:
  3.6 6.3 %copy-start.1 = (bf16[384,512]{1,0:T(8,128)(2,1)S(1)}, bf16[384,512]{1,0:T(8,128)(2,1)}, u32[]{:S(2)}) copy-start(bf16[384,512]{1,0:T(8,128)(2,1)} %refs_2_.7) | copy-start | bytes 1179652
  3.6 24.6 %all-to-all-start = ((bf16[8,384,128]{2,1,0:T(8,128)(2,1)}), bf16[8,384,128]{2,1,0:T(8,128)(2,1)S(1)}, u32[]{:S(2)}, u32[]{:S(2)}) async-start(bf16[8,384,128]{2,1,0:T(8,128)(2,1)} %prep.1), calls=%async_computation | async-start | bytes 1572864 | tf_op jit(solution)/shard_map/all_to_all | solution.py:485
  9.9 25.2 %collective-permute-start.9 = (bf16[384,512]{1,0:T(8,128)(2,1)S(1)}, bf16[384,512]{1,0:T(8,128)(2,1)S(1)}, u32[]{:S(2)}, u32[]{:S(2)}) collective-permute-start(bf16[384,512]{1,0:T(8,128)(2,1)S(1)} %copy-done.1), channel_id=1, source_target_pairs={{8,0},{12,4},{16,8},{20,12},{24,16},{28,20},{9,1},{13,5},{17,9},{2... | collective-permute-start | bytes 1179656 | tf_op jit(solution)/shard_map/ppermute | solution.py:395
  12.4 27.2 %collective-permute-start.3 = (bf16[384,512]{1,0:T(8,128)(2,1)S(1)}, bf16[384,512]{1,0:T(8,128)(2,1)S(1)}, u32[]{:S(2)}, u32[]{:S(2)}) collective-permute-start(bf16[384,512]{1,0:T(8,128)(2,1)S(1)} %copy-done.1), channel_id=1, source_target_pairs={{0,8},{4,12},{8,16},{12,20},{16,24},{20,28},{1,9},{5,13},{9,17},{1... | collective-permute-start | bytes 1179656 | tf_op jit(solution)/shard_map/ppermute | solution.py:395
  28.2 0.9 copy-start.8
  29.1 23.5 %copy-start.9 = (bf16[1,1296,128]{2,1,0:T(8,128)(2,1)}, bf16[1,1296,128]{2,1,0:T(8,128)(2,1)S(1)}, u32[]{:S(2)}) copy-start(bf16[1,1296,128]{2,1,0:T(8,128)(2,1)S(1)} %maximum_bitcast_fusion) | copy-start | bytes 995332
  29.1 21.8 %copy-start.11 = (s32[4]{0:T(128)S(1)}, s32[4]{0:T(128)}, u32[]{:S(2)}) copy-start(s32[4]{0:T(128)} %constant.48.clone) | copy-start | bytes 52
  29.1 21.8 %copy-start = (bf16[128,3072]{1,0:T(8,128)(2,1)S(1)}, bf16[128,3072]{1,0:T(8,128)(2,1)}, u32[]{:S(2)}) copy-start(bf16[128,3072]{1,0:T(8,128)(2,1)} %embed_ref.3) | copy-start | bytes 2359300
  29.1 12.4 %collective-permute-start = (bf16[1,1296,128]{2,1,0:T(8,128)(2,1)S(1)}, bf16[1,1296,128]{2,1,0:T(8,128)(2,1)}, u32[]{:S(2)}, u32[]{:S(2)}) collective-permute-start(bf16[1,1296,128]{2,1,0:T(8,128)(2,1)S(1)} %maximum_bitcast_fusion), channel_id=1, source_target_pairs={{0,2},{1,3},{2,0},{3,1},{4,6},{5,7},{6,4},{7,5},{8,10},{9,11},{10,... | collective-permute-start | bytes 995336 | tf_op jit(solution)/shard_map/ppermute | solution.py:372
  30.6 34.9 %collective-permute-start.2 = (bf16[384,512]{1,0:T(8,128)(2,1)S(1)}, bf16[384,512]{1,0:T(8,128)(2,1)S(1)}, u32[]{:S(2)}, u32[]{:S(2)}) collective-permute-start(bf16[384,512]{1,0:T(8,128)(2,1)S(1)} %copy-done.1), channel_id=1, source_target_pairs={{0,4},{4,0},{8,12},{12,8},{16,20},{20,16},{24,28},{28,24},{1,5},{5... | collective-permute-start | bytes 1179656 | tf_op jit(solution)/shard_map/ppermute | solution.py:384
  35.2 21.5 %collective-permute-start.11 = (bf16[384,512]{1,0:T(8,128)(2,1)S(1)}, bf16[384,512]{1,0:T(8,128)(2,1)S(1)}, u32[]{:S(2)}, u32[]{:S(2)}) collective-permute-start(bf16[384,512]{1,0:T(8,128)(2,1)S(1)} %collective-permute-done.9.refs_10_), channel_id=1, source_target_pairs={{8,0},{12,4},{16,8},{20,12},{9,1},{13,5},{17,9},{21,13},{10,2},{14... | collective-permute-start | bytes 1179656 | tf_op jit(solution)/shard_map/ppermute | solution.py:395
  39.6 17.8 %collective-permute-start.5 = (bf16[384,512]{1,0:T(8,128)(2,1)S(1)}, bf16[384,512]{1,0:T(8,128)(2,1)S(1)}, u32[]{:S(2)}, u32[]{:S(2)}) collective-permute-start(bf16[384,512]{1,0:T(8,128)(2,1)S(1)} %collective-permute-done.3.refs_4_), channel_id=1, source_target_pairs={{8,16},{12,20},{16,24},{20,28},{9,17},{13,21},{17,25},{21,29},{10,... | collective-permute-start | bytes 1179656 | tf_op jit(solution)/shard_map/ppermute | solution.py:395
  43.4 9.9 %copy-start.10 = (s32[8,8]{1,0:T(8,128)S(1)}, s32[8,8]{1,0:T(8,128)}, u32[]{:S(2)}) copy-start(s32[8,8]{1,0:T(8,128)} %param.19) | copy-start | bytes 772
  43.4 16.9 %collective-permute-start.1 = (bf16[2,1296,128]{2,1,0:T(8,128)(2,1)}, bf16[2,1296,128]{2,1,0:T(8,128)(2,1)}, u32[]{:S(2)}, u32[]{:S(2)}) collective-permute-start(bf16[2,1296,128]{2,1,0:T(8,128)(2,1)} %pad_maximum_fusion.1), channel_id=1, source_target_pairs={{0,1},{1,0},{2,3},{3,2},{4,5},{5,4},{6,7},{7,6},{8,9},{9,8},{10,11... | collective-permute-start | bytes 1990664 | tf_op jit(solution)/shard_map/ppermute | solution.py:372
  45.3 28.1 %all-to-all-start.1 = ((bf16[8,192,128]{2,1,0:T(8,128)(2,1)}), bf16[8,192,128]{2,1,0:T(8,128)(2,1)}, u32[]{:S(2)}, u32[]{:S(2)}) async-start(bf16[8,192,128]{2,1,0:T(8,128)(2,1)} %broadcast_in_dim.10), calls=%async_computation.1 | async-start | bytes 786432 | tf_op jit(solution)/shard_map/all_to_all | solution.py:502
  52.6 0.7 copy-start.3
  53.3 15.2 %collective-permute-start.10 = (bf16[384,512]{1,0:T(8,128)(2,1)S(1)}, bf16[384,512]{1,0:T(8,128)(2,1)S(1)}, u32[]{:S(2)}, u32[]{:S(2)}) collective-permute-start(bf16[384,512]{1,0:T(8,128)(2,1)S(1)} %collective-permute-done.9.refs_10_), channel_id=1, source_target_pairs={{0,4},{4,0},{8,12},{12,8},{16,20},{20,16},{1,5},{5,1},{9,13},{13,9... | collective-permute-start | bytes 1179656 | tf_op jit(solution)/shard_map/ppermute | solution.py:401
  56.6 13.9 %collective-permute-start.13 = (bf16[384,512]{1,0:T(8,128)(2,1)S(1)}, bf16[384,512]{1,0:T(8,128)(2,1)S(1)}, u32[]{:S(2)}, u32[]{:S(2)}) collective-permute-start(bf16[384,512]{1,0:T(8,128)(2,1)S(1)} %collective-permute-done.11.refs_12_), channel_id=1, source_target_pairs={{8,0},{12,4},{9,1},{13,5},{10,2},{14,6},{11,3},{15,7}} | collective-permute-start | bytes 1179656 | tf_op jit(solution)/shard_map/ppermute | solution.py:395
  57.3 14.6 %collective-permute-start.7 = (bf16[384,512]{1,0:T(8,128)(2,1)S(1)}, bf16[384,512]{1,0:T(8,128)(2,1)S(1)}, u32[]{:S(2)}, u32[]{:S(2)}) collective-permute-start(bf16[384,512]{1,0:T(8,128)(2,1)S(1)} %collective-permute-done.5.refs_6_), channel_id=1, source_target_pairs={{16,24},{20,28},{17,25},{21,29},{18,26},{22,30},{19,27},{23,31}} | collective-permute-start | bytes 1179656 | tf_op jit(solution)/shard_map/ppermute | solution.py:395
  60.3 36.2 %collective-permute-start.4 = (bf16[384,512]{1,0:T(8,128)(2,1)S(1)}, bf16[384,512]{1,0:T(8,128)(2,1)}, u32[]{:S(2)}, u32[]{:S(2)}) collective-permute-start(bf16[384,512]{1,0:T(8,128)(2,1)S(1)} %collective-permute-done.3.refs_4_), channel_id=1, source_target_pairs={{8,12},{12,8},{16,20},{20,16},{24,28},{28,24},{9,13},{13,9},{17,21... | collective-permute-start | bytes 1179656 | tf_op jit(solution)/shard_map/ppermute | solution.py:401
  65.5 30.9 %collective-permute-start.12 = (bf16[384,512]{1,0:T(8,128)(2,1)S(1)}, bf16[384,512]{1,0:T(8,128)(2,1)}, u32[]{:S(2)}, u32[]{:S(2)}) collective-permute-start(bf16[384,512]{1,0:T(8,128)(2,1)S(1)} %collective-permute-done.11.refs_12_), channel_id=1, source_target_pairs={{0,4},{4,0},{8,12},{12,8},{1,5},{5,1},{9,13},{13,9},{2,6},{6,2},{1... | collective-permute-start | bytes 1179656 | tf_op jit(solution)/shard_map/ppermute | solution.py:401
  68.4 28.0 %collective-permute-start.6 = (bf16[384,512]{1,0:T(8,128)(2,1)S(1)}, bf16[384,512]{1,0:T(8,128)(2,1)}, u32[]{:S(2)}, u32[]{:S(2)}) collective-permute-start(bf16[384,512]{1,0:T(8,128)(2,1)S(1)} %collective-permute-done.5.refs_6_), channel_id=1, source_target_pairs={{16,20},{20,16},{24,28},{28,24},{17,21},{21,17},{25,29},{29,25},{1... | collective-permute-start | bytes 1179656 | tf_op jit(solution)/shard_map/ppermute | solution.py:401
  70.5 25.9 %collective-permute-start.14 = (bf16[384,512]{1,0:T(8,128)(2,1)S(1)}, bf16[384,512]{1,0:T(8,128)(2,1)}, u32[]{:S(2)}, u32[]{:S(2)}) collective-permute-start(bf16[384,512]{1,0:T(8,128)(2,1)S(1)} %collective-permute-done.13.refs_14_), channel_id=1, source_target_pairs={{0,4},{4,0},{1,5},{5,1},{2,6},{6,2},{3,7},{7,3}} | collective-permute-start | bytes 1179656 | tf_op jit(solution)/shard_map/ppermute | solution.py:401
  71.9 24.5 %collective-permute-start.8 = (bf16[384,512]{1,0:T(8,128)(2,1)S(1)}, bf16[384,512]{1,0:T(8,128)(2,1)}, u32[]{:S(2)}, u32[]{:S(2)}) collective-permute-start(bf16[384,512]{1,0:T(8,128)(2,1)S(1)} %collective-permute-done.7.refs_8_), channel_id=1, source_target_pairs={{24,28},{28,24},{25,29},{29,25},{26,30},{30,26},{27,31},{31,27}} | collective-permute-start | bytes 1179656 | tf_op jit(solution)/shard_map/ppermute | solution.py:401
  73.4 1.3 copy-start.2
  74.7 0.9 copy-start.4
  75.6 0.7 copy-start.7
  76.3 11.1 %copy-start.6 = (s32[8]{0:T(128)S(1)}, s32[8]{0:T(128)}, u32[]{:S(2)}) copy-start(s32[8]{0:T(128)} %counts_ref.7) | copy-start | bytes 100
  100.6 24.6 %collective-permute-start.16 = (bf16[128,3072]{1,0:T(8,128)(2,1)S(1)}, bf16[128,3072]{1,0:T(8,128)(2,1)S(1)}, u32[]{:S(2)}, u32[]{:S(2)}) collective-permute-start(bf16[128,3072]{1,0:T(8,128)(2,1)S(1)} %get-tuple-element.30), channel_id=1, source_target_pairs={{0,1},{1,0},{2,3},{3,2},{4,5},{5,4},{6,7},{7,6},{8,9},{9,8},{10,11... | collective-permute-start | bytes 2359304 | tf_op jit(solution)/shard_map/ppermute | solution.py:372
  111.4 16.8 %collective-permute-start.18 = (bf16[128,3072]{1,0:T(8,128)(2,1)S(1)}, bf16[128,3072]{1,0:T(8,128)(2,1)S(1)}, u32[]{:S(2)}, u32[]{:S(2)}) collective-permute-start(bf16[128,3072]{1,0:T(8,128)(2,1)S(1)} %get-tuple-element.34), channel_id=1, source_target_pairs={{0,1},{1,0},{2,3},{3,2},{4,5},{5,4},{6,7},{7,6},{8,9},{9,8},{10,11... | collective-permute-start | bytes 2359304 | tf_op jit(solution)/shard_map/ppermute | solution.py:372
  123.8 17.8 %collective-permute-start.15 = (bf16[256,3072]{1,0:T(8,128)(2,1)S(1)}, bf16[256,3072]{1,0:T(8,128)(2,1)S(1)}, u32[]{:S(2)}, u32[]{:S(2)}) collective-permute-start(bf16[256,3072]{1,0:T(8,128)(2,1)S(1)} %shard_map.112), channel_id=1, source_target_pairs={{0,1},{1,0},{2,3},{3,2},{4,5},{5,4},{6,7},{7,6},{8,9},{9,8},{10,11... | collective-permute-start | bytes 4718600 | tf_op jit(solution)/shard_map/ppermute | solution.py:372
  125.3 21.2 %collective-permute-start.17 = (bf16[128,3072]{1,0:T(8,128)(2,1)S(1)}, bf16[128,3072]{1,0:T(8,128)(2,1)S(1)}, u32[]{:S(2)}, u32[]{:S(2)}) collective-permute-start(bf16[128,3072]{1,0:T(8,128)(2,1)S(1)} %add_convert_fusion.1), channel_id=1, source_target_pairs={{0,2},{1,3},{2,0},{3,1},{4,6},{5,7},{6,4},{7,5},{8,10},{9,11},{10,... | collective-permute-start | bytes 2359304 | tf_op jit(solution)/shard_map/ppermute | solution.py:372
  128.3 34.4 %collective-permute-start.19 = (bf16[128,3072]{1,0:T(8,128)(2,1)S(1)}, bf16[128,3072]{1,0:T(8,128)(2,1)S(1)}, u32[]{:S(2)}, u32[]{:S(2)}) collective-permute-start(bf16[128,3072]{1,0:T(8,128)(2,1)S(1)} %add_convert_fusion), channel_id=1, source_target_pairs={{0,2},{1,3},{2,0},{3,1},{4,6},{5,7},{6,4},{7,5},{8,10},{9,11},{10,... | collective-permute-start | bytes 2359304 | tf_op jit(solution)/shard_map/ppermute | solution.py:372
  137.4 25.3 %copy-start.5 = (f32[3072]{0:T(1024)S(1)}, f32[3072]{0:T(1024)}, u32[]{:S(2)}) copy-start(f32[3072]{0:T(1024)} %param.18) | copy-start | bytes 36868

commit v7 on v6

--- a/solution.py
+++ b/solution.py
@@ -117,14 +117,21 @@
     count = -(-SPAN * share // 16) * 16
     latents = latents_ref[...]
     wanted = lax.broadcasted_iota(jnp.int32, (count, row_total), 0)
+    spot_rows = -(-row_total // 128)
     lane = lax.broadcasted_iota(jnp.int32, (row_total, 128), 1)
     for receiver in range(wide_count):
         first = (receiver - REACH) * share
         chosen = (slot_across == (wanted + first).astype(f32)) & (wanted < SPAN * share)
         rows = jnp.dot(chosen.astype(bf16), latents, preferred_element_type=f32).astype(bf16)
-        mine = (slot_down == (lane + receiver * share).astype(f32)) & (lane < share)
-        spots = jnp.sum(jnp.where(mine, local, 0.0), axis=0, keepdims=True)
-        spots = jnp.broadcast_to(spots, (16, 128)).astype(bf16)
+        lines = []
+        for line in range(spot_rows):
+            place = lane + (line * 128 - at_ref[1])
+            mine = (slot_down == (place + receiver * share).astype(f32)) & (
+                (place >= 0) & (place < share)
+            )
+            lines.append(jnp.sum(jnp.where(mine, local, 0.0), axis=0, keepdims=True))
+        lines.append(jnp.zeros((16 - spot_rows, 128), f32))
+        spots = jnp.concatenate(lines, axis=0).astype(bf16)
         if sliced:
             out_refs[1][receiver, 0:16, :] = bias
             out_refs[1][receiver, 16 : 16 + count, :] = rows
@@ -135,23 +142,44 @@
             out_refs[0][receiver, piece + 16 + count :, :] = spots
 
 
+def middle_kernel(piece, count, arrived_ref, spread_ref, near_ref, bias_ref):
+    senders = arrived_ref.shape[0]
+    row_total = (near_ref.shape[0] - 16) // SPAN
+    share = row_total // senders
+    total = arrived_ref[0, 0:piece].astype(f32)
+    for sender in range(1, senders):
+        total = total + arrived_ref[sender, 0:piece].astype(f32)
+    total = total.astype(bf16)
+    for receiver in range(senders):
+        spread_ref[receiver] = total
+    bias = arrived_ref[0, piece : piece + 16].astype(f32)
+    spots = arrived_ref[0, piece + 16 + count :].astype(f32)
+    for sender in range(1, senders):
+        bias = bias + arrived_ref[sender, piece : piece + 16].astype(f32)
+        spots = spots + arrived_ref[sender, piece + 16 + count :].astype(f32)
+    bias_ref[...] = bias
+    near_ref[SPAN * row_total :, :] = spots.astype(bf16)
+    for tile in range(SPAN):
+        for sender in range(senders):
+            near_ref[pl.ds(tile * row_total + sender * share, share), :] = arrived_ref[
+                sender, pl.ds(piece + 16 + tile * share, share), :
+            ]
+
+
 def project_kernel(
     row_total,
     tile_size,
     order_ref,
-    patches_ref,
     weight_ref,
     bias_ref,
     gram_ref,
-    keys_ref,
-    values_ref,
-    twin_ref,
-    both_ref,
+    *rest,
 ):
+    patches_refs = rest[:-4]
+    keys_ref, values_ref, twin_ref, both_ref = rest[-4:]
     heads_width = keys_ref.shape[0]
     local_heads = heads_width // HEAD
     pairs = heads_width // 128
-    narrow_count = tile_size // row_total
     chunks = heads_width // 128
 
     def doubled(part):
@@ -178,23 +206,24 @@
     gram_top = jnp.concatenate([gram_ref[0], gram_ref[1]], axis=0)
     gram_low = gram_ref[2]
 
-    def scale(step, carry):
-        block = step // SPAN
-        tile = step % SPAN
-        rows = patches_ref[block, pl.ds(pl.multiple_of(tile * row_total, row_total), row_total), :]
-        wide_rows = rows.astype(f32)
-        image = jnp.dot(
-            jnp.concatenate([rows, rows], axis=1), gram_top, preferred_element_type=f32
-        ) + jnp.dot(rows, gram_low, preferred_element_type=f32)
-        variance = jnp.sum(image * wide_rows, axis=1, keepdims=True)
-        scaled = wide_rows * lax.rsqrt(jnp.maximum(variance, 0.0) + EPSILON)
-        high = scaled.astype(bf16)
-        at = pl.multiple_of(tile * tile_size + order_ref[block] * row_total, row_total)
-        both_ref[pl.ds(at, row_total), 0:128] = high
-        both_ref[pl.ds(at, row_total), 128:256] = (scaled - high.astype(f32)).astype(bf16)
-        return carry
-
-    lax.fori_loop(0, SPAN * narrow_count, scale, 0, unroll=SPAN)
+    for block, patches_ref in enumerate(patches_refs):
+        place = order_ref[block] * row_total
+
+        def scale(tile, carry, patches_ref=patches_ref, place=place):
+            rows = patches_ref[pl.ds(pl.multiple_of(tile * row_total, row_total), row_total), :]
+            wide_rows = rows.astype(f32)
+            image = jnp.dot(
+                jnp.concatenate([rows, rows], axis=1), gram_top, preferred_element_type=f32
+            ) + jnp.dot(rows, gram_low, preferred_element_type=f32)
+            variance = jnp.sum(image * wide_rows, axis=1, keepdims=True)
+            scaled = wide_rows * lax.rsqrt(jnp.maximum(variance, 0.0) + EPSILON)
+            high = scaled.astype(bf16)
+            at = pl.multiple_of(tile * tile_size + place, row_total)
+            both_ref[pl.ds(at, row_total), 0:128] = high
+            both_ref[pl.ds(at, row_total), 128:256] = (scaled - high.astype(f32)).astype(bf16)
+            return carry
+
+        lax.fori_loop(0, SPAN, scale, 0, unroll=SPAN)
 
     key_bias = centred_bias(1)
     key_weight = doubled(1)
@@ -219,11 +248,11 @@
     left = lax.broadcasted_iota(jnp.int32, (QB, 128), 1) < HEAD
     spot_rows = row_total // 128
 
-    def ask(block, carry):
+    for block, patches_ref in enumerate(patches_refs):
         place = order_ref[block] * row_total
         spots = jnp.concatenate(
             [
-                patches_ref[block, SPAN * row_total + row : SPAN * row_total + row + 1, :]
+                patches_ref[SPAN * row_total + row : SPAN * row_total + row + 1, :]
                 for row in range(spot_rows)
             ],
             axis=1,
@@ -240,9 +269,6 @@
                 piece = rows[part * QB : (part + 1) * QB, pair * 128 : (pair + 1) * 128]
                 twin_ref[query, pair, 0:QB, :] = jnp.where(left, piece, jnp.zeros_like(piece))
                 twin_ref[query, pair, QB : 2 * QB, :] = jnp.where(left, jnp.zeros_like(piece), piece)
-        return carry
-
-    lax.fori_loop(0, narrow_count, ask, 0)
 
 
 def attend_kernel(
@@ -460,7 +486,7 @@
         name="prep",
     )
     prepared = prepare(
-        first.astype(jnp.int32).reshape(1),
+        jnp.stack([first, wide_index * share]).astype(jnp.int32),
         embed_weight,
         own,
         scale,
@@ -484,20 +510,32 @@
     )(embed_weight)
     arrived = lax.all_to_all(payload, "wide", split_axis=0, concat_axis=0, tiled=True)
 
-    summed = jnp.sum(arrived[:, :piece].astype(f32), axis=0).astype(bf16)
-    bias = jnp.sum(arrived[:, piece : piece + 16].astype(f32), axis=0)
-    spread = jnp.broadcast_to(summed[None], (wide_count,) + summed.shape)
-    near = arrived[:, piece + 16 : piece + 16 + SPAN * share]
-    near = near.reshape(wide_count, SPAN, share, patch).transpose(1, 0, 2, 3)
-    near = near.reshape(SPAN * row_total, patch)
-    mine = arrived[:, piece + 16 + count, :share].reshape(-1)
-    mine = jnp.pad(mine, (0, 16 * 128 - row_total)).reshape(16, 128)
-    group = jnp.concatenate([near, mine], axis=0)[None]
-    order = [0]
+    near_rows = SPAN * row_total + 16
+    if share % 16 == 0 and piece % 16 == 0:
+        spread, near, bias = pl.pallas_call(
+            functools.partial(middle_kernel, piece, count),
+            out_shape=(
+                jax.ShapeDtypeStruct((wide_count, piece, patch), bf16),
+                jax.ShapeDtypeStruct((near_rows, patch), bf16),
+                jax.ShapeDtypeStruct((16, 128), f32),
+            ),
+            in_specs=[whole_spec()],
+            out_specs=(whole_spec(),) * 3,
+            compiler_params=small,
+            name="middle",
+        )(arrived)
+    else:
+        summed = jnp.sum(arrived[:, :piece].astype(f32), axis=0).astype(bf16)
+        bias = jnp.sum(arrived[:, piece : piece + 16].astype(f32), axis=0)
+        spread = jnp.broadcast_to(summed[None], (wide_count,) + summed.shape)
+        near = arrived[:, piece + 16 : piece + 16 + SPAN * share]
+        near = near.reshape(wide_count, SPAN, share, patch).transpose(1, 0, 2, 3)
+        spots = jnp.sum(arrived[:, piece + 16 + count :].astype(f32), axis=0).astype(bf16)
+        near = jnp.concatenate([near.reshape(SPAN * row_total, patch), spots], axis=0)
+    group, order = [near], [0]
     bits = [1 << k for k in range(1, narrow_count.bit_length() - 1)] + [1]
     for bit in bits:
-        other = flip(group, "narrow", bit)
-        group = jnp.concatenate([group, other], axis=0)
+        group = group + [flip(rows, "narrow", bit) for rows in group]
         order = order + [index ^ bit for index in order]
     everything = lax.all_to_all(spread, "wide", split_axis=0, concat_axis=0, tiled=True)
     weight_all = everything.reshape(3 * heads_width, patch)
@@ -513,13 +551,13 @@
             pltpu.VMEM((SPAN * tile_size, heads_width), bf16),
             pltpu.VMEM((tile_size // QB, pairs, 2 * QB, 128), bf16),
         ),
-        in_specs=[smem] + [whole_spec()] * 4,
+        in_specs=[smem] + [whole_spec()] * (3 + narrow_count),
         out_specs=(whole_spec(),) * 3,
         scratch_shapes=[pltpu.VMEM((SPAN * tile_size, 256), bf16)],
         compiler_params=pltpu.CompilerParams(vmem_limit_bytes=PROJECT_VMEM),
         cost_estimate=cost(10 * SPAN * tile_size * patch * heads_width, 16 << 20),
         name="project",
-    )(order_ids, group, weight_all, bias, gram)
+    )(order_ids, weight_all, bias, gram, *group)
 
     def attend(entries):
         return pl.pallas_call(

time: 167 us -> 166 us (level)
  the two profiles are of different devices: /device:TPU:16 before, /device:TPU:0 now
where the time goes in v7:
time: 166 us
  Pallas kernels  63.2 us (38%)
  starting transfers between devices  53.7 us (32%)
  waiting for transfers between devices  44.6 us (27%)
  local copies, waits for them, and re-layouts  3.01 us (2%)
    pallas_call x4, Pallas kernels, attend(): pl.pallas_call(functools.partial(attend_kernel, parts, entries), out_shap...  27.6 us
    ppermute x8, waiting for transfers between devices, flip(): return lax.ppermute(block, axis, [(i, i ^ bit) for i in devices])  21 us
    ppermute x6, waiting for transfers between devices, gathered_rows(): current = lax.ppermute(current, 'wide', route)  19.2 us
    pallas_call x4, Pallas kernels, multiply(): pl.pallas_call(functools.partial(partial_kernel, kept, sent), out_shape=t...  16.8 us
    ppermute x6, starting transfers between devices, gathered_rows(): blocks.append(lax.ppermute(current, 'wide', swap))  13.3 us
    all_to_all x1, starting transfers between devices, block(): lax.all_to_all(spread, 'wide', split_axis=0, concat_axis=0, tiled=True)  10.9 us
    ppermute x6, starting transfers between devices, gathered_rows(): current = lax.ppermute(current, 'wide', route)  10.7 us
    ppermute x8, starting transfers between devices, flip(): return lax.ppermute(block, axis, [(i, i ^ bit) for i in devices])  9.89 us
  transfers between devices with their start and end apart: 23, of which 5 were waited for; matrix products, arithmetic and copies ran while one was open for 0% of the time, Pallas kernels for 32%

profile of v7, /device:TPU:0, one launch (start us, length us, event | category | flops | bytes accessed | tf_op | source)
XLA Modules:
  0.0 165.7 jit_solution(12388195960575549242)
XLA Ops:
  0.0 0.6 pad_add_fusion.at_ref
  0.6 3.7 %prep.1 = bf16[8,384,128]{2,1,0:T(8,128)(2,1)} custom-call(s32[2]{0:T(128)} %pad_add_fusion.at_ref, bf16[128,3072]{1,0:T(8,128)(2,1)} %embed_ref.3, bf16[128,3072]{1,0:T(8,128)(2,1)} %embed_ref.3, f32[1,3072]{1,0:T(1,128)} %bitcast.22, f32[1,3072]{1,0:T(1,128)} %bitcast.23, bf16[3,384,512]{2,1,0:T(8,128)(2,1)} %qkv_ref.1, bf16[256,128]{1,0:T(8,128)(2,1)} %latents_ref.1, ...), custom_call_target="tpu_custom_call" | custom-call | flops 268435456 | bytes 4194304 | tf_op jit(solution)/shard_map/prep/pallas_call | solution.py:488
  4.3 7.5 %all-to-all-start = ((bf16[8,384,128]{2,1,0:T(8,128)(2,1)}), bf16[8,384,128]{2,1,0:T(8,128)(2,1)}, u32[]{:S(2)}, u32[]{:S(2)}) async-start(bf16[8,384,128]{2,1,0:T(8,128)(2,1)} %prep.1), calls=%async_computation | async-start | bytes 1572864 | tf_op jit(solution)/shard_map/all_to_all | solution.py:511
  11.8 0.0 copy-start.9
  11.8 1.3 collective-permute-start.10
  13.1 4.7 %collective-permute-start.4 = (bf16[384,512]{1,0:T(8,128)(2,1)S(1)}, bf16[384,512]{1,0:T(8,128)(2,1)S(1)}, u32[]{:S(2)}, u32[]{:S(2)}) collective-permute-start(bf16[384,512]{1,0:T(8,128)(2,1)S(1)} %copy-done.1), channel_id=1, source_target_pairs={{0,8},{4,12},{8,16},{12,20},{16,24},{20,28},{1,9},{5,13},{9,17},{1... | collective-permute-start | bytes 1179656 | tf_op jit(solution)/shard_map/ppermute | solution.py:421
  17.8 17.4 %collective-permute-done.10.refs_10_ = bf16[384,512]{1,0:T(8,128)(2,1)S(1)} collective-permute-done((bf16[384,512]{1,0:T(8,128)(2,1)S(1)}, bf16[384,512]{1,0:T(8,128)(2,1)S(1)}, u32[]{:S(2)}, u32[]{:S(2)}) %collective-permute-start.10) | collective-permute-done | bytes 393248 | tf_op jit(solution)/shard_map/ppermute | solution.py:421
  35.3 1.3 collective-permute-start.12
  36.5 0.0 collective-permute-done.4.refs_4_
  36.6 0.7 collective-permute-start.6
  37.3 1.5 collective-permute-start.3
  38.7 0.0 all-to-all-done.arrived_ref
  38.7 2.1 %middle.1 = (bf16[8,192,128]{2,1,0:T(8,128)(2,1)}, bf16[1296,128]{1,0:T(8,128)(2,1)}, f32[16,128]{1,0:T(8,128)S(1)}) custom-call(bf16[8,384,128]{2,1,0:T(8,128)(2,1)} %all-to-all-done.arrived_ref), custom_call_target="tpu_custom_call" | custom-call | tf_op jit(solution)/shard_map/middle/pallas_call | solution.py:515
  40.8 0.6 copy-done.6
  41.4 1.5 collective-permute-start
  42.9 10.9 %all-to-all-start.1 = ((bf16[8,192,128]{2,1,0:T(8,128)(2,1)}), bf16[8,192,128]{2,1,0:T(8,128)(2,1)}, u32[]{:S(2)}, u32[]{:S(2)}) async-start(bf16[8,192,128]{2,1,0:T(8,128)(2,1)} %get-tuple-element.23), calls=%async_computation.1 | async-start | bytes 786432 | tf_op jit(solution)/shard_map/all_to_all | solution.py:540
  53.8 3.9 %collective-permute-start.11 = (bf16[384,512]{1,0:T(8,128)(2,1)S(1)}, bf16[384,512]{1,0:T(8,128)(2,1)S(1)}, u32[]{:S(2)}, u32[]{:S(2)}) collective-permute-start(bf16[384,512]{1,0:T(8,128)(2,1)S(1)} %collective-permute-done.10.refs_10_), channel_id=1, source_target_pairs={{0,4},{4,0},{8,12},{12,8},{16,20},{20,16},{1,5},{5,1},{9,13},{13,9... | collective-permute-start | bytes 1179656 | tf_op jit(solution)/shard_map/ppermute | solution.py:427
  57.8 0.0 collective-permute-done.12.refs_12_
  57.8 1.3 collective-permute-start.14
  59.1 0.0 collective-permute-done.6.refs_6_
  59.1 1.4 collective-permute-start.8
  60.5 0.0 collective-permute-done.3.refs_3_
  60.5 0.0 collective-permute-start.1
  60.5 0.0 collective-permute-done.rest_1_
  60.5 0.5 collective-permute-start.2
  61.0 1.7 %gram.1.gram_ref = bf16[3,128,128]{2,1,0:T(8,128)(2,1)S(1)} custom-call(bf16[128,3072]{1,0:T(8,128)(2,1)S(1)} %copy-done), custom_call_target="tpu_custom_call" | custom-call | tf_op jit(solution)/shard_map/gram/pallas_call | solution.py:503
  62.7 0.6 copy-done.2
  63.3 0.1 reshape.18.starts_ref
  63.4 0.1 stack.68.held_ref
  63.5 4.4 %collective-permute-done.11.refs_11_ = bf16[384,512]{1,0:T(8,128)(2,1)S(1)} collective-permute-done((bf16[384,512]{1,0:T(8,128)(2,1)S(1)}, bf16[384,512]{1,0:T(8,128)(2,1)S(1)}, u32[]{:S(2)}, u32[]{:S(2)}) %collective-permute-start.11) | collective-permute-done | bytes 393248 | tf_op jit(solution)/shard_map/ppermute | solution.py:427
  67.9 0.7 collective-permute-start.5
  68.6 1.8 %collective-permute-done.14.refs_14_ = bf16[384,512]{1,0:T(8,128)(2,1)} collective-permute-done((bf16[384,512]{1,0:T(8,128)(2,1)S(1)}, bf16[384,512]{1,0:T(8,128)(2,1)}, u32[]{:S(2)}, u32[]{:S(2)}) %collective-permute-start.14) | collective-permute-done | bytes 393248 | tf_op jit(solution)/shard_map/ppermute | solution.py:421
  70.4 3.4 %collective-permute-start.13 = (bf16[384,512]{1,0:T(8,128)(2,1)S(1)}, bf16[384,512]{1,0:T(8,128)(2,1)S(1)}, u32[]{:S(2)}, u32[]{:S(2)}) collective-permute-start(bf16[384,512]{1,0:T(8,128)(2,1)S(1)} %collective-permute-done.12.refs_12_), channel_id=1, source_target_pairs={{0,4},{4,0},{8,12},{12,8},{1,5},{5,1},{9,13},{13,9},{2,6},{6,2},{1... | collective-permute-start | bytes 1179656 | tf_op jit(solution)/shard_map/ppermute | solution.py:427
  73.8 0.0 collective-permute-done.8.refs_8_
  73.8 1.4 collective-permute-start.7
  75.2 0.0 collective-permute-done.1.rest_2_
  75.2 2.4 %collective-permute-start.15 = (bf16[384,512]{1,0:T(8,128)(2,1)}, bf16[384,512]{1,0:T(8,128)(2,1)}, u32[]{:S(2)}, u32[]{:S(2)}) collective-permute-start(bf16[384,512]{1,0:T(8,128)(2,1)} %collective-permute-done.14.refs_14_), channel_id=1, source_target_pairs={{0,4},{4,0},{1,5},{5,1},{2,6},{6,2},{3,7},{7,3}} | collective-permute-start | bytes 1179656 | tf_op jit(solution)/shard_map/ppermute | solution.py:427
  77.6 0.0 collective-permute-done.2.rest_3_
  77.7 1.4 collective-permute-start.9
  79.1 0.0 all-to-all-done.1
  79.1 0.9 copy-done.3
  80.0 0.7 copy-done.7
  80.7 9.5 %project.1 = (bf16[512,5120]{1,0:T(8,128)(2,1)S(1)}, bf16[5120,512]{1,0:T(8,128)(2,1)S(1)}, bf16[8,4,256,128]{3,2,1,0:T(8,128)(2,1)S(1)}) custom-call(s32[4]{0:T(128)S(1)} %broadcast_xor_fusion.order_ref, bf16[1536,128]{1,0:T(8,128)(2,1)} %bitcast.19.weight_ref, f32[16,128]{1,0:T(8,128)S(1)} %copy-done.7, bf16[3,128,128]{2,1,0:T(8,128)(2,1)S(1)} %copy-done.3, ...), custom_call_target="tpu_custom_call" | custom-call | flops 3355443200 | bytes 16777216 | tf_op jit(solution)/shard_map/project/pallas_call | solution.py:547
  90.2 7.5 %shard_map.113 = (bf16[128,512]{1,0:T(8,128)(2,1)S(1)}, bf16[128,512]{1,0:T(8,128)(2,1)S(1)}) custom-call(s32[4]{0:T(128)S(1)} %broadcast_xor_fusion.order_ref, s32[64]{0:T(128)S(1)} %reshape.18.starts_ref, s32[8]{0:T(128)S(1)} %copy-done.5, bf16[512,5120]{1,0:T(8,128)(2,1)S(1)} %get-tuple-element.26.keys_ref, ...), custom_call_target="tpu_custom_call" | custom-call | flops 2147483648 | bytes 16777216 | tf_op jit(solution)/shard_map/pallas_call | solution.py:563
  97.7 0.0 collective-permute-done.7.refs_7_
  97.7 4.3 %shard_map.114 = (f32[128,3072]{1,0:T(8,128)S(1)}, bf16[128,3072]{1,0:T(8,128)(2,1)S(1)}) custom-call(s32[14]{0:T(128)S(1)} %stack.68.held_ref, bf16[128,512]{1,0:T(8,128)(2,1)S(1)} %get-tuple-element.33.refs_0_, bf16[128,512]{1,0:T(8,128)(2,1)S(1)} %get-tuple-element.34.refs_1_, bf16[384,512]{1,0:T(8,128)(2,1)S(1)} %copy-done.1, ...), custom_call_target="tpu_custom_call" | custom-call | flops 805306368 | bytes 8388608 | tf_op jit(solution)/shard_map/pallas_call | solution.py:583
  102.0 0.1 collective-permute-start.17
  102.1 7.5 %shard_map.115 = (bf16[128,512]{1,0:T(8,128)(2,1)S(1)}, bf16[128,512]{1,0:T(8,128)(2,1)S(1)}) custom-call(s32[4]{0:T(128)S(1)} %broadcast_xor_fusion.order_ref, s32[64]{0:T(128)S(1)} %reshape.18.starts_ref, s32[8]{0:T(128)S(1)} %copy-done.5, bf16[512,5120]{1,0:T(8,128)(2,1)S(1)} %get-tuple-element.26.keys_ref, ...), custom_call_target="tpu_custom_call" | custom-call | flops 2147483648 | bytes 16777216 | tf_op jit(solution)/shard_map/pallas_call | solution.py:563
  109.6 4.1 %shard_map.116 = (f32[128,3072]{1,0:T(8,128)S(1)}, bf16[128,3072]{1,0:T(8,128)(2,1)S(1)}) custom-call(s32[14]{0:T(128)S(1)} %stack.68.held_ref, bf16[128,512]{1,0:T(8,128)(2,1)S(1)} %get-tuple-element.37.refs_0_, bf16[128,512]{1,0:T(8,128)(2,1)S(1)} %get-tuple-element.38.refs_1_, bf16[384,512]{1,0:T(8,128)(2,1)S(1)} %copy-done.1, ...), custom_call_target="tpu_custom_call" | custom-call | flops 805306368 | bytes 8388608 | tf_op jit(solution)/shard_map/pallas_call | solution.py:583
  113.8 0.6 collective-permute-start.19
  114.3 3.8 %shard_map.111 = (bf16[128,512]{1,0:T(8,128)(2,1)S(1)}, bf16[128,512]{1,0:T(8,128)(2,1)S(1)}) custom-call(s32[4]{0:T(128)S(1)} %broadcast_xor_fusion.order_ref, s32[64]{0:T(128)S(1)} %reshape.18.starts_ref, s32[8]{0:T(128)S(1)} %copy-done.5, bf16[512,5120]{1,0:T(8,128)(2,1)S(1)} %get-tuple-element.26.keys_ref, ...), custom_call_target="tpu_custom_call" | custom-call | flops 2147483648 | bytes 16777216 | tf_op jit(solution)/shard_map/pallas_call | solution.py:563
  118.1 4.1 %shard_map.112 = bf16[256,3072]{1,0:T(8,128)(2,1)S(1)} custom-call(s32[14]{0:T(128)S(1)} %stack.68.held_ref, bf16[128,512]{1,0:T(8,128)(2,1)S(1)} %get-tuple-element.31.refs_0_, bf16[128,512]{1,0:T(8,128)(2,1)S(1)} %get-tuple-element.32.refs_1_, bf16[384,512]{1,0:T(8,128)(2,1)S(1)} %copy-done.1, bf16[384,512]{1,0:T(8,128)(2,1)S(1)} %collective-permute-done.3.refs_3_, ...), custom_call_target="tpu_custom_call" | custom-call | flops 805306368 | bytes 8388608 | tf_op jit(solution)/shard_map/pallas_call | solution.py:583
  122.2 5.1 %collective-permute-start.16 = (bf16[256,3072]{1,0:T(8,128)(2,1)S(1)}, bf16[256,3072]{1,0:T(8,128)(2,1)S(1)}, u32[]{:S(2)}, u32[]{:S(2)}) collective-permute-start(bf16[256,3072]{1,0:T(8,128)(2,1)S(1)} %shard_map.112), channel_id=1, source_target_pairs={{0,1},{1,0},{2,3},{3,2},{4,5},{5,4},{6,7},{7,6},{8,9},{9,8},{10,11... | collective-permute-start | bytes 4718600 | tf_op jit(solution)/shard_map/ppermute | solution.py:398
  127.3 0.2 add_convert_fusion.1
  127.5 0.1 collective-permute-start.18
  127.5 0.0 collective-permute-done.19
  127.5 0.2 add_convert_fusion
  127.7 2.1 %collective-permute-start.20 = (bf16[128,3072]{1,0:T(8,128)(2,1)S(1)}, bf16[128,3072]{1,0:T(8,128)(2,1)S(1)}, u32[]{:S(2)}, u32[]{:S(2)}) collective-permute-start(bf16[128,3072]{1,0:T(8,128)(2,1)S(1)} %add_convert_fusion), channel_id=1, source_target_pairs={{0,2},{1,3},{2,0},{3,1},{4,6},{5,7},{6,4},{7,5},{8,10},{9,11},{10,... | collective-permute-start | bytes 2359304 | tf_op jit(solution)/shard_map/ppermute | solution.py:398
  129.8 8.8 %shard_map.109 = (bf16[128,512]{1,0:T(8,128)(2,1)S(1)}, bf16[128,512]{1,0:T(8,128)(2,1)S(1)}) custom-call(s32[4]{0:T(128)S(1)} %broadcast_xor_fusion.order_ref, s32[64]{0:T(128)S(1)} %reshape.18.starts_ref, s32[8]{0:T(128)S(1)} %copy-done.5, bf16[512,5120]{1,0:T(8,128)(2,1)S(1)} %get-tuple-element.26.keys_ref, ...), custom_call_target="tpu_custom_call" | custom-call | flops 2147483648 | bytes 16777216 | tf_op jit(solution)/shard_map/pallas_call | solution.py:563
  138.6 0.0 copy-start.4
  138.6 4.3 %shard_map.110.own_ref = f32[256,3072]{1,0:T(8,128)S(1)} custom-call(s32[14]{0:T(128)S(1)} %stack.68.held_ref, bf16[128,512]{1,0:T(8,128)(2,1)S(1)} %get-tuple-element.29.refs_0_, bf16[128,512]{1,0:T(8,128)(2,1)S(1)} %get-tuple-element.30.refs_1_, bf16[384,512]{1,0:T(8,128)(2,1)S(1)} %copy-done.1, bf16[384,512]{1,0:T(8,128)(2,1)S(1)} %collective-permute-done.3.refs_3_, ...), custom_call_target="tpu_custom_call" | custom-call | flops 805306368 | bytes 8388608 | tf_op jit(solution)/shard_map/pallas_call | solution.py:583
  142.9 5.0 %collective-permute-done.18.second_ref = bf16[128,3072]{1,0:T(8,128)(2,1)S(1)} collective-permute-done((bf16[128,3072]{1,0:T(8,128)(2,1)S(1)}, bf16[128,3072]{1,0:T(8,128)(2,1)S(1)}, u32[]{:S(2)}, u32[]{:S(2)}) %collective-permute-start.18) | collective-permute-done | bytes 786464 | tf_op jit(solution)/shard_map/ppermute | solution.py:398
  147.9 15.9 %collective-permute-done.20.third_ref = bf16[128,3072]{1,0:T(8,128)(2,1)S(1)} collective-permute-done((bf16[128,3072]{1,0:T(8,128)(2,1)S(1)}, bf16[128,3072]{1,0:T(8,128)(2,1)S(1)}, u32[]{:S(2)}, u32[]{:S(2)}) %collective-permute-start.20) | collective-permute-done | bytes 786464 | tf_op jit(solution)/shard_map/ppermute | solution.py:398
  163.8 1.8 %final.1 = bf16[256,3072]{1,0:T(8,128)(2,1)} custom-call(f32[256,3072]{1,0:T(8,128)S(1)} %shard_map.110.own_ref, bf16[256,3072]{1,0:T(8,128)(2,1)S(1)} %collective-permute-done.16.first_ref, bf16[128,3072]{1,0:T(8,128)(2,1)S(1)} %collective-permute-done.18.second_ref, bf16[128,3072]{1,0:T(8,128)(2,1)S(1)} %collective-permute-done.20.third_ref, ...), custom_call_target="tpu_custom_call" | custom-call | tf_op jit(solution)/shard_map/final/pallas_call | solution.py:602
  (22 shorter events, 0.1 us)
Async XLA Ops:
  4.3 7.5 %copy-start.1 = (bf16[384,512]{1,0:T(8,128)(2,1)S(1)}, bf16[384,512]{1,0:T(8,128)(2,1)}, u32[]{:S(2)}) copy-start(bf16[384,512]{1,0:T(8,128)(2,1)} %refs_2_.7) | copy-start | bytes 1179652
  4.3 56.7 %copy-start.8 = (s32[8,8]{1,0:T(8,128)S(1)}, s32[8,8]{1,0:T(8,128)}, u32[]{:S(2)}) copy-start(s32[8,8]{1,0:T(8,128)} %param.19) | copy-start | bytes 772
  4.3 56.7 %copy-start = (bf16[128,3072]{1,0:T(8,128)(2,1)S(1)}, bf16[128,3072]{1,0:T(8,128)(2,1)}, u32[]{:S(2)}) copy-start(bf16[128,3072]{1,0:T(8,128)(2,1)} %embed_ref.3) | copy-start | bytes 2359300
  4.3 34.4 %all-to-all-start = ((bf16[8,384,128]{2,1,0:T(8,128)(2,1)}), bf16[8,384,128]{2,1,0:T(8,128)(2,1)}, u32[]{:S(2)}, u32[]{:S(2)}) async-start(bf16[8,384,128]{2,1,0:T(8,128)(2,1)} %prep.1), calls=%async_computation | async-start | bytes 1572864 | tf_op jit(solution)/shard_map/all_to_all | solution.py:511
  11.8 51.7 %copy-start.9 = (s32[4]{0:T(128)S(1)}, s32[4]{0:T(128)}, u32[]{:S(2)}) copy-start(s32[4]{0:T(128)} %constant.45.clone) | copy-start | bytes 52
  11.8 23.4 %collective-permute-start.10 = (bf16[384,512]{1,0:T(8,128)(2,1)S(1)}, bf16[384,512]{1,0:T(8,128)(2,1)S(1)}, u32[]{:S(2)}, u32[]{:S(2)}) collective-permute-start(bf16[384,512]{1,0:T(8,128)(2,1)S(1)} %copy-done.1), channel_id=1, source_target_pairs={{8,0},{12,4},{16,8},{20,12},{24,16},{28,20},{9,1},{13,5},{17,9},{2... | collective-permute-start | bytes 1179656 | tf_op jit(solution)/shard_map/ppermute | solution.py:421
  13.1 23.4 %collective-permute-start.4 = (bf16[384,512]{1,0:T(8,128)(2,1)S(1)}, bf16[384,512]{1,0:T(8,128)(2,1)S(1)}, u32[]{:S(2)}, u32[]{:S(2)}) collective-permute-start(bf16[384,512]{1,0:T(8,128)(2,1)S(1)} %copy-done.1), channel_id=1, source_target_pairs={{0,8},{4,12},{8,16},{12,20},{16,24},{20,28},{1,9},{5,13},{9,17},{1... | collective-permute-start | bytes 1179656 | tf_op jit(solution)/shard_map/ppermute | solution.py:421
  35.3 22.5 %collective-permute-start.12 = (bf16[384,512]{1,0:T(8,128)(2,1)S(1)}, bf16[384,512]{1,0:T(8,128)(2,1)S(1)}, u32[]{:S(2)}, u32[]{:S(2)}) collective-permute-start(bf16[384,512]{1,0:T(8,128)(2,1)S(1)} %collective-permute-done.10.refs_10_), channel_id=1, source_target_pairs={{8,0},{12,4},{16,8},{20,12},{9,1},{13,5},{17,9},{21,13},{10,2},{14... | collective-permute-start | bytes 1179656 | tf_op jit(solution)/shard_map/ppermute | solution.py:421
  36.6 22.5 %collective-permute-start.6 = (bf16[384,512]{1,0:T(8,128)(2,1)S(1)}, bf16[384,512]{1,0:T(8,128)(2,1)S(1)}, u32[]{:S(2)}, u32[]{:S(2)}) collective-permute-start(bf16[384,512]{1,0:T(8,128)(2,1)S(1)} %collective-permute-done.4.refs_4_), channel_id=1, source_target_pairs={{8,16},{12,20},{16,24},{20,28},{9,17},{13,21},{17,25},{21,29},{10,... | collective-permute-start | bytes 1179656 | tf_op jit(solution)/shard_map/ppermute | solution.py:421
  37.3 23.2 %collective-permute-start.3 = (bf16[384,512]{1,0:T(8,128)(2,1)S(1)}, bf16[384,512]{1,0:T(8,128)(2,1)S(1)}, u32[]{:S(2)}, u32[]{:S(2)}) collective-permute-start(bf16[384,512]{1,0:T(8,128)(2,1)S(1)} %copy-done.1), channel_id=1, source_target_pairs={{0,4},{4,0},{8,12},{12,8},{16,20},{20,16},{24,28},{28,24},{1,5},{5... | collective-permute-start | bytes 1179656 | tf_op jit(solution)/shard_map/ppermute | solution.py:410
  40.8 0.6 copy-start.6
  41.4 19.1 %collective-permute-start = (bf16[1296,128]{1,0:T(8,128)(2,1)}, bf16[1296,128]{1,0:T(8,128)(2,1)}, u32[]{:S(2)}, u32[]{:S(2)}) collective-permute-start(bf16[1296,128]{1,0:T(8,128)(2,1)} %get-tuple-element.25.rest_0_), channel_id=1, source_target_pairs={{0,2},{1,3},{2,0},{3,1},{4,6},{5,7},{6,4},{7,5},{8,10},{9,11},{10,... | collective-permute-start | bytes 995336 | tf_op jit(solution)/shard_map/ppermute | solution.py:398
  42.9 36.2 %all-to-all-start.1 = ((bf16[8,192,128]{2,1,0:T(8,128)(2,1)}), bf16[8,192,128]{2,1,0:T(8,128)(2,1)}, u32[]{:S(2)}, u32[]{:S(2)}) async-start(bf16[8,192,128]{2,1,0:T(8,128)(2,1)} %get-tuple-element.23), calls=%async_computation.1 | async-start | bytes 786432 | tf_op jit(solution)/shard_map/all_to_all | solution.py:540
  53.8 14.1 %collective-permute-start.11 = (bf16[384,512]{1,0:T(8,128)(2,1)S(1)}, bf16[384,512]{1,0:T(8,128)(2,1)S(1)}, u32[]{:S(2)}, u32[]{:S(2)}) collective-permute-start(bf16[384,512]{1,0:T(8,128)(2,1)S(1)} %collective-permute-done.10.refs_10_), channel_id=1, source_target_pairs={{0,4},{4,0},{8,12},{12,8},{16,20},{20,16},{1,5},{5,1},{9,13},{13,9... | collective-permute-start | bytes 1179656 | tf_op jit(solution)/shard_map/ppermute | solution.py:427
  57.8 12.6 %collective-permute-start.14 = (bf16[384,512]{1,0:T(8,128)(2,1)S(1)}, bf16[384,512]{1,0:T(8,128)(2,1)}, u32[]{:S(2)}, u32[]{:S(2)}) collective-permute-start(bf16[384,512]{1,0:T(8,128)(2,1)S(1)} %collective-permute-done.12.refs_12_), channel_id=1, source_target_pairs={{8,0},{12,4},{9,1},{13,5},{10,2},{14,6},{11,3},{15,7}} | collective-permute-start | bytes 1179656 | tf_op jit(solution)/shard_map/ppermute | solution.py:421
  59.1 14.7 %collective-permute-start.8 = (bf16[384,512]{1,0:T(8,128)(2,1)S(1)}, bf16[384,512]{1,0:T(8,128)(2,1)}, u32[]{:S(2)}, u32[]{:S(2)}) collective-permute-start(bf16[384,512]{1,0:T(8,128)(2,1)S(1)} %collective-permute-done.6.refs_6_), channel_id=1, source_target_pairs={{16,24},{20,28},{17,25},{21,29},{18,26},{22,30},{19,27},{23,31}} | collective-permute-start | bytes 1179656 | tf_op jit(solution)/shard_map/ppermute | solution.py:421
  60.5 14.7 %collective-permute-start.1 = (bf16[1296,128]{1,0:T(8,128)(2,1)}, bf16[1296,128]{1,0:T(8,128)(2,1)}, u32[]{:S(2)}, u32[]{:S(2)}) collective-permute-start(bf16[1296,128]{1,0:T(8,128)(2,1)} %get-tuple-element.25.rest_0_), channel_id=1, source_target_pairs={{0,1},{1,0},{2,3},{3,2},{4,5},{5,4},{6,7},{7,6},{8,9},{9,8},{10,11... | collective-permute-start | bytes 995336 | tf_op jit(solution)/shard_map/ppermute | solution.py:398
  60.5 17.1 %collective-permute-start.2 = (bf16[1296,128]{1,0:T(8,128)(2,1)}, bf16[1296,128]{1,0:T(8,128)(2,1)}, u32[]{:S(2)}, u32[]{:S(2)}) collective-permute-start(bf16[1296,128]{1,0:T(8,128)(2,1)} %collective-permute-done.rest_1_), channel_id=1, source_target_pairs={{0,1},{1,0},{2,3},{3,2},{4,5},{5,4},{6,7},{7,6},{8,9},{9,8},{10,11... | collective-permute-start | bytes 995336 | tf_op jit(solution)/shard_map/ppermute | solution.py:398
  62.7 0.6 copy-start.2
  67.9 29.8 %collective-permute-start.5 = (bf16[384,512]{1,0:T(8,128)(2,1)S(1)}, bf16[384,512]{1,0:T(8,128)(2,1)S(1)}, u32[]{:S(2)}, u32[]{:S(2)}) collective-permute-start(bf16[384,512]{1,0:T(8,128)(2,1)S(1)} %collective-permute-done.4.refs_4_), channel_id=1, source_target_pairs={{8,12},{12,8},{16,20},{20,16},{24,28},{28,24},{9,13},{13,9},{17,21... | collective-permute-start | bytes 1179656 | tf_op jit(solution)/shard_map/ppermute | solution.py:427
  70.4 27.3 %collective-permute-start.13 = (bf16[384,512]{1,0:T(8,128)(2,1)S(1)}, bf16[384,512]{1,0:T(8,128)(2,1)S(1)}, u32[]{:S(2)}, u32[]{:S(2)}) collective-permute-start(bf16[384,512]{1,0:T(8,128)(2,1)S(1)} %collective-permute-done.12.refs_12_), channel_id=1, source_target_pairs={{0,4},{4,0},{8,12},{12,8},{1,5},{5,1},{9,13},{13,9},{2,6},{6,2},{1... | collective-permute-start | bytes 1179656 | tf_op jit(solution)/shard_map/ppermute | solution.py:427
  73.8 23.9 %collective-permute-start.7 = (bf16[384,512]{1,0:T(8,128)(2,1)S(1)}, bf16[384,512]{1,0:T(8,128)(2,1)}, u32[]{:S(2)}, u32[]{:S(2)}) collective-permute-start(bf16[384,512]{1,0:T(8,128)(2,1)S(1)} %collective-permute-done.6.refs_6_), channel_id=1, source_target_pairs={{16,20},{20,16},{24,28},{28,24},{17,21},{21,17},{25,29},{29,25},{1... | collective-permute-start | bytes 1179656 | tf_op jit(solution)/shard_map/ppermute | solution.py:427
  75.2 22.5 %collective-permute-start.15 = (bf16[384,512]{1,0:T(8,128)(2,1)}, bf16[384,512]{1,0:T(8,128)(2,1)}, u32[]{:S(2)}, u32[]{:S(2)}) collective-permute-start(bf16[384,512]{1,0:T(8,128)(2,1)} %collective-permute-done.14.refs_14_), channel_id=1, source_target_pairs={{0,4},{4,0},{1,5},{5,1},{2,6},{6,2},{3,7},{7,3}} | collective-permute-start | bytes 1179656 | tf_op jit(solution)/shard_map/ppermute | solution.py:427
  77.7 20.1 %collective-permute-start.9 = (bf16[384,512]{1,0:T(8,128)(2,1)}, bf16[384,512]{1,0:T(8,128)(2,1)}, u32[]{:S(2)}, u32[]{:S(2)}) collective-permute-start(bf16[384,512]{1,0:T(8,128)(2,1)} %collective-permute-done.8.refs_8_), channel_id=1, source_target_pairs={{24,28},{28,24},{25,29},{29,25},{26,30},{30,26},{27,31},{31,27}} | collective-permute-start | bytes 1179656 | tf_op jit(solution)/shard_map/ppermute | solution.py:427
  79.1 0.9 copy-start.3
  80.0 0.7 copy-start.7
  80.7 9.5 %copy-start.5 = (s32[8]{0:T(128)S(1)}, s32[8]{0:T(128)}, u32[]{:S(2)}) copy-start(s32[8]{0:T(128)} %counts_ref.7) | copy-start | bytes 100
  102.0 25.3 %collective-permute-start.17 = (bf16[128,3072]{1,0:T(8,128)(2,1)S(1)}, bf16[128,3072]{1,0:T(8,128)(2,1)S(1)}, u32[]{:S(2)}, u32[]{:S(2)}) collective-permute-start(bf16[128,3072]{1,0:T(8,128)(2,1)S(1)} %get-tuple-element.36), channel_id=1, source_target_pairs={{0,1},{1,0},{2,3},{3,2},{4,5},{5,4},{6,7},{7,6},{8,9},{9,8},{10,11... | collective-permute-start | bytes 2359304 | tf_op jit(solution)/shard_map/ppermute | solution.py:398
  113.8 13.8 %collective-permute-start.19 = (bf16[128,3072]{1,0:T(8,128)(2,1)S(1)}, bf16[128,3072]{1,0:T(8,128)(2,1)S(1)}, u32[]{:S(2)}, u32[]{:S(2)}) collective-permute-start(bf16[128,3072]{1,0:T(8,128)(2,1)S(1)} %get-tuple-element.40), channel_id=1, source_target_pairs={{0,1},{1,0},{2,3},{3,2},{4,5},{5,4},{6,7},{7,6},{8,9},{9,8},{10,11... | collective-permute-start | bytes 2359304 | tf_op jit(solution)/shard_map/ppermute | solution.py:398
  122.2 20.7 %collective-permute-start.16 = (bf16[256,3072]{1,0:T(8,128)(2,1)S(1)}, bf16[256,3072]{1,0:T(8,128)(2,1)S(1)}, u32[]{:S(2)}, u32[]{:S(2)}) collective-permute-start(bf16[256,3072]{1,0:T(8,128)(2,1)S(1)} %shard_map.112), channel_id=1, source_target_pairs={{0,1},{1,0},{2,3},{3,2},{4,5},{5,4},{6,7},{7,6},{8,9},{9,8},{10,11... | collective-permute-start | bytes 4718600 | tf_op jit(solution)/shard_map/ppermute | solution.py:398
  127.5 20.5 %collective-permute-start.18 = (bf16[128,3072]{1,0:T(8,128)(2,1)S(1)}, bf16[128,3072]{1,0:T(8,128)(2,1)S(1)}, u32[]{:S(2)}, u32[]{:S(2)}) collective-permute-start(bf16[128,3072]{1,0:T(8,128)(2,1)S(1)} %add_convert_fusion.1), channel_id=1, source_target_pairs={{0,2},{1,3},{2,0},{3,1},{4,6},{5,7},{6,4},{7,5},{8,10},{9,11},{10,... | collective-permute-start | bytes 2359304 | tf_op jit(solution)/shard_map/ppermute | solution.py:398
  127.7 36.1 %collective-permute-start.20 = (bf16[128,3072]{1,0:T(8,128)(2,1)S(1)}, bf16[128,3072]{1,0:T(8,128)(2,1)S(1)}, u32[]{:S(2)}, u32[]{:S(2)}) collective-permute-start(bf16[128,3072]{1,0:T(8,128)(2,1)S(1)} %add_convert_fusion), channel_id=1, source_target_pairs={{0,2},{1,3},{2,0},{3,1},{4,6},{5,7},{6,4},{7,5},{8,10},{9,11},{10,... | collective-permute-start | bytes 2359304 | tf_op jit(solution)/shard_map/ppermute | solution.py:398
  138.6 25.3 %copy-start.4 = (f32[3072]{0:T(1024)S(1)}, f32[3072]{0:T(1024)}, u32[]{:S(2)}) copy-start(f32[3072]{0:T(1024)} %param.18) | copy-start | bytes 36868

commit v8 on v7

--- a/solution.py
+++ b/solution.py
@@ -521,7 +521,6 @@
             ),
             in_specs=[whole_spec()],
             out_specs=(whole_spec(),) * 3,
-            compiler_params=small,
             name="middle",
         )(arrived)
     else:
@@ -535,7 +534,10 @@
     group, order = [near], [0]
     bits = [1 << k for k in range(1, narrow_count.bit_length() - 1)] + [1]
     for bit in bits:
-        group = group + [flip(rows, "narrow", bit) for rows in group]
+        others = []
+        for rows in group:
+            others.append(flip(rows, "narrow", bit))
+        group = group + others
         order = order + [index ^ bit for index in order]
     everything = lax.all_to_all(spread, "wide", split_axis=0, concat_axis=0, tiled=True)
     weight_all = everything.reshape(3 * heads_width, patch)

time: 166 us -> 167 us (level)
  the two profiles are of different devices: /device:TPU:0 before, /device:TPU:24 now
where the time goes in v8:
time: 167 us; the launch traced here: 166 us
  Pallas kernels  68 us (41%)
  waiting for transfers between devices  46.9 us (28%)
  starting transfers between devices  46.5 us (28%)
  local copies, waits for them, and re-layouts  3.38 us (2%)
    pallas_call x4, Pallas kernels, attend(): pl.pallas_call(functools.partial(attend_kernel, parts, entries), out_shap...  32.6 us
    ppermute x8, waiting for transfers between devices, flip(): return lax.ppermute(block, axis, [(i, i ^ bit) for i in devices])  25.2 us
    ppermute x6, waiting for transfers between devices, gathered_rows(): current = lax.ppermute(current, 'wide', route)  21.7 us
    pallas_call x4, Pallas kernels, multiply(): pl.pallas_call(functools.partial(partial_kernel, kept, sent), out_shape=t...  16.8 us
    all_to_all x1, starting transfers between devices, block(): lax.all_to_all(spread, 'wide', split_axis=0, concat_axis=0, tiled=True)  13.1 us
    ppermute x6, starting transfers between devices, gathered_rows(): blocks.append(lax.ppermute(current, 'wide', swap))  12 us
    pallas_call x1, Pallas kernels, block(): pl.pallas_call(functools.partial(project_kernel, row_total, tile_size), o...  9.35 us
    ppermute x6, starting transfers between devices, gathered_rows(): current = lax.ppermute(current, 'wide', route)  8.59 us
  transfers between devices with their start and end apart: 23, of which 4 were waited for; matrix products, arithmetic and copies ran while one was open for 0% of the time, Pallas kernels for 35%

profile of v8, /device:TPU:24, one launch (start us, length us, event | category | flops | bytes accessed | tf_op | source)
XLA Modules:
  0.0 166.1 jit_solution(8302468146197052116)
XLA Ops:
  0.0 0.6 pad_add_fusion.at_ref
  0.6 3.7 %prep.1 = bf16[8,384,128]{2,1,0:T(8,128)(2,1)} custom-call(s32[2]{0:T(128)} %pad_add_fusion.at_ref, bf16[128,3072]{1,0:T(8,128)(2,1)} %embed_ref.3, bf16[128,3072]{1,0:T(8,128)(2,1)} %embed_ref.3, f32[1,3072]{1,0:T(1,128)} %bitcast.22, f32[1,3072]{1,0:T(1,128)} %bitcast.23, bf16[3,384,512]{2,1,0:T(8,128)(2,1)} %qkv_ref.1, bf16[256,128]{1,0:T(8,128)(2,1)} %latents_ref.1, ...), custom_call_target="tpu_custom_call" | custom-call | flops 268435456 | bytes 4194304 | tf_op jit(solution)/shard_map/prep/pallas_call | solution.py:488
  4.3 6.2 %all-to-all-start = ((bf16[8,384,128]{2,1,0:T(8,128)(2,1)}), bf16[8,384,128]{2,1,0:T(8,128)(2,1)}, u32[]{:S(2)}, u32[]{:S(2)}) async-start(bf16[8,384,128]{2,1,0:T(8,128)(2,1)} %prep.1), calls=%async_computation | async-start | bytes 1572864 | tf_op jit(solution)/shard_map/all_to_all | solution.py:511
  10.5 2.6 %collective-permute-start.10 = (bf16[384,512]{1,0:T(8,128)(2,1)S(1)}, bf16[384,512]{1,0:T(8,128)(2,1)S(1)}, u32[]{:S(2)}, u32[]{:S(2)}) collective-permute-start(bf16[384,512]{1,0:T(8,128)(2,1)S(1)} %copy-done.1), channel_id=1, source_target_pairs={{8,0},{12,4},{16,8},{20,12},{24,16},{28,20},{9,1},{13,5},{17,9},{2... | collective-permute-start | bytes 1179656 | tf_op jit(solution)/shard_map/ppermute | solution.py:421
  13.2 1.3 collective-permute-start.4
  14.5 17.1 %collective-permute-done.10.refs_10_ = bf16[384,512]{1,0:T(8,128)(2,1)S(1)} collective-permute-done((bf16[384,512]{1,0:T(8,128)(2,1)S(1)}, bf16[384,512]{1,0:T(8,128)(2,1)S(1)}, u32[]{:S(2)}, u32[]{:S(2)}) %collective-permute-start.10) | collective-permute-done | bytes 393248 | tf_op jit(solution)/shard_map/ppermute | solution.py:421
  31.6 0.7 collective-permute-start.12
  32.3 0.0 collective-permute-done.4.refs_4_
  32.3 1.3 collective-permute-start.6
  33.6 1.7 %collective-permute-start.3 = (bf16[384,512]{1,0:T(8,128)(2,1)S(1)}, bf16[384,512]{1,0:T(8,128)(2,1)S(1)}, u32[]{:S(2)}, u32[]{:S(2)}) collective-permute-start(bf16[384,512]{1,0:T(8,128)(2,1)S(1)} %copy-done.1), channel_id=1, source_target_pairs={{0,4},{4,0},{8,12},{12,8},{16,20},{20,16},{24,28},{28,24},{1,5},{5... | collective-permute-start | bytes 1179656 | tf_op jit(solution)/shard_map/ppermute | solution.py:410
  35.3 0.0 all-to-all-done.arrived_ref
  35.3 2.0 %middle.1 = (bf16[8,192,128]{2,1,0:T(8,128)(2,1)}, bf16[1296,128]{1,0:T(8,128)(2,1)}, f32[16,128]{1,0:T(8,128)}) custom-call(bf16[8,384,128]{2,1,0:T(8,128)(2,1)} %all-to-all-done.arrived_ref), custom_call_target="tpu_custom_call" | custom-call | tf_op jit(solution)/shard_map/middle/pallas_call | solution.py:515
  37.3 1.5 collective-permute-start
  38.8 13.1 %all-to-all-start.1 = ((bf16[8,192,128]{2,1,0:T(8,128)(2,1)}), bf16[8,192,128]{2,1,0:T(8,128)(2,1)}, u32[]{:S(2)}, u32[]{:S(2)}) async-start(bf16[8,192,128]{2,1,0:T(8,128)(2,1)} %get-tuple-element.23), calls=%async_computation.1 | async-start | bytes 786432 | tf_op jit(solution)/shard_map/all_to_all | solution.py:542
  51.9 0.7 collective-permute-start.11
  52.6 0.0 collective-permute-done.12.refs_12_
  52.6 1.4 collective-permute-start.14
  54.0 0.0 collective-permute-done.6.refs_6_
  54.0 1.3 collective-permute-start.8
  55.3 0.1 collective-permute-start.1
  55.4 0.5 collective-permute-start.2
  55.9 1.7 %gram.1.gram_ref = bf16[3,128,128]{2,1,0:T(8,128)(2,1)S(1)} custom-call(bf16[128,3072]{1,0:T(8,128)(2,1)S(1)} %copy-done), custom_call_target="tpu_custom_call" | custom-call | tf_op jit(solution)/shard_map/gram/pallas_call | solution.py:503
  57.6 0.6 copy-done.2
  58.3 0.1 reshape.18.starts_ref
  58.3 0.1 stack.68.held_ref
  58.5 0.0 collective-permute-done.11.refs_11_
  58.5 3.4 %collective-permute-start.5 = (bf16[384,512]{1,0:T(8,128)(2,1)S(1)}, bf16[384,512]{1,0:T(8,128)(2,1)S(1)}, u32[]{:S(2)}, u32[]{:S(2)}) collective-permute-start(bf16[384,512]{1,0:T(8,128)(2,1)S(1)} %collective-permute-done.4.refs_4_), channel_id=1, source_target_pairs={{8,12},{12,8},{16,20},{20,16},{24,28},{28,24},{9,13},{13,9},{17,21... | collective-permute-start | bytes 1179656 | tf_op jit(solution)/shard_map/ppermute | solution.py:427
  61.8 0.0 collective-permute-done.14.refs_14_
  61.9 0.7 collective-permute-start.13
  62.5 4.6 %collective-permute-done.8.refs_8_ = bf16[384,512]{1,0:T(8,128)(2,1)} collective-permute-done((bf16[384,512]{1,0:T(8,128)(2,1)S(1)}, bf16[384,512]{1,0:T(8,128)(2,1)}, u32[]{:S(2)}, u32[]{:S(2)}) %collective-permute-start.8) | collective-permute-done | bytes 393248 | tf_op jit(solution)/shard_map/ppermute | solution.py:421
  67.1 2.7 %collective-permute-start.7 = (bf16[384,512]{1,0:T(8,128)(2,1)S(1)}, bf16[384,512]{1,0:T(8,128)(2,1)}, u32[]{:S(2)}, u32[]{:S(2)}) collective-permute-start(bf16[384,512]{1,0:T(8,128)(2,1)S(1)} %collective-permute-done.6.refs_6_), channel_id=1, source_target_pairs={{16,20},{20,16},{24,28},{28,24},{17,21},{21,17},{25,29},{29,25},{1... | collective-permute-start | bytes 1179656 | tf_op jit(solution)/shard_map/ppermute | solution.py:427
  69.9 1.4 collective-permute-start.15
  71.3 0.0 collective-permute-done.2.rest_3_
  71.3 3.1 %collective-permute-start.9 = (bf16[384,512]{1,0:T(8,128)(2,1)}, bf16[384,512]{1,0:T(8,128)(2,1)}, u32[]{:S(2)}, u32[]{:S(2)}) collective-permute-start(bf16[384,512]{1,0:T(8,128)(2,1)} %collective-permute-done.8.refs_8_), channel_id=1, source_target_pairs={{24,28},{28,24},{25,29},{29,25},{26,30},{30,26},{27,31},{31,27}} | collective-permute-start | bytes 1179656 | tf_op jit(solution)/shard_map/ppermute | solution.py:427
  74.4 0.9 copy-done.3
  75.3 1.0 copy-done.6
  76.3 0.7 copy-done.7
  77.0 9.4 %project.1 = (bf16[512,5120]{1,0:T(8,128)(2,1)S(1)}, bf16[5120,512]{1,0:T(8,128)(2,1)S(1)}, bf16[8,4,256,128]{3,2,1,0:T(8,128)(2,1)S(1)}) custom-call(s32[4]{0:T(128)S(1)} %broadcast_xor_fusion.order_ref, bf16[1536,128]{1,0:T(8,128)(2,1)} %bitcast.19.weight_ref, f32[16,128]{1,0:T(8,128)S(1)} %copy-done.7, bf16[3,128,128]{2,1,0:T(8,128)(2,1)S(1)} %copy-done.3, ...), custom_call_target="tpu_custom_call" | custom-call | flops 3355443200 | bytes 16777216 | tf_op jit(solution)/shard_map/project/pallas_call | solution.py:549
  86.4 7.5 %shard_map.113 = (bf16[128,512]{1,0:T(8,128)(2,1)S(1)}, bf16[128,512]{1,0:T(8,128)(2,1)S(1)}) custom-call(s32[4]{0:T(128)S(1)} %broadcast_xor_fusion.order_ref, s32[64]{0:T(128)S(1)} %reshape.18.starts_ref, s32[8]{0:T(128)S(1)} %copy-done.5, bf16[512,5120]{1,0:T(8,128)(2,1)S(1)} %get-tuple-element.26.keys_ref, ...), custom_call_target="tpu_custom_call" | custom-call | flops 2147483648 | bytes 16777216 | tf_op jit(solution)/shard_map/pallas_call | solution.py:565
  93.9 0.0 collective-permute-done.5.refs_5_
  93.9 0.0 collective-permute-done.13.refs_13_
  93.9 0.0 collective-permute-done.15.refs_15_
  93.9 0.0 collective-permute-done.9.refs_9_
  94.0 4.3 %shard_map.114 = (f32[128,3072]{1,0:T(8,128)S(1)}, bf16[128,3072]{1,0:T(8,128)(2,1)S(1)}) custom-call(s32[14]{0:T(128)S(1)} %stack.68.held_ref, bf16[128,512]{1,0:T(8,128)(2,1)S(1)} %get-tuple-element.33.refs_0_, bf16[128,512]{1,0:T(8,128)(2,1)S(1)} %get-tuple-element.34.refs_1_, bf16[384,512]{1,0:T(8,128)(2,1)S(1)} %copy-done.1, ...), custom_call_target="tpu_custom_call" | custom-call | flops 805306368 | bytes 8388608 | tf_op jit(solution)/shard_map/pallas_call | solution.py:585
  98.2 0.1 collective-permute-start.17
  98.3 11.3 %shard_map.115 = (bf16[128,512]{1,0:T(8,128)(2,1)S(1)}, bf16[128,512]{1,0:T(8,128)(2,1)S(1)}) custom-call(s32[4]{0:T(128)S(1)} %broadcast_xor_fusion.order_ref, s32[64]{0:T(128)S(1)} %reshape.18.starts_ref, s32[8]{0:T(128)S(1)} %copy-done.5, bf16[512,5120]{1,0:T(8,128)(2,1)S(1)} %get-tuple-element.26.keys_ref, ...), custom_call_target="tpu_custom_call" | custom-call | flops 2147483648 | bytes 16777216 | tf_op jit(solution)/shard_map/pallas_call | solution.py:565
  109.6 4.1 %shard_map.116 = (f32[128,3072]{1,0:T(8,128)S(1)}, bf16[128,3072]{1,0:T(8,128)(2,1)S(1)}) custom-call(s32[14]{0:T(128)S(1)} %stack.68.held_ref, bf16[128,512]{1,0:T(8,128)(2,1)S(1)} %get-tuple-element.37.refs_0_, bf16[128,512]{1,0:T(8,128)(2,1)S(1)} %get-tuple-element.38.refs_1_, bf16[384,512]{1,0:T(8,128)(2,1)S(1)} %copy-done.1, ...), custom_call_target="tpu_custom_call" | custom-call | flops 805306368 | bytes 8388608 | tf_op jit(solution)/shard_map/pallas_call | solution.py:585
  113.7 0.6 collective-permute-start.19
  114.3 8.8 %shard_map.111 = (bf16[128,512]{1,0:T(8,128)(2,1)S(1)}, bf16[128,512]{1,0:T(8,128)(2,1)S(1)}) custom-call(s32[4]{0:T(128)S(1)} %broadcast_xor_fusion.order_ref, s32[64]{0:T(128)S(1)} %reshape.18.starts_ref, s32[8]{0:T(128)S(1)} %copy-done.5, bf16[512,5120]{1,0:T(8,128)(2,1)S(1)} %get-tuple-element.26.keys_ref, ...), custom_call_target="tpu_custom_call" | custom-call | flops 2147483648 | bytes 16777216 | tf_op jit(solution)/shard_map/pallas_call | solution.py:565
  123.1 4.1 %shard_map.112 = bf16[256,3072]{1,0:T(8,128)(2,1)S(1)} custom-call(s32[14]{0:T(128)S(1)} %stack.68.held_ref, bf16[128,512]{1,0:T(8,128)(2,1)S(1)} %get-tuple-element.31.refs_0_, bf16[128,512]{1,0:T(8,128)(2,1)S(1)} %get-tuple-element.32.refs_1_, bf16[384,512]{1,0:T(8,128)(2,1)S(1)} %copy-done.1, bf16[384,512]{1,0:T(8,128)(2,1)S(1)} %collective-permute-done.3.refs_3_, ...), custom_call_target="tpu_custom_call" | custom-call | flops 805306368 | bytes 8388608 | tf_op jit(solution)/shard_map/pallas_call | solution.py:585
  127.2 0.1 collective-permute-start.16
  127.3 0.0 collective-permute-done.17
  127.3 0.2 add_convert_fusion.1
  127.4 0.1 collective-permute-start.18
  127.5 0.0 collective-permute-done.19
  127.5 0.2 add_convert_fusion
  127.7 2.1 %collective-permute-start.20 = (bf16[128,3072]{1,0:T(8,128)(2,1)S(1)}, bf16[128,3072]{1,0:T(8,128)(2,1)S(1)}, u32[]{:S(2)}, u32[]{:S(2)}) collective-permute-start(bf16[128,3072]{1,0:T(8,128)(2,1)S(1)} %add_convert_fusion), channel_id=1, source_target_pairs={{0,2},{1,3},{2,0},{3,1},{4,6},{5,7},{6,4},{7,5},{8,10},{9,11},{10,... | collective-permute-start | bytes 2359304 | tf_op jit(solution)/shard_map/ppermute | solution.py:398
  129.7 5.0 %shard_map.109 = (bf16[128,512]{1,0:T(8,128)(2,1)S(1)}, bf16[128,512]{1,0:T(8,128)(2,1)S(1)}) custom-call(s32[4]{0:T(128)S(1)} %broadcast_xor_fusion.order_ref, s32[64]{0:T(128)S(1)} %reshape.18.starts_ref, s32[8]{0:T(128)S(1)} %copy-done.5, bf16[512,5120]{1,0:T(8,128)(2,1)S(1)} %get-tuple-element.26.keys_ref, ...), custom_call_target="tpu_custom_call" | custom-call | flops 2147483648 | bytes 16777216 | tf_op jit(solution)/shard_map/pallas_call | solution.py:565
  134.8 0.0 copy-start.4
  134.8 4.3 %shard_map.110.own_ref = f32[256,3072]{1,0:T(8,128)S(1)} custom-call(s32[14]{0:T(128)S(1)} %stack.68.held_ref, bf16[128,512]{1,0:T(8,128)(2,1)S(1)} %get-tuple-element.29.refs_0_, bf16[128,512]{1,0:T(8,128)(2,1)S(1)} %get-tuple-element.30.refs_1_, bf16[384,512]{1,0:T(8,128)(2,1)S(1)} %copy-done.1, bf16[384,512]{1,0:T(8,128)(2,1)S(1)} %collective-permute-done.3.refs_3_, ...), custom_call_target="tpu_custom_call" | custom-call | flops 805306368 | bytes 8388608 | tf_op jit(solution)/shard_map/pallas_call | solution.py:585
  139.1 0.0 collective-permute-done.16.first_ref
  139.1 8.8 %collective-permute-done.18.second_ref = bf16[128,3072]{1,0:T(8,128)(2,1)S(1)} collective-permute-done((bf16[128,3072]{1,0:T(8,128)(2,1)S(1)}, bf16[128,3072]{1,0:T(8,128)(2,1)S(1)}, u32[]{:S(2)}, u32[]{:S(2)}) %collective-permute-start.18) | collective-permute-done | bytes 786464 | tf_op jit(solution)/shard_map/ppermute | solution.py:398
  147.9 16.4 %collective-permute-done.20.third_ref = bf16[128,3072]{1,0:T(8,128)(2,1)S(1)} collective-permute-done((bf16[128,3072]{1,0:T(8,128)(2,1)S(1)}, bf16[128,3072]{1,0:T(8,128)(2,1)S(1)}, u32[]{:S(2)}, u32[]{:S(2)}) %collective-permute-start.20) | collective-permute-done | bytes 786464 | tf_op jit(solution)/shard_map/ppermute | solution.py:398
  164.3 1.8 %final.1 = bf16[256,3072]{1,0:T(8,128)(2,1)} custom-call(f32[256,3072]{1,0:T(8,128)S(1)} %shard_map.110.own_ref, bf16[256,3072]{1,0:T(8,128)(2,1)S(1)} %collective-permute-done.16.first_ref, bf16[128,3072]{1,0:T(8,128)(2,1)S(1)} %collective-permute-done.18.second_ref, bf16[128,3072]{1,0:T(8,128)(2,1)S(1)} %collective-permute-done.20.third_ref, ...), custom_call_target="tpu_custom_call" | custom-call | tf_op jit(solution)/shard_map/final/pallas_call | solution.py:604
  (22 shorter events, 0.1 us)
Async XLA Ops:
  4.3 6.2 %copy-start.1 = (bf16[384,512]{1,0:T(8,128)(2,1)S(1)}, bf16[384,512]{1,0:T(8,128)(2,1)}, u32[]{:S(2)}) copy-start(bf16[384,512]{1,0:T(8,128)(2,1)} %refs_2_.7) | copy-start | bytes 1179652
  4.3 51.6 %copy-start.8 = (s32[8,8]{1,0:T(8,128)S(1)}, s32[8,8]{1,0:T(8,128)}, u32[]{:S(2)}) copy-start(s32[8,8]{1,0:T(8,128)} %param.19) | copy-start | bytes 772
  4.3 51.6 %copy-start = (bf16[128,3072]{1,0:T(8,128)(2,1)S(1)}, bf16[128,3072]{1,0:T(8,128)(2,1)}, u32[]{:S(2)}) copy-start(bf16[128,3072]{1,0:T(8,128)(2,1)} %embed_ref.3) | copy-start | bytes 2359300
  4.3 31.0 %all-to-all-start = ((bf16[8,384,128]{2,1,0:T(8,128)(2,1)}), bf16[8,384,128]{2,1,0:T(8,128)(2,1)}, u32[]{:S(2)}, u32[]{:S(2)}) async-start(bf16[8,384,128]{2,1,0:T(8,128)(2,1)} %prep.1), calls=%async_computation | async-start | bytes 1572864 | tf_op jit(solution)/shard_map/all_to_all | solution.py:511
  10.5 47.9 %copy-start.9 = (s32[4]{0:T(128)S(1)}, s32[4]{0:T(128)}, u32[]{:S(2)}) copy-start(s32[4]{0:T(128)} %constant.45.clone) | copy-start | bytes 52
  10.5 21.0 %collective-permute-start.10 = (bf16[384,512]{1,0:T(8,128)(2,1)S(1)}, bf16[384,512]{1,0:T(8,128)(2,1)S(1)}, u32[]{:S(2)}, u32[]{:S(2)}) collective-permute-start(bf16[384,512]{1,0:T(8,128)(2,1)S(1)} %copy-done.1), channel_id=1, source_target_pairs={{8,0},{12,4},{16,8},{20,12},{24,16},{28,20},{9,1},{13,5},{17,9},{2... | collective-permute-start | bytes 1179656 | tf_op jit(solution)/shard_map/ppermute | solution.py:421
  13.2 19.1 %collective-permute-start.4 = (bf16[384,512]{1,0:T(8,128)(2,1)S(1)}, bf16[384,512]{1,0:T(8,128)(2,1)S(1)}, u32[]{:S(2)}, u32[]{:S(2)}) collective-permute-start(bf16[384,512]{1,0:T(8,128)(2,1)S(1)} %copy-done.1), channel_id=1, source_target_pairs={{0,8},{4,12},{8,16},{12,20},{16,24},{20,28},{1,9},{5,13},{9,17},{1... | collective-permute-start | bytes 1179656 | tf_op jit(solution)/shard_map/ppermute | solution.py:421
  31.6 21.0 %collective-permute-start.12 = (bf16[384,512]{1,0:T(8,128)(2,1)S(1)}, bf16[384,512]{1,0:T(8,128)(2,1)S(1)}, u32[]{:S(2)}, u32[]{:S(2)}) collective-permute-start(bf16[384,512]{1,0:T(8,128)(2,1)S(1)} %collective-permute-done.10.refs_10_), channel_id=1, source_target_pairs={{8,0},{12,4},{16,8},{20,12},{9,1},{13,5},{17,9},{21,13},{10,2},{14... | collective-permute-start | bytes 1179656 | tf_op jit(solution)/shard_map/ppermute | solution.py:421
  32.3 21.8 %collective-permute-start.6 = (bf16[384,512]{1,0:T(8,128)(2,1)S(1)}, bf16[384,512]{1,0:T(8,128)(2,1)S(1)}, u32[]{:S(2)}, u32[]{:S(2)}) collective-permute-start(bf16[384,512]{1,0:T(8,128)(2,1)S(1)} %collective-permute-done.4.refs_4_), channel_id=1, source_target_pairs={{8,16},{12,20},{16,24},{20,28},{9,17},{13,21},{17,25},{21,29},{10,... | collective-permute-start | bytes 1179656 | tf_op jit(solution)/shard_map/ppermute | solution.py:421
  33.6 21.8 %collective-permute-start.3 = (bf16[384,512]{1,0:T(8,128)(2,1)S(1)}, bf16[384,512]{1,0:T(8,128)(2,1)S(1)}, u32[]{:S(2)}, u32[]{:S(2)}) collective-permute-start(bf16[384,512]{1,0:T(8,128)(2,1)S(1)} %copy-done.1), channel_id=1, source_target_pairs={{0,4},{4,0},{8,12},{12,8},{16,20},{20,16},{24,28},{28,24},{1,5},{5... | collective-permute-start | bytes 1179656 | tf_op jit(solution)/shard_map/ppermute | solution.py:410
  37.3 18.1 %collective-permute-start = (bf16[1296,128]{1,0:T(8,128)(2,1)}, bf16[1296,128]{1,0:T(8,128)(2,1)}, u32[]{:S(2)}, u32[]{:S(2)}) collective-permute-start(bf16[1296,128]{1,0:T(8,128)(2,1)} %get-tuple-element.25.rest_0_), channel_id=1, source_target_pairs={{0,2},{1,3},{2,0},{3,1},{4,6},{5,7},{6,4},{7,5},{8,10},{9,11},{10,... | collective-permute-start | bytes 995336 | tf_op jit(solution)/shard_map/ppermute | solution.py:398
  38.8 35.6 %all-to-all-start.1 = ((bf16[8,192,128]{2,1,0:T(8,128)(2,1)}), bf16[8,192,128]{2,1,0:T(8,128)(2,1)}, u32[]{:S(2)}, u32[]{:S(2)}) async-start(bf16[8,192,128]{2,1,0:T(8,128)(2,1)} %get-tuple-element.23), calls=%async_computation.1 | async-start | bytes 786432 | tf_op jit(solution)/shard_map/all_to_all | solution.py:542
  51.9 6.5 %collective-permute-start.11 = (bf16[384,512]{1,0:T(8,128)(2,1)S(1)}, bf16[384,512]{1,0:T(8,128)(2,1)S(1)}, u32[]{:S(2)}, u32[]{:S(2)}) collective-permute-start(bf16[384,512]{1,0:T(8,128)(2,1)S(1)} %collective-permute-done.10.refs_10_), channel_id=1, source_target_pairs={{0,4},{4,0},{8,12},{12,8},{16,20},{20,16},{1,5},{5,1},{9,13},{13,9... | collective-permute-start | bytes 1179656 | tf_op jit(solution)/shard_map/ppermute | solution.py:427
  52.6 9.2 %collective-permute-start.14 = (bf16[384,512]{1,0:T(8,128)(2,1)S(1)}, bf16[384,512]{1,0:T(8,128)(2,1)}, u32[]{:S(2)}, u32[]{:S(2)}) collective-permute-start(bf16[384,512]{1,0:T(8,128)(2,1)S(1)} %collective-permute-done.12.refs_12_), channel_id=1, source_target_pairs={{8,0},{12,4},{9,1},{13,5},{10,2},{14,6},{11,3},{15,7}} | collective-permute-start | bytes 1179656 | tf_op jit(solution)/shard_map/ppermute | solution.py:421
  54.0 13.1 %collective-permute-start.8 = (bf16[384,512]{1,0:T(8,128)(2,1)S(1)}, bf16[384,512]{1,0:T(8,128)(2,1)}, u32[]{:S(2)}, u32[]{:S(2)}) collective-permute-start(bf16[384,512]{1,0:T(8,128)(2,1)S(1)} %collective-permute-done.6.refs_6_), channel_id=1, source_target_pairs={{16,24},{20,28},{17,25},{21,29},{18,26},{22,30},{19,27},{23,31}} | collective-permute-start | bytes 1179656 | tf_op jit(solution)/shard_map/ppermute | solution.py:421
  55.3 14.5 %collective-permute-start.1 = (bf16[1296,128]{1,0:T(8,128)(2,1)}, bf16[1296,128]{1,0:T(8,128)(2,1)}, u32[]{:S(2)}, u32[]{:S(2)}) collective-permute-start(bf16[1296,128]{1,0:T(8,128)(2,1)} %get-tuple-element.25.rest_0_), channel_id=1, source_target_pairs={{0,1},{1,0},{2,3},{3,2},{4,5},{5,4},{6,7},{7,6},{8,9},{9,8},{10,11... | collective-permute-start | bytes 995336 | tf_op jit(solution)/shard_map/ppermute | solution.py:398
  55.4 15.9 %collective-permute-start.2 = (bf16[1296,128]{1,0:T(8,128)(2,1)}, bf16[1296,128]{1,0:T(8,128)(2,1)}, u32[]{:S(2)}, u32[]{:S(2)}) collective-permute-start(bf16[1296,128]{1,0:T(8,128)(2,1)} %collective-permute-done.rest_1_), channel_id=1, source_target_pairs={{0,1},{1,0},{2,3},{3,2},{4,5},{5,4},{6,7},{7,6},{8,9},{9,8},{10,11... | collective-permute-start | bytes 995336 | tf_op jit(solution)/shard_map/ppermute | solution.py:398
  57.6 0.6 copy-start.2
  58.5 35.4 %collective-permute-start.5 = (bf16[384,512]{1,0:T(8,128)(2,1)S(1)}, bf16[384,512]{1,0:T(8,128)(2,1)S(1)}, u32[]{:S(2)}, u32[]{:S(2)}) collective-permute-start(bf16[384,512]{1,0:T(8,128)(2,1)S(1)} %collective-permute-done.4.refs_4_), channel_id=1, source_target_pairs={{8,12},{12,8},{16,20},{20,16},{24,28},{28,24},{9,13},{13,9},{17,21... | collective-permute-start | bytes 1179656 | tf_op jit(solution)/shard_map/ppermute | solution.py:427
  61.9 32.1 %collective-permute-start.13 = (bf16[384,512]{1,0:T(8,128)(2,1)S(1)}, bf16[384,512]{1,0:T(8,128)(2,1)S(1)}, u32[]{:S(2)}, u32[]{:S(2)}) collective-permute-start(bf16[384,512]{1,0:T(8,128)(2,1)S(1)} %collective-permute-done.12.refs_12_), channel_id=1, source_target_pairs={{0,4},{4,0},{8,12},{12,8},{1,5},{5,1},{9,13},{13,9},{2,6},{6,2},{1... | collective-permute-start | bytes 1179656 | tf_op jit(solution)/shard_map/ppermute | solution.py:427
  67.1 26.8 %collective-permute-start.7 = (bf16[384,512]{1,0:T(8,128)(2,1)S(1)}, bf16[384,512]{1,0:T(8,128)(2,1)}, u32[]{:S(2)}, u32[]{:S(2)}) collective-permute-start(bf16[384,512]{1,0:T(8,128)(2,1)S(1)} %collective-permute-done.6.refs_6_), channel_id=1, source_target_pairs={{16,20},{20,16},{24,28},{28,24},{17,21},{21,17},{25,29},{29,25},{1... | collective-permute-start | bytes 1179656 | tf_op jit(solution)/shard_map/ppermute | solution.py:427
  69.9 24.0 %collective-permute-start.15 = (bf16[384,512]{1,0:T(8,128)(2,1)}, bf16[384,512]{1,0:T(8,128)(2,1)}, u32[]{:S(2)}, u32[]{:S(2)}) collective-permute-start(bf16[384,512]{1,0:T(8,128)(2,1)} %collective-permute-done.14.refs_14_), channel_id=1, source_target_pairs={{0,4},{4,0},{1,5},{5,1},{2,6},{6,2},{3,7},{7,3}} | collective-permute-start | bytes 1179656 | tf_op jit(solution)/shard_map/ppermute | solution.py:427
  71.3 22.6 %collective-permute-start.9 = (bf16[384,512]{1,0:T(8,128)(2,1)}, bf16[384,512]{1,0:T(8,128)(2,1)}, u32[]{:S(2)}, u32[]{:S(2)}) collective-permute-start(bf16[384,512]{1,0:T(8,128)(2,1)} %collective-permute-done.8.refs_8_), channel_id=1, source_target_pairs={{24,28},{28,24},{25,29},{29,25},{26,30},{30,26},{27,31},{31,27}} | collective-permute-start | bytes 1179656 | tf_op jit(solution)/shard_map/ppermute | solution.py:427
  74.4 0.9 copy-start.3
  75.3 1.0 copy-start.6
  76.3 0.7 copy-start.7
  77.0 9.4 %copy-start.5 = (s32[8]{0:T(128)S(1)}, s32[8]{0:T(128)}, u32[]{:S(2)}) copy-start(s32[8]{0:T(128)} %counts_ref.7) | copy-start | bytes 100
  98.2 29.0 %collective-permute-start.17 = (bf16[128,3072]{1,0:T(8,128)(2,1)S(1)}, bf16[128,3072]{1,0:T(8,128)(2,1)S(1)}, u32[]{:S(2)}, u32[]{:S(2)}) collective-permute-start(bf16[128,3072]{1,0:T(8,128)(2,1)S(1)} %get-tuple-element.36), channel_id=1, source_target_pairs={{0,1},{1,0},{2,3},{3,2},{4,5},{5,4},{6,7},{7,6},{8,9},{9,8},{10,11... | collective-permute-start | bytes 2359304 | tf_op jit(solution)/shard_map/ppermute | solution.py:398
  113.7 13.8 %collective-permute-start.19 = (bf16[128,3072]{1,0:T(8,128)(2,1)S(1)}, bf16[128,3072]{1,0:T(8,128)(2,1)S(1)}, u32[]{:S(2)}, u32[]{:S(2)}) collective-permute-start(bf16[128,3072]{1,0:T(8,128)(2,1)S(1)} %get-tuple-element.40), channel_id=1, source_target_pairs={{0,1},{1,0},{2,3},{3,2},{4,5},{5,4},{6,7},{7,6},{8,9},{9,8},{10,11... | collective-permute-start | bytes 2359304 | tf_op jit(solution)/shard_map/ppermute | solution.py:398
  127.2 11.9 %collective-permute-start.16 = (bf16[256,3072]{1,0:T(8,128)(2,1)S(1)}, bf16[256,3072]{1,0:T(8,128)(2,1)S(1)}, u32[]{:S(2)}, u32[]{:S(2)}) collective-permute-start(bf16[256,3072]{1,0:T(8,128)(2,1)S(1)} %shard_map.112), channel_id=1, source_target_pairs={{0,1},{1,0},{2,3},{3,2},{4,5},{5,4},{6,7},{7,6},{8,9},{9,8},{10,11... | collective-permute-start | bytes 4718600 | tf_op jit(solution)/shard_map/ppermute | solution.py:398
  127.4 20.5 %collective-permute-start.18 = (bf16[128,3072]{1,0:T(8,128)(2,1)S(1)}, bf16[128,3072]{1,0:T(8,128)(2,1)S(1)}, u32[]{:S(2)}, u32[]{:S(2)}) collective-permute-start(bf16[128,3072]{1,0:T(8,128)(2,1)S(1)} %add_convert_fusion.1), channel_id=1, source_target_pairs={{0,2},{1,3},{2,0},{3,1},{4,6},{5,7},{6,4},{7,5},{8,10},{9,11},{10,... | collective-permute-start | bytes 2359304 | tf_op jit(solution)/shard_map/ppermute | solution.py:398
  127.7 36.6 %collective-permute-start.20 = (bf16[128,3072]{1,0:T(8,128)(2,1)S(1)}, bf16[128,3072]{1,0:T(8,128)(2,1)S(1)}, u32[]{:S(2)}, u32[]{:S(2)}) collective-permute-start(bf16[128,3072]{1,0:T(8,128)(2,1)S(1)} %add_convert_fusion), channel_id=1, source_target_pairs={{0,2},{1,3},{2,0},{3,1},{4,6},{5,7},{6,4},{7,5},{8,10},{9,11},{10,... | collective-permute-start | bytes 2359304 | tf_op jit(solution)/shard_map/ppermute | solution.py:398
  134.8 29.5 %copy-start.4 = (f32[3072]{0:T(1024)S(1)}, f32[3072]{0:T(1024)}, u32[]{:S(2)}) copy-start(f32[3072]{0:T(1024)} %param.18) | copy-start | bytes 36868

commit v9 on v8

--- a/solution.py
+++ b/solution.py
@@ -407,25 +407,41 @@
     index = lax.axis_index("wide")
     length = count // 2
     blocks, held = [own], [index]
+
+    def add(array, source, route):
+        valid = (source >= 0) & (source < count)
+        other = lax.ppermute(array, "wide", route)
+        blocks.extend([array, other])
+        held.extend([jnp.where(valid, source, -1), jnp.where(valid, source ^ 1, -1)])
+
     blocks.append(lax.ppermute(own, "wide", [(i, i ^ 1) for i in range(count)]))
     held.append(index ^ 1)
-    for sign in (1, -1):
-        current = own
-        for step in range(1, length):
-            move = 2 * sign
-            route = [
-                (i, i + move)
-                for i in range(count)
-                if 0 <= i + move < count and 0 <= i - move * (step - 1) < count
-            ]
-            current = lax.ppermute(current, "wide", route)
-            source = index - move * step
-            valid = (source >= 0) & (source < count)
-            blocks.append(current)
-            held.append(jnp.where(valid, source, -1))
-            swap = [(i, i ^ 1) for i in range(count) if 0 <= i - move * step < count]
-            blocks.append(lax.ppermute(current, "wide", swap))
-            held.append(jnp.where(valid, source ^ 1, -1))
+
+    def reached(step, move):
+        return [i for i in range(count) if 0 <= i - move * step < count]
+
+    def sent(step, move):
+        return [(i - move, i) for i in reached(step, move)]
+
+    forward, backward, single = own, own, None
+    for step in range(1, length):
+        apart = not set(reached(step, 2)) & set(reached(step, -2))
+        if single is None:
+            forward = lax.ppermute(forward, "wide", sent(step, 2))
+            backward = lax.ppermute(backward, "wide", sent(step, -2))
+        else:
+            single = lax.ppermute(single, "wide", sent(step, 2) + sent(step, -2))
+        if not apart:
+            for array, move in ((forward, 2), (backward, -2)):
+                swap = [(i, i ^ 1) for i in reached(step, move)]
+                add(array, index - move * step, swap)
+            continue
+        ahead = index - 2 * step >= 0
+        if single is None:
+            single = jnp.where(ahead, forward, backward)
+        source = jnp.where(ahead, index - 2 * step, index + 2 * step)
+        swap = [(i, i ^ 1) for i in reached(step, 2) + reached(step, -2)]
+        add(single, source, swap)
     return blocks, jnp.stack(held).astype(jnp.int32)
 
 

time: 167 us -> 169 us (1.012)
  waiting for transfers between devices: 46.9 us -> 53.1 us
  starting transfers between devices: 46.5 us -> 42.3 us
  Pallas kernels: 68 us -> 66.3 us
    ppermute x12 -> x9, waiting for transfers between devices: 21.7 us -> 27.3 us  [the longest x2 17.1 us: gathered_rows(): backward = lax.ppermute(backward, 'wide', sent(step, -2))]
    ppermute x12 -> x9, starting transfers between devices: 20.6 us -> 15.7 us  [the longest x4 7.82 us: add(): other = lax.ppermute(array, 'wide', route)]
    pallas_call x4, Pallas kernels: 16.8 us -> 14.3 us  [multiply(): pl.pallas_call(functools.partial(partial_kernel, kept, sent), out_shape=t...]
    unnamed x20 -> x24, local copies, waits for them, and re-layouts: 3.21 us -> 4.1 us
  transfers between devices with their start and end apart: 23 -> 20, of which waited for: 4 -> 5; matrix products, arithmetic and copies ran while one was open for 0% -> 1% of each run, Pallas kernels for 35% -> 34%
where the time goes in v9:
time: 169 us; the launch traced here: 168 us
  Pallas kernels  66.3 us (39%)
  waiting for transfers between devices  53.1 us (31%)
  starting transfers between devices  42.3 us (25%)
  local copies, waits for them, and re-layouts  4.26 us (3%)
  other arithmetic  2.05 us (1%)
    pallas_call x4, Pallas kernels, attend(): pl.pallas_call(functools.partial(attend_kernel, parts, entries), out_shap...  33.3 us
    ppermute x8, waiting for transfers between devices, flip(): return lax.ppermute(block, axis, [(i, i ^ bit) for i in devices])  25.8 us
    ppermute x2, waiting for transfers between devices, gathered_rows(): backward = lax.ppermute(backward, 'wide', sent(step, -2))  17.1 us
    pallas_call x4, Pallas kernels, multiply(): pl.pallas_call(functools.partial(partial_kernel, kept, sent), out_shape=t...  14.3 us
    all_to_all x1, starting transfers between devices, block(): lax.all_to_all(spread, 'wide', split_axis=0, concat_axis=0, tiled=True)  14.1 us
    pallas_call x1, Pallas kernels, block(): pl.pallas_call(functools.partial(project_kernel, row_total, tile_size), o...  9.35 us
    ppermute x1, waiting for transfers between devices, gathered_rows(): single = lax.ppermute(single, 'wide', sent(step, 2) + sent(step, -2))  8.46 us
    ppermute x4, starting transfers between devices, add(): other = lax.ppermute(array, 'wide', route)  7.82 us
  transfers between devices with their start and end apart: 20, of which 5 were waited for; matrix products, arithmetic and copies ran while one was open for 1% of the time, Pallas kernels for 34%

profile of v9, /device:TPU:24, one launch (start us, length us, event | category | flops | bytes accessed | tf_op | source)
XLA Modules:
  0.0 168.4 jit_solution(16972363043701820267)
XLA Ops:
  0.0 0.6 pad_add_fusion.at_ref
  0.6 3.7 %prep.1 = bf16[8,384,128]{2,1,0:T(8,128)(2,1)} custom-call(s32[2]{0:T(128)} %pad_add_fusion.at_ref, bf16[128,3072]{1,0:T(8,128)(2,1)} %embed_ref.3, bf16[128,3072]{1,0:T(8,128)(2,1)} %embed_ref.3, f32[1,3072]{1,0:T(1,128)} %bitcast.18, f32[1,3072]{1,0:T(1,128)} %bitcast.19, bf16[3,384,512]{2,1,0:T(8,128)(2,1)} %qkv_ref.1, bf16[256,128]{1,0:T(8,128)(2,1)} %latents_ref.1, ...), custom_call_target="tpu_custom_call" | custom-call | flops 268435456 | bytes 4194304 | tf_op jit(solution)/shard_map/prep/pallas_call | solution.py:504
  4.3 6.2 %all-to-all-start = ((bf16[8,384,128]{2,1,0:T(8,128)(2,1)}), bf16[8,384,128]{2,1,0:T(8,128)(2,1)S(1)}, u32[]{:S(2)}, u32[]{:S(2)}) async-start(bf16[8,384,128]{2,1,0:T(8,128)(2,1)} %prep.1), calls=%async_computation | async-start | bytes 1572864 | tf_op jit(solution)/shard_map/all_to_all | solution.py:527
  10.5 2.6 %collective-permute-start.6 = (bf16[384,512]{1,0:T(8,128)(2,1)S(1)}, bf16[384,512]{1,0:T(8,128)(2,1)S(1)}, u32[]{:S(2)}, u32[]{:S(2)}) collective-permute-start(bf16[384,512]{1,0:T(8,128)(2,1)S(1)} %copy-done.1), channel_id=1, source_target_pairs={{8,0},{12,4},{16,8},{20,12},{24,16},{28,20},{9,1},{13,5},{17,9},{2... | collective-permute-start | bytes 1179656 | tf_op jit(solution)/shard_map/ppermute | solution.py:431
  13.2 1.3 collective-permute-start.4
  14.5 17.1 %collective-permute-done.6.refs_6_ = bf16[384,512]{1,0:T(8,128)(2,1)S(1)} collective-permute-done((bf16[384,512]{1,0:T(8,128)(2,1)S(1)}, bf16[384,512]{1,0:T(8,128)(2,1)S(1)}, u32[]{:S(2)}, u32[]{:S(2)}) %collective-permute-start.6) | collective-permute-done | bytes 393248 | tf_op jit(solution)/shard_map/ppermute | solution.py:431
  31.6 1.4 collective-permute-start.9
  33.0 0.0 collective-permute-done.4.refs_4_
  33.0 1.3 collective-permute-start.8
  34.3 0.0 all-to-all-done.arrived_ref
  34.3 0.0 copy-start.9
  34.3 0.9 copy-done.9
  35.2 2.1 %middle.1 = (bf16[8,192,128]{2,1,0:T(8,128)(2,1)}, bf16[1296,128]{1,0:T(8,128)(2,1)}, f32[16,128]{1,0:T(8,128)}) custom-call(bf16[8,384,128]{2,1,0:T(8,128)(2,1)} %copy-done.9), custom_call_target="tpu_custom_call" | custom-call | tf_op jit(solution)/shard_map/middle/pallas_call | solution.py:531
  37.2 1.5 collective-permute-start
  38.7 1.4 collective-permute-start.3
  40.1 14.1 %all-to-all-start.1 = ((bf16[8,192,128]{2,1,0:T(8,128)(2,1)}), bf16[8,192,128]{2,1,0:T(8,128)(2,1)}, u32[]{:S(2)}, u32[]{:S(2)}) async-start(bf16[8,192,128]{2,1,0:T(8,128)(2,1)} %get-tuple-element.23), calls=%async_computation.1 | async-start | bytes 786432 | tf_op jit(solution)/shard_map/all_to_all | solution.py:558
  54.2 0.0 collective-permute-done.9
  54.2 0.0 collective-permute-done.8
  54.2 1.1 broadcast_select_fusion.refs_8_
  55.2 1.3 collective-permute-start.11
  56.5 0.1 collective-permute-start.1
  56.6 0.0 collective-permute-done.rest_1_
  56.6 0.5 collective-permute-start.2
  57.1 1.7 %gram.1.gram_ref = bf16[3,128,128]{2,1,0:T(8,128)(2,1)S(1)} custom-call(bf16[128,3072]{1,0:T(8,128)(2,1)S(1)} %copy-done), custom_call_target="tpu_custom_call" | custom-call | tf_op jit(solution)/shard_map/gram/pallas_call | solution.py:519
  58.8 0.0 copy-start.2
  58.8 0.6 copy-done.2
  59.5 0.1 reshape.18.starts_ref
  59.5 0.1 stack.52.held_ref
  59.7 0.7 collective-permute-start.7
  60.4 8.5 %collective-permute-done.11.refs_10_ = bf16[384,512]{1,0:T(8,128)(2,1)S(1)} collective-permute-done((bf16[384,512]{1,0:T(8,128)(2,1)S(1)}, bf16[384,512]{1,0:T(8,128)(2,1)S(1)}, u32[]{:S(2)}, u32[]{:S(2)}) %collective-permute-start.11) | collective-permute-done | bytes 393248 | tf_op jit(solution)/shard_map/ppermute | solution.py:433
  68.8 3.1 %collective-permute-start.5 = (bf16[384,512]{1,0:T(8,128)(2,1)S(1)}, bf16[384,512]{1,0:T(8,128)(2,1)S(1)}, u32[]{:S(2)}, u32[]{:S(2)}) collective-permute-start(bf16[384,512]{1,0:T(8,128)(2,1)S(1)} %collective-permute-done.4.refs_4_), channel_id=1, source_target_pairs={{8,12},{12,8},{16,20},{20,16},{24,28},{28,24},{9,13},{13,9},{17,21... | collective-permute-start | bytes 1179656 | tf_op jit(solution)/shard_map/ppermute | solution.py:413
  72.0 0.0 collective-permute-done.1.rest_2_
  72.0 0.8 collective-permute-start.10
  72.8 3.1 %collective-permute-start.12 = (bf16[384,512]{1,0:T(8,128)(2,1)S(1)}, bf16[384,512]{1,0:T(8,128)(2,1)}, u32[]{:S(2)}, u32[]{:S(2)}) collective-permute-start(bf16[384,512]{1,0:T(8,128)(2,1)S(1)} %collective-permute-done.11.refs_10_), channel_id=1, source_target_pairs={{24,28},{28,24},{0,4},{4,0},{25,29},{29,25},{1,5},{5,1},{26,30},{3... | collective-permute-start | bytes 1179656 | tf_op jit(solution)/shard_map/ppermute | solution.py:413
  76.0 0.0 all-to-all-done.1
  76.0 0.0 copy-start.3
  76.0 0.9 copy-done.3
  76.9 1.0 copy-done.7
  77.9 0.7 copy-done.8
  78.6 9.3 %project.1 = (bf16[512,5120]{1,0:T(8,128)(2,1)S(1)}, bf16[5120,512]{1,0:T(8,128)(2,1)S(1)}, bf16[8,4,256,128]{3,2,1,0:T(8,128)(2,1)S(1)}) custom-call(s32[4]{0:T(128)S(1)} %broadcast_xor_fusion.order_ref, bf16[1536,128]{1,0:T(8,128)(2,1)} %bitcast.15.weight_ref, f32[16,128]{1,0:T(8,128)S(1)} %copy-done.8, bf16[3,128,128]{2,1,0:T(8,128)(2,1)S(1)} %copy-done.3, ...), custom_call_target="tpu_custom_call" | custom-call | flops 3355443200 | bytes 16777216 | tf_op jit(solution)/shard_map/project/pallas_call | solution.py:565
  87.9 7.7 %shard_map.113 = (bf16[128,512]{1,0:T(8,128)(2,1)S(1)}, bf16[128,512]{1,0:T(8,128)(2,1)S(1)}) custom-call(s32[4]{0:T(128)S(1)} %broadcast_xor_fusion.order_ref, s32[64]{0:T(128)S(1)} %reshape.18.starts_ref, s32[8]{0:T(128)S(1)} %copy-done.5, bf16[512,5120]{1,0:T(8,128)(2,1)S(1)} %get-tuple-element.26.keys_ref, ...), custom_call_target="tpu_custom_call" | custom-call | flops 2147483648 | bytes 16777216 | tf_op jit(solution)/shard_map/pallas_call | solution.py:581
  95.6 0.0 collective-permute-done.3.refs_3_
  95.6 0.0 collective-permute-done.10.refs_9_
  95.6 1.8 %collective-permute-done.12.refs_11_ = bf16[384,512]{1,0:T(8,128)(2,1)} collective-permute-done((bf16[384,512]{1,0:T(8,128)(2,1)S(1)}, bf16[384,512]{1,0:T(8,128)(2,1)}, u32[]{:S(2)}, u32[]{:S(2)}) %collective-permute-start.12) | collective-permute-done | bytes 393248 | tf_op jit(solution)/shard_map/ppermute | solution.py:413
  97.4 3.6 %shard_map.114 = (f32[128,3072]{1,0:T(8,128)S(1)}, bf16[128,3072]{1,0:T(8,128)(2,1)S(1)}) custom-call(s32[10]{0:T(128)S(1)} %stack.52.held_ref, bf16[128,512]{1,0:T(8,128)(2,1)S(1)} %get-tuple-element.33.refs_0_, bf16[128,512]{1,0:T(8,128)(2,1)S(1)} %get-tuple-element.34.refs_1_, bf16[384,512]{1,0:T(8,128)(2,1)S(1)} %copy-done.1, ...), custom_call_target="tpu_custom_call" | custom-call | flops 805306368 | bytes 8388608 | tf_op jit(solution)/shard_map/pallas_call | solution.py:601
  101.0 0.1 collective-permute-start.14
  101.1 11.7 %shard_map.115 = (bf16[128,512]{1,0:T(8,128)(2,1)S(1)}, bf16[128,512]{1,0:T(8,128)(2,1)S(1)}) custom-call(s32[4]{0:T(128)S(1)} %broadcast_xor_fusion.order_ref, s32[64]{0:T(128)S(1)} %reshape.18.starts_ref, s32[8]{0:T(128)S(1)} %copy-done.5, bf16[512,5120]{1,0:T(8,128)(2,1)S(1)} %get-tuple-element.26.keys_ref, ...), custom_call_target="tpu_custom_call" | custom-call | flops 2147483648 | bytes 16777216 | tf_op jit(solution)/shard_map/pallas_call | solution.py:581
  112.7 3.6 %shard_map.116 = (f32[128,3072]{1,0:T(8,128)S(1)}, bf16[128,3072]{1,0:T(8,128)(2,1)S(1)}) custom-call(s32[10]{0:T(128)S(1)} %stack.52.held_ref, bf16[128,512]{1,0:T(8,128)(2,1)S(1)} %get-tuple-element.37.refs_0_, bf16[128,512]{1,0:T(8,128)(2,1)S(1)} %get-tuple-element.38.refs_1_, bf16[384,512]{1,0:T(8,128)(2,1)S(1)} %copy-done.1, ...), custom_call_target="tpu_custom_call" | custom-call | flops 805306368 | bytes 8388608 | tf_op jit(solution)/shard_map/pallas_call | solution.py:601
  116.3 0.6 collective-permute-start.16
  116.9 8.9 %shard_map.111 = (bf16[128,512]{1,0:T(8,128)(2,1)S(1)}, bf16[128,512]{1,0:T(8,128)(2,1)S(1)}) custom-call(s32[4]{0:T(128)S(1)} %broadcast_xor_fusion.order_ref, s32[64]{0:T(128)S(1)} %reshape.18.starts_ref, s32[8]{0:T(128)S(1)} %copy-done.5, bf16[512,5120]{1,0:T(8,128)(2,1)S(1)} %get-tuple-element.26.keys_ref, ...), custom_call_target="tpu_custom_call" | custom-call | flops 2147483648 | bytes 16777216 | tf_op jit(solution)/shard_map/pallas_call | solution.py:581
  125.8 3.6 %shard_map.112 = bf16[256,3072]{1,0:T(8,128)(2,1)S(1)} custom-call(s32[10]{0:T(128)S(1)} %stack.52.held_ref, bf16[128,512]{1,0:T(8,128)(2,1)S(1)} %get-tuple-element.31.refs_0_, bf16[128,512]{1,0:T(8,128)(2,1)S(1)} %get-tuple-element.32.refs_1_, bf16[384,512]{1,0:T(8,128)(2,1)S(1)} %copy-done.1, bf16[384,512]{1,0:T(8,128)(2,1)S(1)} %collective-permute-done.3.refs_3_, ...), custom_call_target="tpu_custom_call" | custom-call | flops 805306368 | bytes 8388608 | tf_op jit(solution)/shard_map/pallas_call | solution.py:601
  129.4 0.1 collective-permute-start.13
  129.5 0.0 collective-permute-done.14
  129.5 0.2 add_convert_fusion.1
  129.7 0.1 collective-permute-start.15
  129.8 0.2 add_convert_fusion
  130.0 2.1 %collective-permute-start.17 = (bf16[128,3072]{1,0:T(8,128)(2,1)S(1)}, bf16[128,3072]{1,0:T(8,128)(2,1)S(1)}, u32[]{:S(2)}, u32[]{:S(2)}) collective-permute-start(bf16[128,3072]{1,0:T(8,128)(2,1)S(1)} %add_convert_fusion), channel_id=1, source_target_pairs={{0,2},{1,3},{2,0},{3,1},{4,6},{5,7},{6,4},{7,5},{8,10},{9,11},{10,... | collective-permute-start | bytes 2359304 | tf_op jit(solution)/shard_map/ppermute | solution.py:398
  132.1 5.1 %shard_map.109 = (bf16[128,512]{1,0:T(8,128)(2,1)S(1)}, bf16[128,512]{1,0:T(8,128)(2,1)S(1)}) custom-call(s32[4]{0:T(128)S(1)} %broadcast_xor_fusion.order_ref, s32[64]{0:T(128)S(1)} %reshape.18.starts_ref, s32[8]{0:T(128)S(1)} %copy-done.5, bf16[512,5120]{1,0:T(8,128)(2,1)S(1)} %get-tuple-element.26.keys_ref, ...), custom_call_target="tpu_custom_call" | custom-call | flops 2147483648 | bytes 16777216 | tf_op jit(solution)/shard_map/pallas_call | solution.py:581
  137.2 0.0 copy-start.4
  137.2 3.6 %shard_map.110.own_ref = f32[256,3072]{1,0:T(8,128)S(1)} custom-call(s32[10]{0:T(128)S(1)} %stack.52.held_ref, bf16[128,512]{1,0:T(8,128)(2,1)S(1)} %get-tuple-element.29.refs_0_, bf16[128,512]{1,0:T(8,128)(2,1)S(1)} %get-tuple-element.30.refs_1_, bf16[384,512]{1,0:T(8,128)(2,1)S(1)} %copy-done.1, bf16[384,512]{1,0:T(8,128)(2,1)S(1)} %collective-permute-done.3.refs_3_, ...), custom_call_target="tpu_custom_call" | custom-call | flops 805306368 | bytes 8388608 | tf_op jit(solution)/shard_map/pallas_call | solution.py:601
  140.8 0.0 collective-permute-done.13.first_ref
  140.8 9.4 %collective-permute-done.15.second_ref = bf16[128,3072]{1,0:T(8,128)(2,1)S(1)} collective-permute-done((bf16[128,3072]{1,0:T(8,128)(2,1)S(1)}, bf16[128,3072]{1,0:T(8,128)(2,1)S(1)}, u32[]{:S(2)}, u32[]{:S(2)}) %collective-permute-start.15) | collective-permute-done | bytes 786464 | tf_op jit(solution)/shard_map/ppermute | solution.py:398
  150.2 16.4 %collective-permute-done.17.third_ref = bf16[128,3072]{1,0:T(8,128)(2,1)S(1)} collective-permute-done((bf16[128,3072]{1,0:T(8,128)(2,1)S(1)}, bf16[128,3072]{1,0:T(8,128)(2,1)S(1)}, u32[]{:S(2)}, u32[]{:S(2)}) %collective-permute-start.17) | collective-permute-done | bytes 786464 | tf_op jit(solution)/shard_map/ppermute | solution.py:398
  166.6 1.8 %final.1 = bf16[256,3072]{1,0:T(8,128)(2,1)} custom-call(f32[256,3072]{1,0:T(8,128)S(1)} %shard_map.110.own_ref, bf16[256,3072]{1,0:T(8,128)(2,1)S(1)} %collective-permute-done.13.first_ref, bf16[128,3072]{1,0:T(8,128)(2,1)S(1)} %collective-permute-done.15.second_ref, bf16[128,3072]{1,0:T(8,128)(2,1)S(1)} %collective-permute-done.17.third_ref, ...), custom_call_target="tpu_custom_call" | custom-call | tf_op jit(solution)/shard_map/final/pallas_call | solution.py:620
  (21 shorter events, 0.0 us)
Async XLA Ops:
  4.3 6.2 %copy-start.1 = (bf16[384,512]{1,0:T(8,128)(2,1)S(1)}, bf16[384,512]{1,0:T(8,128)(2,1)}, u32[]{:S(2)}) copy-start(bf16[384,512]{1,0:T(8,128)(2,1)} %refs_2_.7) | copy-start | bytes 1179652
  4.3 29.9 %all-to-all-start = ((bf16[8,384,128]{2,1,0:T(8,128)(2,1)}), bf16[8,384,128]{2,1,0:T(8,128)(2,1)S(1)}, u32[]{:S(2)}, u32[]{:S(2)}) async-start(bf16[8,384,128]{2,1,0:T(8,128)(2,1)} %prep.1), calls=%async_computation | async-start | bytes 1572864 | tf_op jit(solution)/shard_map/all_to_all | solution.py:527
  10.5 46.6 %copy-start.10 = (s32[8,8]{1,0:T(8,128)S(1)}, s32[8,8]{1,0:T(8,128)}, u32[]{:S(2)}) copy-start(s32[8,8]{1,0:T(8,128)} %param.19) | copy-start | bytes 772
  10.5 46.6 %copy-start = (bf16[128,3072]{1,0:T(8,128)(2,1)S(1)}, bf16[128,3072]{1,0:T(8,128)(2,1)}, u32[]{:S(2)}) copy-start(bf16[128,3072]{1,0:T(8,128)(2,1)} %embed_ref.3) | copy-start | bytes 2359300
  10.5 21.0 %collective-permute-start.6 = (bf16[384,512]{1,0:T(8,128)(2,1)S(1)}, bf16[384,512]{1,0:T(8,128)(2,1)S(1)}, u32[]{:S(2)}, u32[]{:S(2)}) collective-permute-start(bf16[384,512]{1,0:T(8,128)(2,1)S(1)} %copy-done.1), channel_id=1, source_target_pairs={{8,0},{12,4},{16,8},{20,12},{24,16},{28,20},{9,1},{13,5},{17,9},{2... | collective-permute-start | bytes 1179656 | tf_op jit(solution)/shard_map/ppermute | solution.py:431
  13.2 19.8 %collective-permute-start.4 = (bf16[384,512]{1,0:T(8,128)(2,1)S(1)}, bf16[384,512]{1,0:T(8,128)(2,1)S(1)}, u32[]{:S(2)}, u32[]{:S(2)}) collective-permute-start(bf16[384,512]{1,0:T(8,128)(2,1)S(1)} %copy-done.1), channel_id=1, source_target_pairs={{0,8},{4,12},{8,16},{12,20},{16,24},{20,28},{1,9},{5,13},{9,17},{1... | collective-permute-start | bytes 1179656 | tf_op jit(solution)/shard_map/ppermute | solution.py:430
  31.6 22.6 %collective-permute-start.9 = (bf16[384,512]{1,0:T(8,128)(2,1)S(1)}, bf16[384,512]{1,0:T(8,128)(2,1)}, u32[]{:S(2)}, u32[]{:S(2)}) collective-permute-start(bf16[384,512]{1,0:T(8,128)(2,1)S(1)} %collective-permute-done.6.refs_6_), channel_id=1, source_target_pairs={{8,0},{12,4},{16,8},{20,12},{9,1},{13,5},{17,9},{21,13},{10,2},{14... | collective-permute-start | bytes 1179656 | tf_op jit(solution)/shard_map/ppermute | solution.py:431
  33.0 21.2 %collective-permute-start.8 = (bf16[384,512]{1,0:T(8,128)(2,1)S(1)}, bf16[384,512]{1,0:T(8,128)(2,1)}, u32[]{:S(2)}, u32[]{:S(2)}) collective-permute-start(bf16[384,512]{1,0:T(8,128)(2,1)S(1)} %collective-permute-done.4.refs_4_), channel_id=1, source_target_pairs={{8,16},{12,20},{16,24},{20,28},{9,17},{13,21},{17,25},{21,29},{10,... | collective-permute-start | bytes 1179656 | tf_op jit(solution)/shard_map/ppermute | solution.py:430
  34.3 0.9 copy-start.9
  37.2 19.3 %copy-start.6 = (bf16[1296,128]{1,0:T(8,128)(2,1)S(1)}, bf16[1296,128]{1,0:T(8,128)(2,1)}, u32[]{:S(2)}) copy-start(bf16[1296,128]{1,0:T(8,128)(2,1)} %get-tuple-element.25.rest_0_) | copy-start | bytes 995332
  37.2 22.4 %copy-start.11 = (s32[4]{0:T(128)S(1)}, s32[4]{0:T(128)}, u32[]{:S(2)}) copy-start(s32[4]{0:T(128)} %constant.41.clone) | copy-start | bytes 52
  37.2 19.4 %collective-permute-start = (bf16[1296,128]{1,0:T(8,128)(2,1)}, bf16[1296,128]{1,0:T(8,128)(2,1)}, u32[]{:S(2)}, u32[]{:S(2)}) collective-permute-start(bf16[1296,128]{1,0:T(8,128)(2,1)} %get-tuple-element.25.rest_0_), channel_id=1, source_target_pairs={{0,2},{1,3},{2,0},{3,1},{4,6},{5,7},{6,4},{7,5},{8,10},{9,11},{10,... | collective-permute-start | bytes 995336 | tf_op jit(solution)/shard_map/ppermute | solution.py:398
  38.7 56.9 %collective-permute-start.3 = (bf16[384,512]{1,0:T(8,128)(2,1)S(1)}, bf16[384,512]{1,0:T(8,128)(2,1)S(1)}, u32[]{:S(2)}, u32[]{:S(2)}) collective-permute-start(bf16[384,512]{1,0:T(8,128)(2,1)S(1)} %copy-done.1), channel_id=1, source_target_pairs={{0,4},{4,0},{8,12},{12,8},{16,20},{20,16},{24,28},{28,24},{1,5},{5... | collective-permute-start | bytes 1179656 | tf_op jit(solution)/shard_map/ppermute | solution.py:417
  40.1 35.9 %all-to-all-start.1 = ((bf16[8,192,128]{2,1,0:T(8,128)(2,1)}), bf16[8,192,128]{2,1,0:T(8,128)(2,1)}, u32[]{:S(2)}, u32[]{:S(2)}) async-start(bf16[8,192,128]{2,1,0:T(8,128)(2,1)} %get-tuple-element.23), calls=%async_computation.1 | async-start | bytes 786432 | tf_op jit(solution)/shard_map/all_to_all | solution.py:558
  55.2 13.6 %collective-permute-start.11 = (bf16[384,512]{1,0:T(8,128)(2,1)S(1)}, bf16[384,512]{1,0:T(8,128)(2,1)S(1)}, u32[]{:S(2)}, u32[]{:S(2)}) collective-permute-start(bf16[384,512]{1,0:T(8,128)(2,1)S(1)} %broadcast_select_fusion.refs_8_), channel_id=1, source_target_pairs={{16,24},{20,28},{8,0},{12,4},{17,25},{21,29},{9,1},{13,5},{18,26},... | collective-permute-start | bytes 1179656 | tf_op jit(solution)/shard_map/ppermute | solution.py:433
  56.5 15.4 %collective-permute-start.1 = (bf16[1296,128]{1,0:T(8,128)(2,1)S(1)}, bf16[1296,128]{1,0:T(8,128)(2,1)}, u32[]{:S(2)}, u32[]{:S(2)}) collective-permute-start(bf16[1296,128]{1,0:T(8,128)(2,1)S(1)} %copy-done.6), channel_id=1, source_target_pairs={{0,1},{1,0},{2,3},{3,2},{4,5},{5,4},{6,7},{7,6},{8,9},{9,8},{10,11... | collective-permute-start | bytes 995336 | tf_op jit(solution)/shard_map/ppermute | solution.py:398
  56.6 16.2 %collective-permute-start.2 = (bf16[1296,128]{1,0:T(8,128)(2,1)}, bf16[1296,128]{1,0:T(8,128)(2,1)}, u32[]{:S(2)}, u32[]{:S(2)}) collective-permute-start(bf16[1296,128]{1,0:T(8,128)(2,1)} %collective-permute-done.rest_1_), channel_id=1, source_target_pairs={{0,1},{1,0},{2,3},{3,2},{4,5},{5,4},{6,7},{7,6},{8,9},{9,8},{10,11... | collective-permute-start | bytes 995336 | tf_op jit(solution)/shard_map/ppermute | solution.py:398
  58.8 0.6 copy-start.2
  59.7 35.9 %collective-permute-start.7 = (bf16[384,512]{1,0:T(8,128)(2,1)S(1)}, bf16[384,512]{1,0:T(8,128)(2,1)S(1)}, u32[]{:S(2)}, u32[]{:S(2)}) collective-permute-start(bf16[384,512]{1,0:T(8,128)(2,1)S(1)} %collective-permute-done.6.refs_6_), channel_id=1, source_target_pairs={{0,4},{4,0},{8,12},{12,8},{16,20},{20,16},{1,5},{5,1},{9,13},{13,9... | collective-permute-start | bytes 1179656 | tf_op jit(solution)/shard_map/ppermute | solution.py:413
  68.8 26.8 %collective-permute-start.5 = (bf16[384,512]{1,0:T(8,128)(2,1)S(1)}, bf16[384,512]{1,0:T(8,128)(2,1)S(1)}, u32[]{:S(2)}, u32[]{:S(2)}) collective-permute-start(bf16[384,512]{1,0:T(8,128)(2,1)S(1)} %collective-permute-done.4.refs_4_), channel_id=1, source_target_pairs={{8,12},{12,8},{16,20},{20,16},{24,28},{28,24},{9,13},{13,9},{17,21... | collective-permute-start | bytes 1179656 | tf_op jit(solution)/shard_map/ppermute | solution.py:413
  72.0 23.7 %collective-permute-start.10 = (bf16[384,512]{1,0:T(8,128)(2,1)S(1)}, bf16[384,512]{1,0:T(8,128)(2,1)S(1)}, u32[]{:S(2)}, u32[]{:S(2)}) collective-permute-start(bf16[384,512]{1,0:T(8,128)(2,1)S(1)} %broadcast_select_fusion.refs_8_), channel_id=1, source_target_pairs={{16,20},{20,16},{24,28},{28,24},{0,4},{4,0},{8,12},{12,8},{17,21},... | collective-permute-start | bytes 1179656 | tf_op jit(solution)/shard_map/ppermute | solution.py:413
  72.8 24.6 %collective-permute-start.12 = (bf16[384,512]{1,0:T(8,128)(2,1)S(1)}, bf16[384,512]{1,0:T(8,128)(2,1)}, u32[]{:S(2)}, u32[]{:S(2)}) collective-permute-start(bf16[384,512]{1,0:T(8,128)(2,1)S(1)} %collective-permute-done.11.refs_10_), channel_id=1, source_target_pairs={{24,28},{28,24},{0,4},{4,0},{25,29},{29,25},{1,5},{5,1},{26,30},{3... | collective-permute-start | bytes 1179656 | tf_op jit(solution)/shard_map/ppermute | solution.py:413
  76.0 0.9 copy-start.3
  76.9 1.0 copy-start.7
  77.9 0.7 copy-start.8
  78.6 9.4 %copy-start.5 = (s32[8]{0:T(128)S(1)}, s32[8]{0:T(128)}, u32[]{:S(2)}) copy-start(s32[8]{0:T(128)} %counts_ref.7) | copy-start | bytes 100
  101.0 28.5 %collective-permute-start.14 = (bf16[128,3072]{1,0:T(8,128)(2,1)S(1)}, bf16[128,3072]{1,0:T(8,128)(2,1)S(1)}, u32[]{:S(2)}, u32[]{:S(2)}) collective-permute-start(bf16[128,3072]{1,0:T(8,128)(2,1)S(1)} %get-tuple-element.36), channel_id=1, source_target_pairs={{0,1},{1,0},{2,3},{3,2},{4,5},{5,4},{6,7},{7,6},{8,9},{9,8},{10,11... | collective-permute-start | bytes 2359304 | tf_op jit(solution)/shard_map/ppermute | solution.py:398
  116.3 13.5 %collective-permute-start.16 = (bf16[128,3072]{1,0:T(8,128)(2,1)S(1)}, bf16[128,3072]{1,0:T(8,128)(2,1)S(1)}, u32[]{:S(2)}, u32[]{:S(2)}) collective-permute-start(bf16[128,3072]{1,0:T(8,128)(2,1)S(1)} %get-tuple-element.40), channel_id=1, source_target_pairs={{0,1},{1,0},{2,3},{3,2},{4,5},{5,4},{6,7},{7,6},{8,9},{9,8},{10,11... | collective-permute-start | bytes 2359304 | tf_op jit(solution)/shard_map/ppermute | solution.py:398
  129.4 11.4 %collective-permute-start.13 = (bf16[256,3072]{1,0:T(8,128)(2,1)S(1)}, bf16[256,3072]{1,0:T(8,128)(2,1)S(1)}, u32[]{:S(2)}, u32[]{:S(2)}) collective-permute-start(bf16[256,3072]{1,0:T(8,128)(2,1)S(1)} %shard_map.112), channel_id=1, source_target_pairs={{0,1},{1,0},{2,3},{3,2},{4,5},{5,4},{6,7},{7,6},{8,9},{9,8},{10,11... | collective-permute-start | bytes 4718600 | tf_op jit(solution)/shard_map/ppermute | solution.py:398
  129.7 20.5 %collective-permute-start.15 = (bf16[128,3072]{1,0:T(8,128)(2,1)S(1)}, bf16[128,3072]{1,0:T(8,128)(2,1)S(1)}, u32[]{:S(2)}, u32[]{:S(2)}) collective-permute-start(bf16[128,3072]{1,0:T(8,128)(2,1)S(1)} %add_convert_fusion.1), channel_id=1, source_target_pairs={{0,2},{1,3},{2,0},{3,1},{4,6},{5,7},{6,4},{7,5},{8,10},{9,11},{10,... | collective-permute-start | bytes 2359304 | tf_op jit(solution)/shard_map/ppermute | solution.py:398
  130.0 36.6 %collective-permute-start.17 = (bf16[128,3072]{1,0:T(8,128)(2,1)S(1)}, bf16[128,3072]{1,0:T(8,128)(2,1)S(1)}, u32[]{:S(2)}, u32[]{:S(2)}) collective-permute-start(bf16[128,3072]{1,0:T(8,128)(2,1)S(1)} %add_convert_fusion), channel_id=1, source_target_pairs={{0,2},{1,3},{2,0},{3,1},{4,6},{5,7},{6,4},{7,5},{8,10},{9,11},{10,... | collective-permute-start | bytes 2359304 | tf_op jit(solution)/shard_map/ppermute | solution.py:398
  137.2 29.4 %copy-start.4 = (f32[3072]{0:T(1024)S(1)}, f32[3072]{0:T(1024)}, u32[]{:S(2)}) copy-start(f32[3072]{0:T(1024)} %param.18) | copy-start | bytes 36868
